TPU v7x, 32 devices: a whole 2x2x4 slice. The times are simulated.
32 devices in a mesh: row: 2 (over x), col: 4 (over y, core), layer: 4 (over z).
Axes of the slice: x: 2, y: 2, z: 4, core: 2. Of those that a mesh axis runs over, the one named last changes fastest.
Arguments:
- source_matrix_strip: bfloat16 [4096, 512], P('row', 'col')
- target_matrix_strip: bfloat16 [512, 8192], P('row', ('col', 'layer'))
- stored_tile_flag: int32 [32, 4], P('row', 'col'), may hold values from 0 to 1
- target_place_tile_index: int32 [32, 32], P('row', ('col', 'layer')), may hold values from 0 to 3, as said below
- retained_target_flag: int32 [32, 32], P('row', ('col', 'layer')), may hold values 0 or 1
Outputs:
- clustered: bfloat16 [4096, 4096], P(('row', 'layer'), 'col')
Inputs may be any that keep to these rules, and one draw needn't show every extreme that they name: `target_place_tile_index`: within each block row, the 2 slots of one column tile name distinct column blocks.
All inputs are finite; a program needn't handle non-finite values. No bound on the sum of `retained_target_flag` on one device may be relied on, other than what follows from the above.
Results may differ from a plain program's by a relative error of at most 0.0012.
Values may be sent and summed in bfloat16 or wider, within the bound.
No kernel may reach another device: no remote copies, remote signals or barrier semaphores. Data moves between devices by JAX's collectives and lax.ppermute only.
A program may use at most 64 MiB of HBM per device.

v0:
```python
import jax
import jax.numpy as jnp
from jax import lax
from jax.sharding import PartitionSpec as P

BS = 128
COLB = 4
KOL = 2


def matrix_squaring_step(walk_matrix_result, target_place_tile_index, retained_target_flag):
    block_rows = walk_matrix_result.shape[0] // BS
    product_blocks = walk_matrix_result.reshape(block_rows, BS, COLB, BS)
    block_selector = (
        target_place_tile_index[:, :, None] == jnp.arange(COLB, dtype=jnp.int32)[None, None, :]
    ).astype(jnp.float32)
    picked = jnp.einsum(
        "rsc,rick->rsik", block_selector, product_blocks, precision=lax.Precision.HIGHEST
    )
    retain_weight = retained_target_flag.astype(jnp.float32)
    raised_power_blocks = picked * picked * retain_weight[:, :, None, None]
    row_sums = jnp.sum(raised_power_blocks, axis=2)
    partial_column_sums = jnp.einsum(
        "rsc,rsk->ck", block_selector, row_sums, precision=lax.Precision.HIGHEST
    )
    return (block_selector, raised_power_blocks, partial_column_sums)


def normalize_blocks(block_selector, raised_power_blocks, column_sums, total_rows):
    column_mean = column_sums / jnp.float32(total_rows)
    denominator = (
        jnp.einsum("rsc,ck->rsk", block_selector, column_mean, precision=lax.Precision.HIGHEST)
        + 1e-06
    )
    normalized = (raised_power_blocks / denominator[:, :, None, :]).astype(jnp.bfloat16)
    block_rows = raised_power_blocks.shape[0]
    return jnp.transpose(normalized, (0, 2, 1, 3)).reshape(block_rows * BS, KOL * BS)


def shards(
    source_matrix_strip,
    target_matrix_strip,
    stored_tile_flag,
    target_place_tile_index,
    retained_target_flag,
):
    local_rows = source_matrix_strip.shape[0]
    expanded = jnp.repeat(jnp.repeat(stored_tile_flag, BS, axis=0), BS, axis=1)
    masked = source_matrix_strip * expanded.astype(jnp.bfloat16)
    right_whole = lax.all_gather(target_matrix_strip, "row", axis=0, tiled=True)
    total_rows = local_rows * lax.axis_size("row")
    walk_matrix_result = jnp.dot(
        lax.all_gather(masked, "col", axis=1, tiled=True),
        right_whole,
        preferred_element_type=jnp.float32,
    )
    block_selector, raised_power_blocks, partial_column_sums = matrix_squaring_step(
        walk_matrix_result, target_place_tile_index, retained_target_flag
    )
    column_sums = lax.psum(partial_column_sums, "row")
    arranged = normalize_blocks(block_selector, raised_power_blocks, column_sums, total_rows)
    return lax.all_to_all(arranged, "layer", split_axis=0, concat_axis=1, tiled=True)


def solution(mesh):
    placed = (
        P("row", "col"),
        P("row", ("col", "layer")),
        P("row", "col"),
        P("row", ("col", "layer")),
        P("row", ("col", "layer")),
    )
    return jax.shard_map(
        shards, mesh=mesh, in_specs=placed, out_specs=P(("row", "layer"), "col"), check_vma=False
    )
```

profile of v0, /device:TPU:0, one launch (start us, length us, event | category | flops | bytes accessed | tf_op | source)
XLA Modules:
  0.0 96.9 jit_solution(11177682488823599812)
XLA Ops:
  6.5 0.0 all-gather.2.cloned.1.call-start
  6.5 0.7 convert_bitcast_fusion
  7.2 0.1 broadcast_bitcast_fusion
  7.3 2.2 %broadcast_multiply_fusion = bf16[2048,128]{1,0:T(8,128)(2,1)} fusion(bf16[2048,128]{1,0:T(8,128)(2,1)} %param.5, bf16[2048]{0:T(1024)(128)(2,1)S(1)} %broadcast_bitcast_fusion), kind=kLoop, calls=%fused_computation.5 | loop fusion | flops 262144 | bytes 1052672 | tf_op jit(solution)/shard_map/mul | solution.py:49
  9.4 0.0 all-gather.2.cloned.1.call-update
  9.5 0.7 fusion.2
  10.2 0.1 copy.10
  10.3 0.7 convert_element_type.25
  11.0 0.1 copy.7
  11.0 10.2 %all_gather.7 = bf16[512,512]{1,0:T(8,128)(2,1)S(1)} all-gather(bf16[256,512]{1,0:T(8,128)(2,1)} %param.6), channel_id=1, replica_groups=mesh['row'=2,'col'=4,'layer'=4] {'row'}, dimensions={0}, use_global_device_ids=true | all-gather | bytes 786432 | tf_op jit(solution)/shard_map/all_gather | solution.py:50
  21.2 14.0 %all-gather.2.cloned.1.call-done = bf16[2048,512]{1,0:T(8,128)(2,1)} async-done(((bf16[2048,128]{1,0:T(8,128)(2,1)}), bf16[2048,512]{1,0:T(8,128)(2,1)}) %all-gather.2.cloned.1.call-update) | async-done | bytes 2097168 | tf_op jit(solution)/shard_map/all_gather | solution.py:53
  35.2 4.8 %fusion.10 = f32[2048,512]{1,0:T(8,128)} fusion(bf16[2048,512]{1,0:T(8,128)(2,1)} %all-gather.2.cloned.1.call-done, bf16[512,512]{1,0:T(8,128)(2,1)S(1)} %all_gather.7), kind=kOutput, calls=%fused_computation.18 | convolution fusion | flops 1073741824 | bytes 6815744 | tf_op jit(solution)/shard_map/dot_general | solution.py:52
  39.9 5.2 %reshape.22 = f32[16,128,4,128]{3,2,1,0:T(4,128)} reshape(f32[2048,512]{1,0:T(8,128)} %fusion.10) | data formatting | bytes 8388608 | tf_op jit(solution)/shard_map/reshape | solution.py:13
  45.2 0.0 copy-start
  45.2 7.3 %fusion.9 = (f32[16,2,128]{2,1,0:T(2,128)S(1)}, f32[16,2,128,128]{3,1,2,0:T(2,128)S(1)}) fusion(f32[16,2]{1,0:T(8,128)S(1)} %copy.7, pred[16,2,4,1]{2,1,3,0:T(4,128)(4,1)S(1)} %copy.10, f32[16,128,4,128]{3,2,1,0:T(4,128)} %reshape.22), kind=kOutput, calls=%fused_computation.17 | convolution fusion | flops 26734592 | bytes 6308096 | tf_op jit(solution)/shard_map/rsc,rick->rsik/dot_general | solution.py:17
  52.5 0.0 copy-done
  52.5 0.2 convolution_bitcast_fusion
  52.7 4.9 %psum.7 = f32[4,128]{1,0:T(4,128)S(1)} all-reduce(f32[4,128]{1,0:T(4,128)S(1)} %convolution_bitcast_fusion), channel_id=1, replica_groups=mesh['row'=2,'col'=4,'layer'=4] {'row'}, use_global_device_ids=true, to_apply=%region_1.0 | all-reduce | flops 512 | bytes 4096 | tf_op jit(solution)/shard_map/psum | solution.py:60
  57.6 0.2 convolution_add_fusion
  57.9 0.9 fusion
  58.8 0.7 all_to_all.14
  59.5 29.4 %all_to_all.19 = bf16[4,512,256]{2,1,0:T(8,128)(2,1)S(1)} all-to-all(bf16[4,512,256]{2,1,0:T(8,128)(2,1)S(1)} %all_to_all.14), channel_id=1, replica_groups=mesh['row'=2,'col'=4,'layer'=4] {'layer'}, dimensions={0} | all-to-all | bytes 2097152 | tf_op jit(solution)/shard_map/all_to_all | solution.py:62
  88.9 1.1 %copy.14 = bf16[4,64,8,256]{3,2,0,1:T(8,128)(2,1)} copy(bf16[4,64,8,256]{3,2,1,0:T(8,128)(2,1)S(1)} %bitcast.20) | data formatting | bytes 2097152 | tf_op jit(solution)/shard_map/all_to_all | solution.py:62
  (1 shorter events, 0.0 us)
Async XLA Ops:
  6.5 28.6 %all-gather.2.cloned.1.call-start = ((), (), s32[]{:S(2)}) async-start(), calls=%async_computation.1 | async-start | bytes 2621440 | tf_op jit(solution)/shard_map/all_gather | solution.py:53
  45.2 7.3 %copy-start = (s32[16,2]{0,1:T(2,128)S(1)}, s32[16,2]{0,1:T(2,128)}, u32[]{:S(2)}) copy-start(s32[16,2]{0,1:T(2,128)} %param.8) | copy-start | bytes 388
Sparse Core Ops, SparseCore 0:
  9.6 25.5 all-gather.1
where the time goes:
time: 97.3 us; the launch traced here: 96.9 us
  blocking collectives  44.5 us (46%)
  waiting for transfers between devices  14 us (14%)
  between operations  13.4 us (14%)
  matrix products  12.5 us (13%)
  local copies, waits for them, and re-layouts  7.34 us (8%)
  other arithmetic  5.11 us (5%)
    all_to_all x1, blocking collectives, shards(): lax.all_to_all(arranged, 'layer', split_axis=0, concat_axis=1, tiled=True)  29.4 us
    all_gather x1, waiting for transfers between devices, shards(): lax.all_gather(masked, 'col', axis=1, tiled=True)  14 us
    all_gather x1, blocking collectives, shards(): right_whole = lax.all_gather(target_matrix_strip, 'row', axis=0, tiled=True)  10.2 us
    dot_general x1, matrix products, matrix_squaring_step(): jnp.einsum('rsc,rick->rsik', block_selector, product_blocks, precision=la...  7.34 us
    reshape x1, local copies, waits for them, and re-layouts, matrix_squaring_step(): product_blocks = walk_matrix_result.reshape(block_rows, BS, COLB, BS)  5.23 us
    psum x1, blocking collectives, shards(): column_sums = lax.psum(partial_column_sums, 'row')  4.93 us
    dot_general x1, matrix products, shards(): jnp.dot(lax.all_gather(masked, 'col', axis=1, tiled=True), right_whole, p...  4.76 us
    mul x1, other arithmetic, shards(): masked = source_matrix_strip * expanded.astype(jnp.bfloat16)  2.18 us
  transfers between devices with their start and end apart: 1, of which 1 were waited for; matrix products, arithmetic and copies ran while one was open for 2% of the time, Pallas kernels for 0%

commit v1 on v0

v1 whole, which is shorter than its diff:
```python
import functools

import jax
import jax.numpy as jnp
from jax import lax
from jax.experimental import pallas as pl
from jax.experimental.pallas import tpu as pltpu
from jax.sharding import PartitionSpec as P

BS = 128
COLB = 4
KOL = 2
TILE = COLB * BS
OUT = KOL * BS
META = COLB
VMEM_LIMIT = 48 * 1024 * 1024

ANY = pl.BlockSpec(memory_space=pl.ANY)
VMEM = pl.BlockSpec(memory_space=pltpu.VMEM)
SMEM = pl.BlockSpec(memory_space=pltpu.SMEM)


def swap(value, axis, bit):
    count = lax.axis_size(axis)
    return lax.ppermute(value, axis, [(i, i ^ bit) for i in range(count)])


def gather(piece, axis):
    count = lax.axis_size(axis)
    pieces = {0: piece}
    bit = count // 2
    while bit:
        for k in list(pieces):
            pieces[k ^ bit] = swap(pieces[k], axis, bit)
        bit //= 2
    return [pieces[k] for k in range(count)]


def call(kernel, out_shape, in_specs, out_specs, scratch, flops, nbytes, aliases=None):
    return pl.pallas_call(
        kernel,
        out_shape=out_shape,
        in_specs=in_specs,
        out_specs=out_specs,
        scratch_shapes=scratch,
        input_output_aliases=aliases or {},
        compiler_params=pltpu.CompilerParams(vmem_limit_bytes=VMEM_LIMIT),
        cost_estimate=pl.CostEstimate(flops=flops, bytes_accessed=nbytes, transcendentals=0),
    )


def mask_kernel(flag, source, masked):
    for i in range(source.shape[0] // BS):
        rows = pl.ds(i * BS, BS)
        block = source[rows, :]
        masked[rows, :] = jnp.where(flag[0, i] != 0, block, jnp.zeros_like(block))


def mask_blocks(flag, source):
    size = source.size * 2
    return call(
        mask_kernel,
        jax.ShapeDtypeStruct(source.shape, source.dtype),
        [SMEM, VMEM],
        VMEM,
        [],
        source.size,
        2 * size,
    )(flag, source)


def fetch_left(lefts, panel, sem):
    me = lax.axis_index("col")
    copies = []
    for k, left in enumerate(lefts):
        place = pl.ds(pl.multiple_of((me ^ k) * BS, BS), BS)
        copies.append(pltpu.make_async_copy(left, panel.at[:, place], sem.at[k]))
    return copies


def fetch_right(rights, panel, sem):
    me = lax.axis_index("row")
    depth = rights[0].shape[0]
    copies = []
    for k, right in enumerate(rights):
        place = pl.ds(pl.multiple_of((me ^ k) * depth, depth), depth)
        copies.append(pltpu.make_async_copy(right, panel.at[place, :], sem.at[k]))
    return copies


def own_tile_kernel(n_left, n_right, layers, *refs):
    place_s, keep_s, place_v, keep_v = refs[:4]
    lefts = refs[4 : 4 + n_left]
    rights = refs[4 + n_left : 4 + n_left + n_right]
    sums, inflated, own_left = refs[4 + n_left + n_right : 7 + n_left + n_right]
    left, right, product, kept, partial, left_sem, right_sem, out_sem = refs[7 + n_left + n_right :]
    layer = lax.axis_index("layer")
    copies = fetch_left(lefts, left, left_sem) + fetch_right(rights, right, right_sem)
    for copy in copies:
        copy.start()
    partial[...] = jnp.zeros_like(partial)
    for copy in copies:
        copy.wait()
    band = left.shape[0] // layers
    own_rows = pl.ds(pl.multiple_of(layer * band, band), band)
    left_out = pltpu.make_async_copy(left.at[own_rows, :], own_left, out_sem.at[0])
    left_out.start()

    @pl.loop(0, layers)
    def _(q):
        first = pl.multiple_of(q * band, band)
        product[...] = jnp.dot(
            left[pl.ds(first, band), :], right[...], preferred_element_type=jnp.float32
        )
        for i in range(band // BS):
            for s in range(KOL):
                row = q * (band // BS) + i
                block = place_s[s, row]
                picked = product[
                    pl.ds(i * BS, BS), pl.ds(pl.multiple_of(block * BS, BS), BS)
                ]
                squares = picked * picked * keep_s[s, row].astype(jnp.float32)
                kept[pl.ds(pl.multiple_of(first + i * BS, BS), BS), pl.ds(s * BS, BS)] = squares
                partial[block] += jnp.sum(squares.reshape(BS // 8, 8, BS), axis=0)

    for part in range(2):
        rows = pl.ds(pl.multiple_of((layer ^ part) * band, band), band)
        pltpu.make_async_copy(kept.at[rows, :], inflated.at[pl.ds(part * band, band), :], out_sem.at[1 + part]).start()
    sums[...] = jnp.zeros_like(sums)
    for block in range(COLB):
        sums[pl.ds(block, 1), :] = jnp.sum(partial[block], axis=0, keepdims=True)
    bands = place_v.shape[1]
    sums[META : META + KOL, 0:bands] = place_v[...].astype(jnp.float32)
    sums[META + KOL : META + 2 * KOL, 0:bands] = keep_v[...].astype(jnp.float32)
    left_out.wait()
    for part in range(2):
        rows = pl.ds(pl.multiple_of((layer ^ part) * band, band), band)
        pltpu.make_async_copy(kept.at[rows, :], inflated.at[pl.ds(part * band, band), :], out_sem.at[1 + part]).wait()


def own_tile(place, keep, lefts, rights, layers):
    rows = lefts[0].shape[0]
    inner = len(lefts) * BS
    band = rows // layers
    return call(
        functools.partial(own_tile_kernel, len(lefts), len(rights), layers),
        (
            jax.ShapeDtypeStruct((2 * COLB, BS), jnp.float32),
            jax.ShapeDtypeStruct((2 * band, OUT), jnp.float32),
            jax.ShapeDtypeStruct((band, inner), jnp.bfloat16),
        ),
        [SMEM, SMEM, VMEM, VMEM] + [ANY] * (len(lefts) + len(rights)),
        (VMEM, ANY, ANY),
        [
            pltpu.VMEM((rows, inner), jnp.bfloat16),
            pltpu.VMEM((inner, TILE), jnp.bfloat16),
            pltpu.VMEM((band, TILE), jnp.float32),
            pltpu.VMEM((rows, OUT), jnp.float32),
            pltpu.VMEM((COLB, 8, BS), jnp.float32),
            pltpu.SemaphoreType.DMA((len(lefts),)),
            pltpu.SemaphoreType.DMA((len(rights),)),
            pltpu.SemaphoreType.DMA((3,)),
        ],
        2 * rows * inner * TILE,
        2 * (rows + TILE) * inner + 4 * rows * OUT,
    )(place, keep, place, keep, *lefts, *rights)


def scale_kernel(total_rows, place, sums, other, inflated, out, sent, all_sums, own, scale, sem):
    layer = lax.axis_index("layer")
    whole = sums[0:COLB, :] + other[0:COLB, :]
    all_sums[...] = sums[...]
    all_sums[0:COLB, :] = whole
    scale[...] = 1.0 / (whole / jnp.float32(total_rows) + 1e-6)
    band = own.shape[0]
    for part, target in ((1, sent), (0, own)):
        for i in range(band // BS):
            row = (layer ^ part) * (band // BS) + i
            for s in range(KOL):
                at = (pl.ds(part * band + i * BS, BS), pl.ds(s * BS, BS))
                to = (pl.ds(i * BS, BS), pl.ds(s * BS, BS))
                block = place[s, row]
                target[to] = (inflated[at] * scale[pl.ds(block, 1), :]).astype(target.dtype)
    columns = pl.ds(pl.multiple_of(layer * OUT, OUT), OUT)
    copy = pltpu.make_async_copy(own, out.at[:, columns], sem)
    copy.start()
    copy.wait()


def scale_own(place, sums, other, inflated, layers, total_rows):
    band = inflated.shape[0] // 2
    return call(
        functools.partial(scale_kernel, total_rows),
        (
            jax.ShapeDtypeStruct((band, layers * OUT), jnp.bfloat16),
            jax.ShapeDtypeStruct((band, OUT), jnp.bfloat16),
            jax.ShapeDtypeStruct(sums.shape, jnp.float32),
        ),
        [SMEM, VMEM, VMEM, VMEM],
        (ANY, VMEM, VMEM),
        [
            pltpu.VMEM((band, OUT), jnp.bfloat16),
            pltpu.VMEM((COLB, BS), jnp.float32),
            pltpu.SemaphoreType.DMA,
        ],
        4 * inflated.size,
        6 * inflated.size,
    )(place, sums, other, inflated)


def far_tile_kernel(n_right, bit, total_rows, with_sent, *refs):
    sums_s, sums, own_left = refs[:3]
    rights = refs[3 : 3 + n_right]
    rest = refs[3 + n_right :]
    sent = None
    if with_sent:
        sent, rest = rest[0], rest[1:]
    _, out, right, product, result, scale, right_sem, out_sem = rest
    layer = lax.axis_index("layer")
    copies = fetch_right(rights, right, right_sem)
    for copy in copies:
        copy.start()
    outs = []
    if with_sent:
        columns = pl.ds(pl.multiple_of((layer ^ 1) * OUT, OUT), OUT)
        outs.append(pltpu.make_async_copy(sent, out.at[:, columns], out_sem.at[1]))
        outs[0].start()
    scale[...] = 1.0 / (sums[0:COLB, :] / jnp.float32(total_rows) + 1e-6)
    for copy in copies:
        copy.wait()
    product[...] = jnp.dot(own_left[...], right[...], preferred_element_type=jnp.float32)
    bands = own_left.shape[0] // BS
    for i in range(bands):
        for s in range(KOL):
            row = layer * bands + i
            block = sums_s[META + s, row].astype(jnp.int32)
            keep = sums_s[META + KOL + s, row]
            picked = product[pl.ds(i * BS, BS), pl.ds(pl.multiple_of(block * BS, BS), BS)]
            squares = picked * picked * keep
            result[pl.ds(i * BS, BS), pl.ds(s * BS, BS)] = (
                squares * scale[pl.ds(block, 1), :]
            ).astype(result.dtype)
    columns = pl.ds(pl.multiple_of((layer ^ bit) * OUT, OUT), OUT)
    outs.append(pltpu.make_async_copy(result, out.at[:, columns], out_sem.at[0]))
    outs[-1].start()
    for copy in outs:
        copy.wait()


def far_tile(sums, own_left, rights, sent, out, bit, total_rows):
    band, inner = own_left.shape
    extra = [] if sent is None else [sent]
    operands = [sums, sums, own_left, *rights, *extra, out]
    return call(
        functools.partial(far_tile_kernel, len(rights), bit, total_rows, sent is not None),
        jax.ShapeDtypeStruct(out.shape, out.dtype),
        [SMEM, VMEM, VMEM] + [ANY] * (len(rights) + len(extra) + 1),
        ANY,
        [
            pltpu.VMEM((inner, TILE), jnp.bfloat16),
            pltpu.VMEM((band, TILE), jnp.float32),
            pltpu.VMEM((band, OUT), jnp.bfloat16),
            pltpu.VMEM((COLB, BS), jnp.float32),
            pltpu.SemaphoreType.DMA((len(rights),)),
            pltpu.SemaphoreType.DMA((2,)),
        ],
        2 * band * inner * TILE,
        2 * (band + TILE) * inner + 2 * band * OUT,
        {len(operands) - 1: 0},
    )(*operands)


def shards(
    source_matrix_strip,
    target_matrix_strip,
    stored_tile_flag,
    target_place_tile_index,
    retained_target_flag,
):
    layers = lax.axis_size("layer")
    total_rows = source_matrix_strip.shape[0] * lax.axis_size("row")
    place = target_place_tile_index.T
    keep = retained_target_flag.T
    masked = mask_blocks(stored_tile_flag.T, source_matrix_strip)
    lefts = gather(masked, "col")
    near = gather(target_matrix_strip, "row")
    far = swap(target_matrix_strip, "layer", 2)
    sums, inflated, own_left = own_tile(place, keep, lefts, near, layers)
    opposite = swap(far, "layer", 1)
    far_pieces = gather(far, "row")
    opposite_pieces = gather(opposite, "row")
    bit = lax.axis_size("row") // 2
    while bit > 1:
        other = swap(sums, "row", bit)
        sums = jnp.concatenate([sums[:COLB] + other[:COLB], sums[COLB:]])
        bit //= 2
    other = swap(sums, "row", 1)
    out, sent, sums = scale_own(place, sums, other, inflated, layers, total_rows)
    sent = swap(sent, "layer", 1)
    far_sums = swap(sums, "layer", 2)
    opposite_sums = swap(far_sums, "layer", 1)
    out = far_tile(far_sums, own_left, far_pieces, None, out, 2, total_rows)
    return far_tile(opposite_sums, own_left, opposite_pieces, sent, out, 3, total_rows)


def solution(mesh):
    placed = (
        P("row", "col"),
        P("row", ("col", "layer")),
        P("row", "col"),
        P("row", ("col", "layer")),
        P("row", ("col", "layer")),
    )
    return jax.shard_map(
        shards, mesh=mesh, in_specs=placed, out_specs=P(("row", "layer"), "col"), check_vma=False
    )
```

time: 97.3 us -> 58.6 us (0.60)
  blocking collectives: 44.5 us -> 0 us
  starting transfers between devices: 0.01 us -> 20.2 us
  between operations: 13.4 us -> 0.09 us
  waiting for transfers between devices: 14 us -> 26.6 us
  matrix products: 12.5 us -> 0 us
  Pallas kernels: 0 us -> 9.12 us
  other arithmetic: 5.11 us -> 0 us
  local copies, waits for them, and re-layouts: 7.34 us -> 2.37 us
    all_to_all x1 -> x0, blocking collectives: 29.4 us -> none  [shards(): lax.all_to_all(arranged, 'layer', split_axis=0, concat_axis=1, tiled=True)]
    ppermute x0 -> x12, waiting for transfers between devices: none -> 26.6 us  [swap(): return lax.ppermute(value, axis, [(i, i ^ bit) for i in range(count)])]
    ppermute x0 -> x12, starting transfers between devices: none -> 20.2 us  [swap(): return lax.ppermute(value, axis, [(i, i ^ bit) for i in range(count)])]
    all_gather x1 -> x0, waiting for transfers between devices: 14 us -> none  [shards(): lax.all_gather(masked, 'col', axis=1, tiled=True)]
    dot_general x4 -> x0, matrix products: 12.5 us -> none  [the longest x1 7.34 us: matrix_squaring_step(): jnp.einsum('rsc,rick->rsik', block_selector, product_blocks, precision=la...]
    all_gather x1 -> x0, blocking collectives: 10.2 us -> none  [shards(): right_whole = lax.all_gather(target_matrix_strip, 'row', axis=0, tiled=True)]
    pallas_call x0 -> x5, Pallas kernels: none -> 9.12 us  [the longest x2 3.84 us: far_tile(): call(functools.partial(far_tile_kernel, len(rights), bit, total_rows, sen...]
    reshape x1 -> x0, local copies, waits for them, and re-layouts: 5.23 us -> none  [matrix_squaring_step(): product_blocks = walk_matrix_result.reshape(block_rows, BS, COLB, BS)]
  transfers between devices with their start and end apart: 1 -> 12, of which waited for: 1 -> 5; matrix products, arithmetic and copies ran while one was open for 2% -> 0% of each run, Pallas kernels for 0% -> 11%
where the time goes in v1:
time: 58.6 us; the launch traced here: 58.4 us
  waiting for transfers between devices  26.6 us (45%)
  starting transfers between devices  20.2 us (34%)
  Pallas kernels  9.12 us (16%)
  local copies, waits for them, and re-layouts  2.37 us (4%)
    ppermute x12, waiting for transfers between devices, swap(): return lax.ppermute(value, axis, [(i, i ^ bit) for i in range(count)])  26.6 us
    ppermute x12, starting transfers between devices, swap(): return lax.ppermute(value, axis, [(i, i ^ bit) for i in range(count)])  20.2 us
    pallas_call x2, Pallas kernels, far_tile(): call(functools.partial(far_tile_kernel, len(rights), bit, total_rows, sen...  3.84 us
    pallas_call x1, Pallas kernels, own_tile(): call(functools.partial(own_tile_kernel, len(lefts), len(rights), layers),...  3.26 us
    unnamed x10, local copies, waits for them, and re-layouts  2.37 us
    pallas_call x1, Pallas kernels, scale_own(): call(functools.partial(scale_kernel, total_rows), (jax.ShapeDtypeStruct((...  1.36 us
  transfers between devices with their start and end apart: 12, of which 5 were waited for; matrix products, arithmetic and copies ran while one was open for 0% of the time, Pallas kernels for 11%

profile of v1, /device:TPU:0, one launch (start us, length us, event | category | flops | bytes accessed | tf_op | source)
XLA Modules:
  0.0 58.4 jit_solution(2473136446058631811)
XLA Ops:
  0.0 0.7 %copy-done.2 = s32[16,1]{0,1:T(1,128)S(1)} copy-done((s32[16,1]{0,1:T(1,128)S(1)}, s32[16,1]{0,1:T(1,128)}, u32[]{:S(2)}) %copy-start.2) | copy-done | bytes 88
  0.7 1.0 %copy-done = bf16[2048,128]{1,0:T(8,128)(2,1)S(1)} copy-done((bf16[2048,128]{1,0:T(8,128)(2,1)S(1)}, bf16[2048,128]{1,0:T(8,128)(2,1)}, u32[]{:S(2)}) %copy-start) | copy-done | bytes 524312
  1.7 0.7 %shard_map.55.refs_4_ = bf16[2048,128]{1,0:T(8,128)(2,1)S(1)} custom-call(s32[1,16]{1,0:T(1,128)S(1)} %bitcast.6, bf16[2048,128]{1,0:T(8,128)(2,1)S(1)} %copy-done), custom_call_target="tpu_custom_call" | custom-call | flops 262144 | bytes 1048576 | tf_op jit(solution)/shard_map/pallas_call | solution.py:61
  2.4 3.0 %collective-permute-start.1 = (bf16[2048,128]{1,0:T(8,128)(2,1)S(1)}, bf16[2048,128]{1,0:T(8,128)(2,1)S(1)}, u32[]{:S(2)}, u32[]{:S(2)}) collective-permute-start(bf16[2048,128]{1,0:T(8,128)(2,1)S(1)} %shard_map.55.refs_4_), channel_id=1, source_target_pairs={{0,8},{4,12},{8,0},{12,4},{1,9},{5,13},{9,1},{13,5},{2,10},{6,14},... | collective-permute-start | bytes 1572872 | tf_op jit(solution)/shard_map/ppermute | solution.py:25
  5.4 0.0 collective-permute-start
  5.4 11.9 %collective-permute-done.1.refs_6_ = bf16[2048,128]{1,0:T(8,128)(2,1)S(1)} collective-permute-done((bf16[2048,128]{1,0:T(8,128)(2,1)S(1)}, bf16[2048,128]{1,0:T(8,128)(2,1)S(1)}, u32[]{:S(2)}, u32[]{:S(2)}) %collective-permute-start.1) | collective-permute-done | bytes 524320 | tf_op jit(solution)/shard_map/ppermute | solution.py:25
  17.3 0.0 collective-permute-start.2
  17.3 2.8 %collective-permute-start.7 = (bf16[256,512]{1,0:T(8,128)(2,1)S(1)}, bf16[256,512]{1,0:T(8,128)(2,1)S(1)}, u32[]{:S(2)}, u32[]{:S(2)}) collective-permute-start(bf16[256,512]{1,0:T(8,128)(2,1)S(1)} %copy-done.3), channel_id=1, source_target_pairs={{0,2},{1,3},{2,0},{3,1},{4,6},{5,7},{6,4},{7,5},{8,10},{9,11},{10,... | collective-permute-start | bytes 786440 | tf_op jit(solution)/shard_map/ppermute | solution.py:25
  20.1 1.5 %collective-permute-start.3 = (bf16[256,512]{1,0:T(8,128)(2,1)S(1)}, bf16[256,512]{1,0:T(8,128)(2,1)S(1)}, u32[]{:S(2)}, u32[]{:S(2)}) collective-permute-start(bf16[256,512]{1,0:T(8,128)(2,1)S(1)} %copy-done.3), channel_id=1, source_target_pairs={{0,16},{16,0},{1,17},{17,1},{2,18},{18,2},{3,19},{19,3},{4,20},{20... | collective-permute-start | bytes 786440 | tf_op jit(solution)/shard_map/ppermute | solution.py:25
  21.6 11.1 %collective-permute-done.7.refs_3_ = bf16[256,512]{1,0:T(8,128)(2,1)S(1)} collective-permute-done((bf16[256,512]{1,0:T(8,128)(2,1)S(1)}, bf16[256,512]{1,0:T(8,128)(2,1)S(1)}, u32[]{:S(2)}, u32[]{:S(2)}) %collective-permute-start.7) | collective-permute-done | bytes 262176 | tf_op jit(solution)/shard_map/ppermute | solution.py:25
  32.7 0.7 %collective-permute-start.8 = (bf16[256,512]{1,0:T(8,128)(2,1)S(1)}, bf16[256,512]{1,0:T(8,128)(2,1)S(1)}, u32[]{:S(2)}, u32[]{:S(2)}) collective-permute-start(bf16[256,512]{1,0:T(8,128)(2,1)S(1)} %collective-permute-done.7.refs_3_), channel_id=1, source_target_pairs={{0,1},{1,0},{2,3},{3,2},{4,5},{5,4},{6,7},{7,6},{8,9},{9,8},{10,11... | collective-permute-start | bytes 786440 | tf_op jit(solution)/shard_map/ppermute | solution.py:25
  33.5 1.5 %collective-permute-start.11 = (bf16[256,512]{1,0:T(8,128)(2,1)S(1)}, bf16[256,512]{1,0:T(8,128)(2,1)S(1)}, u32[]{:S(2)}, u32[]{:S(2)}) collective-permute-start(bf16[256,512]{1,0:T(8,128)(2,1)S(1)} %collective-permute-done.7.refs_3_), channel_id=1, source_target_pairs={{0,16},{16,0},{1,17},{17,1},{2,18},{18,2},{3,19},{19,3},{4,20},{20... | collective-permute-start | bytes 786440 | tf_op jit(solution)/shard_map/ppermute | solution.py:25
  35.0 0.0 collective-permute-done.3.refs_9_
  35.0 0.0 collective-permute-done.refs_5_
  35.0 0.0 collective-permute-done.2.refs_7_
  35.0 0.0 copy-start.1
  35.0 0.7 %copy-done.1 = s32[16,2]{0,1:T(2,128)S(1)} copy-done((s32[16,2]{0,1:T(2,128)S(1)}, s32[16,2]{0,1:T(2,128)}, u32[]{:S(2)}) %copy-start.1) | copy-done | bytes 152
  35.7 3.3 %shard_map.56 = (f32[8,128]{1,0:T(8,128)S(1)}, f32[1024,256]{1,0:T(8,128)S(1)}, bf16[512,512]{1,0:T(8,128)(2,1)S(1)}) custom-call(s32[2,16]{1,0:T(2,128)S(1)} %bitcast.3, s32[2,16]{1,0:T(2,128)S(1)} %bitcast.7, s32[2,16]{1,0:T(2,128)S(1)} %bitcast.4, s32[2,16]{1,0:T(2,128)S(1)} %bitcast.8, bf16[2048,128]{1,0:T(8,128)(2,1)S(1)} %shard_map.55.refs_4_, ...), custom_call_target="tpu_custom_call" | custom-call | flops 1073741824 | bytes 4718592 | tf_op jit(solution)/shard_map/pallas_call | solution.py:145
  38.9 0.6 %collective-permute-start.4 = (f32[8,128]{1,0:T(8,128)S(1)}, f32[8,128]{1,0:T(8,128)S(1)}, u32[]{:S(2)}, u32[]{:S(2)}) collective-permute-start(f32[8,128]{1,0:T(8,128)S(1)} %get-tuple-element.11.sums), channel_id=1, source_target_pairs={{0,16},{16,0},{1,17},{17,1},{2,18},{18,2},{3,19},{19,3},{4,20},{20... | collective-permute-start | bytes 12296 | tf_op jit(solution)/shard_map/ppermute | solution.py:25
  39.5 1.2 %collective-permute-done.8.refs_3_ = bf16[256,512]{1,0:T(8,128)(2,1)S(1)} collective-permute-done((bf16[256,512]{1,0:T(8,128)(2,1)S(1)}, bf16[256,512]{1,0:T(8,128)(2,1)S(1)}, u32[]{:S(2)}, u32[]{:S(2)}) %collective-permute-start.8) | collective-permute-done | bytes 262176 | tf_op jit(solution)/shard_map/ppermute | solution.py:25
  40.8 1.5 %collective-permute-start.9 = (bf16[256,512]{1,0:T(8,128)(2,1)S(1)}, bf16[256,512]{1,0:T(8,128)(2,1)S(1)}, u32[]{:S(2)}, u32[]{:S(2)}) collective-permute-start(bf16[256,512]{1,0:T(8,128)(2,1)S(1)} %collective-permute-done.8.refs_3_), channel_id=1, source_target_pairs={{0,16},{16,0},{1,17},{17,1},{2,18},{18,2},{3,19},{19,3},{4,20},{20... | collective-permute-start | bytes 786440 | tf_op jit(solution)/shard_map/ppermute | solution.py:25
  42.2 0.4 collective-permute-done.4.other
  42.7 1.4 %shard_map.57 = (bf16[512,1024]{1,0:T(8,128)(2,1)}, bf16[512,256]{1,0:T(8,128)(2,1)S(1)}, f32[8,128]{1,0:T(8,128)S(1)}) custom-call(s32[2,16]{1,0:T(2,128)S(1)} %bitcast.5, f32[8,128]{1,0:T(8,128)S(1)} %get-tuple-element.11.sums, f32[8,128]{1,0:T(8,128)S(1)} %collective-permute-done.4.other, f32[1024,256]{1,0:T(8,128)S(1)} %get-tuple-element.12.inflated), custom_call_target="tpu_custom_call" | custom-call | flops 1048576 | bytes 1572864 | tf_op jit(solution)/shard_map/pallas_call | solution.py:192
  44.0 1.4 %collective-permute-start.10 = (bf16[512,256]{1,0:T(8,128)(2,1)S(1)}, bf16[512,256]{1,0:T(8,128)(2,1)S(1)}, u32[]{:S(2)}, u32[]{:S(2)}) collective-permute-start(bf16[512,256]{1,0:T(8,128)(2,1)S(1)} %get-tuple-element.15), channel_id=1, source_target_pairs={{0,1},{1,0},{2,3},{3,2},{4,5},{5,4},{6,7},{7,6},{8,9},{9,8},{10,11... | collective-permute-start | bytes 786440 | tf_op jit(solution)/shard_map/ppermute | solution.py:25
  45.4 2.7 %collective-permute-start.5 = (f32[8,128]{1,0:T(8,128)S(1)}, f32[8,128]{1,0:T(8,128)S(1)}, u32[]{:S(2)}, u32[]{:S(2)}) collective-permute-start(f32[8,128]{1,0:T(8,128)S(1)} %get-tuple-element.13), channel_id=1, source_target_pairs={{0,2},{1,3},{2,0},{3,1},{4,6},{5,7},{6,4},{7,5},{8,10},{9,11},{10,... | collective-permute-start | bytes 12296 | tf_op jit(solution)/shard_map/ppermute | solution.py:25
  48.1 1.9 %collective-permute-done.5.refs_0_.refs_1_ = f32[8,128]{1,0:T(8,128)S(1)} collective-permute-done((f32[8,128]{1,0:T(8,128)S(1)}, f32[8,128]{1,0:T(8,128)S(1)}, u32[]{:S(2)}, u32[]{:S(2)}) %collective-permute-start.5) | collective-permute-done | bytes 4128 | tf_op jit(solution)/shard_map/ppermute | solution.py:25
  50.0 4.5 %collective-permute-start.6 = (f32[8,128]{1,0:T(8,128)S(1)}, f32[8,128]{1,0:T(8,128)S(1)}, u32[]{:S(2)}, u32[]{:S(2)}) collective-permute-start(f32[8,128]{1,0:T(8,128)S(1)} %collective-permute-done.5.refs_0_.refs_1_), channel_id=1, source_target_pairs={{0,1},{1,0},{2,3},{3,2},{4,5},{5,4},{6,7},{7,6},{8,9},{9,8},{10,11... | collective-permute-start | bytes 12296 | tf_op jit(solution)/shard_map/ppermute | solution.py:25
  54.5 0.0 collective-permute-done.11.refs_4_
  54.5 1.9 %shard_map.58.refs_6_ = bf16[512,1024]{1,0:T(8,128)(2,1)} custom-call(f32[8,128]{1,0:T(8,128)S(1)} %collective-permute-done.5.refs_0_.refs_1_, f32[8,128]{1,0:T(8,128)S(1)} %collective-permute-done.5.refs_0_.refs_1_, bf16[512,512]{1,0:T(8,128)(2,1)S(1)} %get-tuple-element.14.refs_2_, ...), custom_call_target="tpu_custom_call", output_to_operand_aliasing={{}: (5, {})} | custom-call | flops 268435456 | bytes 1310720 | tf_op jit(solution)/shard_map/pallas_call | solution.py:254
  56.4 0.0 collective-permute-done.9.refs_4_
  56.5 0.0 collective-permute-done.6.refs_0_.refs_1_
  56.5 1.9 %shard_map.59 = bf16[512,1024]{1,0:T(8,128)(2,1)} custom-call(f32[8,128]{1,0:T(8,128)S(1)} %collective-permute-done.6.refs_0_.refs_1_, f32[8,128]{1,0:T(8,128)S(1)} %collective-permute-done.6.refs_0_.refs_1_, bf16[512,512]{1,0:T(8,128)(2,1)S(1)} %get-tuple-element.14.refs_2_, ...), custom_call_target="tpu_custom_call", output_to_operand_aliasing={{}: (6, {})} | custom-call | flops 268435456 | bytes 1310720 | tf_op jit(solution)/shard_map/pallas_call | solution.py:254
  (7 shorter events, 0.0 us)
Async XLA Ops:
  0.0 0.7 %copy-start.2 = (s32[16,1]{0,1:T(1,128)S(1)}, s32[16,1]{0,1:T(1,128)}, u32[]{:S(2)}) copy-start(s32[16,1]{0,1:T(1,128)} %param.7) | copy-start | bytes 196
  0.7 1.0 %copy-start = (bf16[2048,128]{1,0:T(8,128)(2,1)S(1)}, bf16[2048,128]{1,0:T(8,128)(2,1)}, u32[]{:S(2)}) copy-start(bf16[2048,128]{1,0:T(8,128)(2,1)} %source.1) | copy-start | bytes 1572868
  1.7 15.6 %copy-start.3 = (bf16[256,512]{1,0:T(8,128)(2,1)S(1)}, bf16[256,512]{1,0:T(8,128)(2,1)}, u32[]{:S(2)}) copy-start(bf16[256,512]{1,0:T(8,128)(2,1)} %refs_8_.1) | copy-start | bytes 786436
  1.7 33.3 %copy-start.4 = (s32[16,2]{0,1:T(2,128)S(1)}, s32[16,2]{0,1:T(2,128)}, u32[]{:S(2)}) copy-start(s32[16,2]{0,1:T(2,128)} %param.9) | copy-start | bytes 388
  2.4 15.0 %collective-permute-start.1 = (bf16[2048,128]{1,0:T(8,128)(2,1)S(1)}, bf16[2048,128]{1,0:T(8,128)(2,1)S(1)}, u32[]{:S(2)}, u32[]{:S(2)}) collective-permute-start(bf16[2048,128]{1,0:T(8,128)(2,1)S(1)} %shard_map.55.refs_4_), channel_id=1, source_target_pairs={{0,8},{4,12},{8,0},{12,4},{1,9},{5,13},{9,1},{13,5},{2,10},{6,14},... | collective-permute-start | bytes 1572872 | tf_op jit(solution)/shard_map/ppermute | solution.py:25
  5.4 29.6 %collective-permute-start = (bf16[2048,128]{1,0:T(8,128)(2,1)S(1)}, bf16[2048,128]{1,0:T(8,128)(2,1)S(1)}, u32[]{:S(2)}, u32[]{:S(2)}) collective-permute-start(bf16[2048,128]{1,0:T(8,128)(2,1)S(1)} %shard_map.55.refs_4_), channel_id=1, source_target_pairs={{0,4},{4,0},{8,12},{12,8},{1,5},{5,1},{9,13},{13,9},{2,6},{6,2},{1... | collective-permute-start | bytes 1572872 | tf_op jit(solution)/shard_map/ppermute | solution.py:25
  17.3 17.7 %collective-permute-start.2 = (bf16[2048,128]{1,0:T(8,128)(2,1)S(1)}, bf16[2048,128]{1,0:T(8,128)(2,1)S(1)}, u32[]{:S(2)}, u32[]{:S(2)}) collective-permute-start(bf16[2048,128]{1,0:T(8,128)(2,1)S(1)} %collective-permute-done.1.refs_6_), channel_id=1, source_target_pairs={{0,4},{4,0},{8,12},{12,8},{1,5},{5,1},{9,13},{13,9},{2,6},{6,2},{1... | collective-permute-start | bytes 1572872 | tf_op jit(solution)/shard_map/ppermute | solution.py:25
  17.3 15.4 %collective-permute-start.7 = (bf16[256,512]{1,0:T(8,128)(2,1)S(1)}, bf16[256,512]{1,0:T(8,128)(2,1)S(1)}, u32[]{:S(2)}, u32[]{:S(2)}) collective-permute-start(bf16[256,512]{1,0:T(8,128)(2,1)S(1)} %copy-done.3), channel_id=1, source_target_pairs={{0,2},{1,3},{2,0},{3,1},{4,6},{5,7},{6,4},{7,5},{8,10},{9,11},{10,... | collective-permute-start | bytes 786440 | tf_op jit(solution)/shard_map/ppermute | solution.py:25
  20.1 14.8 %collective-permute-start.3 = (bf16[256,512]{1,0:T(8,128)(2,1)S(1)}, bf16[256,512]{1,0:T(8,128)(2,1)S(1)}, u32[]{:S(2)}, u32[]{:S(2)}) collective-permute-start(bf16[256,512]{1,0:T(8,128)(2,1)S(1)} %copy-done.3), channel_id=1, source_target_pairs={{0,16},{16,0},{1,17},{17,1},{2,18},{18,2},{3,19},{19,3},{4,20},{20... | collective-permute-start | bytes 786440 | tf_op jit(solution)/shard_map/ppermute | solution.py:25
  32.7 8.0 %collective-permute-start.8 = (bf16[256,512]{1,0:T(8,128)(2,1)S(1)}, bf16[256,512]{1,0:T(8,128)(2,1)S(1)}, u32[]{:S(2)}, u32[]{:S(2)}) collective-permute-start(bf16[256,512]{1,0:T(8,128)(2,1)S(1)} %collective-permute-done.7.refs_3_), channel_id=1, source_target_pairs={{0,1},{1,0},{2,3},{3,2},{4,5},{5,4},{6,7},{7,6},{8,9},{9,8},{10,11... | collective-permute-start | bytes 786440 | tf_op jit(solution)/shard_map/ppermute | solution.py:25
  33.5 21.0 %collective-permute-start.11 = (bf16[256,512]{1,0:T(8,128)(2,1)S(1)}, bf16[256,512]{1,0:T(8,128)(2,1)S(1)}, u32[]{:S(2)}, u32[]{:S(2)}) collective-permute-start(bf16[256,512]{1,0:T(8,128)(2,1)S(1)} %collective-permute-done.7.refs_3_), channel_id=1, source_target_pairs={{0,16},{16,0},{1,17},{17,1},{2,18},{18,2},{3,19},{19,3},{4,20},{20... | collective-permute-start | bytes 786440 | tf_op jit(solution)/shard_map/ppermute | solution.py:25
  35.0 0.7 %copy-start.1 = (s32[16,2]{0,1:T(2,128)S(1)}, s32[16,2]{0,1:T(2,128)}, u32[]{:S(2)}) copy-start(s32[16,2]{0,1:T(2,128)} %param.8) | copy-start | bytes 388
  38.9 3.7 %collective-permute-start.4 = (f32[8,128]{1,0:T(8,128)S(1)}, f32[8,128]{1,0:T(8,128)S(1)}, u32[]{:S(2)}, u32[]{:S(2)}) collective-permute-start(f32[8,128]{1,0:T(8,128)S(1)} %get-tuple-element.11.sums), channel_id=1, source_target_pairs={{0,16},{16,0},{1,17},{17,1},{2,18},{18,2},{3,19},{19,3},{4,20},{20... | collective-permute-start | bytes 12296 | tf_op jit(solution)/shard_map/ppermute | solution.py:25
  40.8 15.7 %collective-permute-start.9 = (bf16[256,512]{1,0:T(8,128)(2,1)S(1)}, bf16[256,512]{1,0:T(8,128)(2,1)S(1)}, u32[]{:S(2)}, u32[]{:S(2)}) collective-permute-start(bf16[256,512]{1,0:T(8,128)(2,1)S(1)} %collective-permute-done.8.refs_3_), channel_id=1, source_target_pairs={{0,16},{16,0},{1,17},{17,1},{2,18},{18,2},{3,19},{19,3},{4,20},{20... | collective-permute-start | bytes 786440 | tf_op jit(solution)/shard_map/ppermute | solution.py:25
  44.0 12.4 %collective-permute-start.10 = (bf16[512,256]{1,0:T(8,128)(2,1)S(1)}, bf16[512,256]{1,0:T(8,128)(2,1)S(1)}, u32[]{:S(2)}, u32[]{:S(2)}) collective-permute-start(bf16[512,256]{1,0:T(8,128)(2,1)S(1)} %get-tuple-element.15), channel_id=1, source_target_pairs={{0,1},{1,0},{2,3},{3,2},{4,5},{5,4},{6,7},{7,6},{8,9},{9,8},{10,11... | collective-permute-start | bytes 786440 | tf_op jit(solution)/shard_map/ppermute | solution.py:25
  45.4 4.6 %collective-permute-start.5 = (f32[8,128]{1,0:T(8,128)S(1)}, f32[8,128]{1,0:T(8,128)S(1)}, u32[]{:S(2)}, u32[]{:S(2)}) collective-permute-start(f32[8,128]{1,0:T(8,128)S(1)} %get-tuple-element.13), channel_id=1, source_target_pairs={{0,2},{1,3},{2,0},{3,1},{4,6},{5,7},{6,4},{7,5},{8,10},{9,11},{10,... | collective-permute-start | bytes 12296 | tf_op jit(solution)/shard_map/ppermute | solution.py:25
  50.0 6.5 %collective-permute-start.6 = (f32[8,128]{1,0:T(8,128)S(1)}, f32[8,128]{1,0:T(8,128)S(1)}, u32[]{:S(2)}, u32[]{:S(2)}) collective-permute-start(f32[8,128]{1,0:T(8,128)S(1)} %collective-permute-done.5.refs_0_.refs_1_), channel_id=1, source_target_pairs={{0,1},{1,0},{2,3},{3,2},{4,5},{5,4},{6,7},{7,6},{8,9},{9,8},{10,11... | collective-permute-start | bytes 12296 | tf_op jit(solution)/shard_map/ppermute | solution.py:25

commit v2 on v1

v2 whole, which is shorter than its diff:
```python
import functools

import jax
import jax.numpy as jnp
from jax import lax
from jax.experimental import pallas as pl
from jax.experimental.pallas import tpu as pltpu
from jax.sharding import PartitionSpec as P

BS = 128
COLB = 4
KOL = 2
TILE = COLB * BS
OUT = KOL * BS
META = COLB
VMEM_LIMIT = 48 * 1024 * 1024

ANY = pl.BlockSpec(memory_space=pl.ANY)
VMEM = pl.BlockSpec(memory_space=pltpu.VMEM)
SMEM = pl.BlockSpec(memory_space=pltpu.SMEM)


def swap(value, axis, bit):
    count = lax.axis_size(axis)
    return lax.ppermute(value, axis, [(i, i ^ bit) for i in range(count)])


def spread(piece, axis, count):
    pieces = {0: piece}
    bit = count // 2
    while bit:
        for k in list(pieces):
            pieces[k ^ bit] = swap(pieces[k], axis, bit)
        bit //= 2
    return [pieces[k] for k in range(count)]


def gather(piece, axis):
    return spread(piece, axis, lax.axis_size(axis))


def call(kernel, out_shape, in_specs, out_specs, scratch, flops, nbytes, aliases=None):
    return pl.pallas_call(
        kernel,
        out_shape=out_shape,
        in_specs=in_specs,
        out_specs=out_specs,
        scratch_shapes=scratch,
        input_output_aliases=aliases or {},
        compiler_params=pltpu.CompilerParams(vmem_limit_bytes=VMEM_LIMIT),
        cost_estimate=pl.CostEstimate(flops=flops, bytes_accessed=nbytes, transcendentals=0),
    )


def mask_kernel(flag, source, masked):
    for i in range(source.shape[0] // BS):
        rows = pl.ds(i * BS, BS)
        block = source[rows, :]
        masked[rows, :] = jnp.where(flag[0, i] != 0, block, jnp.zeros_like(block))


def mask_blocks(flag, source):
    size = source.size * 2
    return call(
        mask_kernel,
        jax.ShapeDtypeStruct(source.shape, source.dtype),
        [SMEM, VMEM],
        VMEM,
        [],
        source.size,
        2 * size,
    )(flag, source)


def fetch_right(rights, panel, sem):
    me = lax.axis_index("row")
    depth = rights[0].shape[0]
    copies = []
    for k, right in enumerate(rights):
        place = pl.ds(pl.multiple_of((me ^ k) * depth, depth), depth)
        copies.append(pltpu.make_async_copy(right, panel.at[place, :], sem.at[k]))
    return copies


def partial_product(lefts, first_k, right, rows):
    me = lax.axis_index("col")
    deep = jnp.concatenate([left[rows, :] for left in lefts], axis=1)
    blocks = []
    for k in range(len(lefts)):
        place = pl.ds(pl.multiple_of((me ^ (first_k + k)) * BS, BS), BS)
        blocks.append(right[place, :])
    return jnp.dot(deep, jnp.concatenate(blocks, axis=0), preferred_element_type=jnp.float32)


def early_kernel(n_left, n_right, band, *refs):
    place = refs[0]
    lefts = refs[1 : 1 + n_left]
    rights = refs[1 + n_left : 1 + n_left + n_right]
    right, picked, product, sem = refs[1 + n_left + n_right :]
    copies = fetch_right(rights, right, sem)
    for copy in copies:
        copy.start()
    for copy in copies:
        copy.wait()

    @pl.loop(0, picked.shape[0] // band)
    def _(q):
        first = pl.multiple_of(q * band, band)
        product[...] = partial_product(lefts, 0, right, pl.ds(first, band))
        for i in range(band // BS):
            rows = pl.ds(pl.multiple_of(first + i * BS, BS), BS)
            for s in range(KOL):
                block = place[s, q * (band // BS) + i]
                picked[rows, pl.ds(s * BS, BS)] = product[
                    pl.ds(i * BS, BS), pl.ds(pl.multiple_of(block * BS, BS), BS)
                ]


def early(place, lefts, rights, band):
    rows = lefts[0].shape[0]
    inner = sum(right.shape[0] for right in rights)
    return call(
        functools.partial(early_kernel, len(lefts), len(rights), band),
        (
            jax.ShapeDtypeStruct((inner, TILE), jnp.bfloat16),
            jax.ShapeDtypeStruct((rows, OUT), jnp.float32),
        ),
        [SMEM] + [VMEM] * len(lefts) + [ANY] * len(rights),
        (VMEM, VMEM),
        [pltpu.VMEM((band, TILE), jnp.float32), pltpu.SemaphoreType.DMA((len(rights),))],
        rows * inner * TILE,
        2 * (rows // 2 + TILE) * inner + 4 * rows * OUT,
    )(place, *lefts, *rights)


def late_kernel(n_left, band, place, keep, place_v, keep_v, right, picked, *refs):
    lefts = refs[:n_left]
    sums, meta, inflated, own_left, product, partial = refs[n_left:]
    lates = lefts[n_left // 2 :]
    layer = lax.axis_index("layer")
    me = lax.axis_index("col")
    partial[...] = jnp.zeros_like(partial)

    @pl.loop(0, picked.shape[0] // band)
    def _(q):
        first = pl.multiple_of(q * band, band)
        product[...] = partial_product(lates, n_left // 2, right, pl.ds(first, band))
        for i in range(band // BS):
            rows = pl.ds(pl.multiple_of(first + i * BS, BS), BS)
            for s in range(KOL):
                row = q * (band // BS) + i
                block = place[s, row]
                late = product[pl.ds(i * BS, BS), pl.ds(pl.multiple_of(block * BS, BS), BS)]
                whole = picked[rows, pl.ds(s * BS, BS)] + late
                squares = whole * whole * keep[s, row].astype(jnp.float32)
                partial[block] += jnp.sum(squares.reshape(BS // 8, 8, BS), axis=0)
                for part in range(2):

                    @pl.when(q == layer ^ part)
                    def _():
                        inflated[pl.ds(part * band + i * BS, BS), pl.ds(s * BS, BS)] = squares

    for block in range(COLB):
        sums[pl.ds(block, 1), :] = jnp.sum(partial[block], axis=0, keepdims=True)
    bands = place_v.shape[1]
    meta[...] = jnp.zeros_like(meta)
    meta[0:KOL, 0:bands] = place_v[...].astype(jnp.float32)
    meta[KOL : 2 * KOL, 0:bands] = keep_v[...].astype(jnp.float32)
    own_rows = pl.ds(pl.multiple_of(layer * band, band), band)
    for k, left in enumerate(lefts):
        place_k = pl.ds(pl.multiple_of((me ^ k) * BS, BS), BS)
        own_left[:, place_k] = left[own_rows, :]


def late(place, keep, right, picked, lefts, band):
    rows = picked.shape[0]
    inner = right.shape[0]
    return call(
        functools.partial(late_kernel, len(lefts), band),
        (
            jax.ShapeDtypeStruct((COLB, BS), jnp.float32),
            jax.ShapeDtypeStruct((2 * KOL, BS), jnp.float32),
            jax.ShapeDtypeStruct((2 * band, OUT), jnp.float32),
            jax.ShapeDtypeStruct((band, inner), jnp.bfloat16),
        ),
        [SMEM, SMEM] + [VMEM] * (4 + len(lefts)),
        (VMEM, VMEM, VMEM, VMEM),
        [pltpu.VMEM((band, TILE), jnp.float32), pltpu.VMEM((COLB, 8, BS), jnp.float32)],
        rows * inner * TILE,
        2 * (rows // 2 + TILE) * inner + 4 * rows * OUT,
    )(place, keep, place, keep, right, picked, *lefts)


def scaled(place_of, inflated, first, scale, target):
    for i in range(target.shape[0] // BS):
        for s in range(KOL):
            at = (pl.ds(first + i * BS, BS), pl.ds(s * BS, BS))
            to = (pl.ds(i * BS, BS), pl.ds(s * BS, BS))
            row = scale[pl.ds(place_of(s, i), 1), :]
            target[to] = (inflated[at] * row).astype(target.dtype)


def scale_kernel(total_rows, place, sums, other, meta, inflated, sent, all_sums, scale):
    layer = lax.axis_index("layer")
    whole = sums[...] + other[...]
    all_sums[0:COLB, :] = whole
    all_sums[META : META + 2 * KOL, :] = meta[...]
    scale[...] = 1.0 / (whole / jnp.float32(total_rows) + 1e-6)
    band = sent.shape[0]
    bands = band // BS
    scaled(lambda s, i: place[s, (layer ^ 1) * bands + i], inflated, band, scale, sent)


def scale_sent(place, sums, other, meta, inflated, total_rows):
    band = inflated.shape[0] // 2
    return call(
        functools.partial(scale_kernel, total_rows),
        (
            jax.ShapeDtypeStruct((band, OUT), jnp.bfloat16),
            jax.ShapeDtypeStruct((COLB + 2 * KOL, BS), jnp.float32),
        ),
        [SMEM, VMEM, VMEM, VMEM, VMEM],
        (VMEM, VMEM),
        [pltpu.VMEM((COLB, BS), jnp.float32)],
        2 * inflated.size,
        3 * inflated.size,
    )(place, sums, other, meta, inflated)


def far_result(sums_s, sums, own_left, rights, total_rows, product, scale, result):
    layer = lax.axis_index("layer")
    me = lax.axis_index("row")
    scale[...] = 1.0 / (sums[0:COLB, :] / jnp.float32(total_rows) + 1e-6)
    depth = rights[0].shape[0]
    whole = None
    for k, right in enumerate(rights):
        place = pl.ds(pl.multiple_of((me ^ k) * depth, depth), depth)
        term = jnp.dot(own_left[:, place], right[...], preferred_element_type=jnp.float32)
        whole = term if whole is None else whole + term
    product[...] = whole
    bands = own_left.shape[0] // BS
    for i in range(bands):
        for s in range(KOL):
            row = layer * bands + i
            block = sums_s[META + s, row].astype(jnp.int32)
            keep = sums_s[META + KOL + s, row]
            picked = product[pl.ds(i * BS, BS), pl.ds(pl.multiple_of(block * BS, BS), BS)]
            squares = picked * picked * keep
            result[pl.ds(i * BS, BS), pl.ds(s * BS, BS)] = (
                squares * scale[pl.ds(block, 1), :]
            ).astype(result.dtype)


def columns_of(layer):
    return pl.ds(pl.multiple_of(layer * OUT, OUT), OUT)


def first_tiles_kernel(n_right, total_rows, place, sums_s, sums, own_left, own_sums, inflated, *refs):
    rights = refs[:n_right]
    out, product, scale, own, result, sem = refs[n_right:]
    layer = lax.axis_index("layer")
    scale[...] = 1.0 / (own_sums[0:COLB, :] / jnp.float32(total_rows) + 1e-6)
    bands = own.shape[0] // BS
    scaled(lambda s, i: place[s, layer * bands + i], inflated, 0, scale, own)
    own_copy = pltpu.make_async_copy(own, out.at[:, columns_of(layer)], sem.at[0])
    own_copy.start()
    far_result(sums_s, sums, own_left, rights, total_rows, product, scale, result)
    far_copy = pltpu.make_async_copy(result, out.at[:, columns_of(layer ^ 2)], sem.at[1])
    far_copy.start()
    own_copy.wait()
    far_copy.wait()


def first_tiles(place, sums, own_left, own_sums, inflated, rights, layers, total_rows):
    band, inner = own_left.shape
    return call(
        functools.partial(first_tiles_kernel, len(rights), total_rows),
        jax.ShapeDtypeStruct((band, layers * OUT), jnp.bfloat16),
        [SMEM, SMEM] + [VMEM] * (4 + len(rights)),
        ANY,
        [
            pltpu.VMEM((band, TILE), jnp.float32),
            pltpu.VMEM((COLB, BS), jnp.float32),
            pltpu.VMEM((band, OUT), jnp.bfloat16),
            pltpu.VMEM((band, OUT), jnp.bfloat16),
            pltpu.SemaphoreType.DMA((2,)),
        ],
        2 * band * inner * TILE,
        2 * (band + TILE) * inner + 2 * band * OUT,
    )(place, sums, sums, own_left, own_sums, inflated, *rights)


def last_tiles_kernel(n_right, total_rows, sums_s, sums, own_left, sent, *refs):
    rights = refs[:n_right]
    _, out, product, scale, result, sem = refs[n_right:]
    layer = lax.axis_index("layer")
    sent_copy = pltpu.make_async_copy(sent, out.at[:, columns_of(layer ^ 1)], sem.at[0])
    sent_copy.start()
    far_result(sums_s, sums, own_left, rights, total_rows, product, scale, result)
    far_copy = pltpu.make_async_copy(result, out.at[:, columns_of(layer ^ 3)], sem.at[1])
    far_copy.start()
    sent_copy.wait()
    far_copy.wait()


def last_tiles(sums, own_left, sent, rights, out, total_rows):
    band, inner = own_left.shape
    return call(
        functools.partial(last_tiles_kernel, len(rights), total_rows),
        jax.ShapeDtypeStruct(out.shape, out.dtype),
        [SMEM] + [VMEM] * (3 + len(rights)) + [ANY],
        ANY,
        [
            pltpu.VMEM((band, TILE), jnp.float32),
            pltpu.VMEM((COLB, BS), jnp.float32),
            pltpu.VMEM((band, OUT), jnp.bfloat16),
            pltpu.SemaphoreType.DMA((2,)),
        ],
        2 * band * inner * TILE,
        2 * (band + TILE) * inner + 2 * band * OUT,
        {4 + len(rights): 0},
    )(sums, sums, own_left, sent, *rights, out)


def shards(
    source_matrix_strip,
    target_matrix_strip,
    stored_tile_flag,
    target_place_tile_index,
    retained_target_flag,
):
    layers = lax.axis_size("layer")
    total_rows = source_matrix_strip.shape[0] * lax.axis_size("row")
    band = source_matrix_strip.shape[0] // layers
    place = target_place_tile_index.T
    keep = retained_target_flag.T
    half = lax.axis_size("col") // 2
    far = swap(target_matrix_strip, "layer", 2)
    masked = mask_blocks(stored_tile_flag.T, source_matrix_strip)
    across = swap(masked, "col", half)
    near = gather(target_matrix_strip, "row")
    earlies = spread(masked, "col", half)
    right, picked = early(place, earlies, near, band)
    across, far, picked = lax.optimization_barrier((across, far, picked))
    opposite = swap(far, "layer", 1)
    lates = spread(across, "col", half)
    far_pieces = gather(far, "row")
    sums, meta, inflated, own_left = late(place, keep, right, picked, earlies + lates, band)
    opposite_pieces = gather(opposite, "row")
    bit = lax.axis_size("row") // 2
    while bit > 1:
        sums = sums + swap(sums, "row", bit)
        bit //= 2
    other = swap(sums, "row", 1)
    sent, sums = scale_sent(place, sums, other, meta, inflated, total_rows)
    sent = swap(sent, "layer", 1)
    far_sums = swap(sums, "layer", 2)
    opposite_sums = swap(sums, "layer", 3)
    out = first_tiles(place, far_sums, own_left, sums, inflated, far_pieces, layers, total_rows)
    return last_tiles(opposite_sums, own_left, sent, opposite_pieces, out, total_rows)


def solution(mesh):
    placed = (
        P("row", "col"),
        P("row", ("col", "layer")),
        P("row", "col"),
        P("row", ("col", "layer")),
        P("row", ("col", "layer")),
    )
    return jax.shard_map(
        shards, mesh=mesh, in_specs=placed, out_specs=P(("row", "layer"), "col"), check_vma=False
    )
```

time: 58.6 us -> 44.3 us (0.76)
  waiting for transfers between devices: 26.6 us -> 13.8 us
  starting transfers between devices: 20.2 us -> 14.6 us
  local copies, waits for them, and re-layouts: 2.37 us -> 4.67 us
  Pallas kernels: 9.12 us -> 10.9 us
    ppermute x12, waiting for transfers between devices: 26.6 us -> 13.8 us  [swap(): return lax.ppermute(value, axis, [(i, i ^ bit) for i in range(count)])]
    ppermute x12, starting transfers between devices: 20.2 us -> 14.6 us  [swap(): return lax.ppermute(value, axis, [(i, i ^ bit) for i in range(count)])]
    unnamed x10 -> x12, local copies, waits for them, and re-layouts: 2.37 us -> 4.67 us
    pallas_call x4 -> x5, Pallas kernels: 8.46 us -> 10.3 us  [the longest x1 3.84 us: late(): call(functools.partial(late_kernel, len(lefts), band), (jax.ShapeDtypeStr...]
  transfers between devices with their start and end apart: 12 -> 12, of which waited for: 5 -> 7; matrix products, arithmetic and copies ran while one was open for 0% -> 0% of each run, Pallas kernels for 11% -> 19%
where the time goes in v2:
time: 44.3 us; the launch traced here: 44.1 us
  starting transfers between devices  14.6 us (33%)
  waiting for transfers between devices  13.8 us (31%)
  Pallas kernels  10.9 us (25%)
  local copies, waits for them, and re-layouts  4.67 us (11%)
    ppermute x12, starting transfers between devices, swap(): return lax.ppermute(value, axis, [(i, i ^ bit) for i in range(count)])  14.6 us
    ppermute x12, waiting for transfers between devices, swap(): return lax.ppermute(value, axis, [(i, i ^ bit) for i in range(count)])  13.8 us
    unnamed x12, local copies, waits for them, and re-layouts  4.67 us
    pallas_call x1, Pallas kernels, late(): call(functools.partial(late_kernel, len(lefts), band), (jax.ShapeDtypeStr...  3.84 us
    pallas_call x1, Pallas kernels, early(): call(functools.partial(early_kernel, len(lefts), len(rights), band), (jax...  2.08 us
    pallas_call x1, Pallas kernels, first_tiles(): call(functools.partial(first_tiles_kernel, len(rights), total_rows), jax....  1.92 us
    pallas_call x1, Pallas kernels, last_tiles(): call(functools.partial(last_tiles_kernel, len(rights), total_rows), jax.S...  1.84 us
  transfers between devices with their start and end apart: 12, of which 7 were waited for; matrix products, arithmetic and copies ran while one was open for 0% of the time, Pallas kernels for 19%

profile of v2, /device:TPU:0, one launch (start us, length us, event | category | flops | bytes accessed | tf_op | source)
XLA Modules:
  0.0 44.1 jit_solution(3790418375537686395)
XLA Ops:
  0.0 1.1 %copy-done.1 = bf16[2048,128]{1,0:T(8,128)(2,1)S(1)} copy-done((bf16[2048,128]{1,0:T(8,128)(2,1)S(1)}, bf16[2048,128]{1,0:T(8,128)(2,1)}, u32[]{:S(2)}) %copy-start.1) | copy-done | bytes 524312
  1.1 0.7 %copy-done.4 = s32[16,1]{0,1:T(1,128)S(1)} copy-done((s32[16,1]{0,1:T(1,128)S(1)}, s32[16,1]{0,1:T(1,128)}, u32[]{:S(2)}) %copy-start.4) | copy-done | bytes 88
  1.7 0.7 %shard_map.55.refs_1_.refs_0_ = bf16[2048,128]{1,0:T(8,128)(2,1)S(1)} custom-call(s32[1,16]{1,0:T(1,128)S(1)} %bitcast.10, bf16[2048,128]{1,0:T(8,128)(2,1)S(1)} %copy-done.1), custom_call_target="tpu_custom_call" | custom-call | flops 262144 | bytes 1048576 | tf_op jit(solution)/shard_map/pallas_call | solution.py:64
  2.4 0.5 %collective-permute-start = (bf16[2048,128]{1,0:T(8,128)(2,1)S(1)}, bf16[2048,128]{1,0:T(8,128)(2,1)S(1)}, u32[]{:S(2)}, u32[]{:S(2)}) collective-permute-start(bf16[2048,128]{1,0:T(8,128)(2,1)S(1)} %shard_map.55.refs_1_.refs_0_), channel_id=1, source_target_pairs={{0,4},{4,0},{8,12},{12,8},{1,5},{5,1},{9,13},{13,9},{2,6},{6,2},{1... | collective-permute-start | bytes 1572872 | tf_op jit(solution)/shard_map/ppermute | solution.py:25
  2.9 2.6 %collective-permute-start.2 = (bf16[2048,128]{1,0:T(8,128)(2,1)S(1)}, bf16[2048,128]{1,0:T(8,128)(2,1)S(1)}, u32[]{:S(2)}, u32[]{:S(2)}) collective-permute-start(bf16[2048,128]{1,0:T(8,128)(2,1)S(1)} %shard_map.55.refs_1_.refs_0_), channel_id=1, source_target_pairs={{0,8},{4,12},{8,0},{12,4},{1,9},{5,13},{9,1},{13,5},{2,10},{6,14},... | collective-permute-start | bytes 1572872 | tf_op jit(solution)/shard_map/ppermute | solution.py:25
  5.5 1.5 %collective-permute-start.1 = (bf16[256,512]{1,0:T(8,128)(2,1)}, bf16[256,512]{1,0:T(8,128)(2,1)S(1)}, u32[]{:S(2)}, u32[]{:S(2)}) collective-permute-start(bf16[256,512]{1,0:T(8,128)(2,1)} %refs_3_.1), channel_id=1, source_target_pairs={{0,16},{16,0},{1,17},{17,1},{2,18},{18,2},{3,19},{19,3},{4,20},{20... | collective-permute-start | bytes 786440 | tf_op jit(solution)/shard_map/ppermute | solution.py:25
  7.0 2.6 %collective-permute-start.3 = (bf16[256,512]{1,0:T(8,128)(2,1)}, bf16[256,512]{1,0:T(8,128)(2,1)S(1)}, u32[]{:S(2)}, u32[]{:S(2)}) collective-permute-start(bf16[256,512]{1,0:T(8,128)(2,1)} %refs_3_.1), channel_id=1, source_target_pairs={{0,2},{1,3},{2,0},{3,1},{4,6},{5,7},{6,4},{7,5},{8,10},{9,11},{10,... | collective-permute-start | bytes 786440 | tf_op jit(solution)/shard_map/ppermute | solution.py:25
  9.6 4.5 %collective-permute-done.1.refs_4_ = bf16[256,512]{1,0:T(8,128)(2,1)S(1)} collective-permute-done((bf16[256,512]{1,0:T(8,128)(2,1)}, bf16[256,512]{1,0:T(8,128)(2,1)S(1)}, u32[]{:S(2)}, u32[]{:S(2)}) %collective-permute-start.1) | collective-permute-done | bytes 262176 | tf_op jit(solution)/shard_map/ppermute | solution.py:25
  14.1 0.0 collective-permute-done.refs_2_.refs_1_
  14.1 0.7 %copy-done.2 = s32[16,2]{0,1:T(2,128)S(1)} copy-done((s32[16,2]{0,1:T(2,128)S(1)}, s32[16,2]{0,1:T(2,128)}, u32[]{:S(2)}) %copy-start.2) | copy-done | bytes 152
  14.8 0.9 %copy-done.5 = bf16[256,512]{1,0:T(8,128)(2,1)S(1)} copy-done((bf16[256,512]{1,0:T(8,128)(2,1)S(1)}, bf16[256,512]{1,0:T(8,128)(2,1)}, u32[]{:S(2)}) %copy-start.5) | copy-done | bytes 262168
  15.7 2.1 %shard_map.56 = (bf16[512,512]{1,0:T(8,128)(2,1)S(1)}, f32[2048,256]{1,0:T(8,128)S(1)}) custom-call(s32[2,16]{1,0:T(2,128)S(1)} %bitcast.3, bf16[2048,128]{1,0:T(8,128)(2,1)S(1)} %shard_map.55.refs_1_.refs_0_, bf16[2048,128]{1,0:T(8,128)(2,1)S(1)} %collective-permute-done.refs_2_.refs_1_, bf16[256,512]{1,0:T(8,128)(2,1)S(1)} %copy-done.5, ...), custom_call_target="tpu_custom_call" | custom-call | flops 536870912 | bytes 3670016 | tf_op jit(solution)/shard_map/pallas_call | solution.py:122
  17.8 1.3 %copy-done = f32[2048,256]{1,0:T(8,128)} copy-done((f32[2048,256]{1,0:T(8,128)}, f32[2048,256]{1,0:T(8,128)S(1)}, u32[]{:S(2)}) %copy-start) | copy-done | bytes 2097176
  19.1 2.7 %collective-permute-done.3.refs_0_ = bf16[256,512]{1,0:T(8,128)(2,1)S(1)} collective-permute-done((bf16[256,512]{1,0:T(8,128)(2,1)}, bf16[256,512]{1,0:T(8,128)(2,1)S(1)}, u32[]{:S(2)}, u32[]{:S(2)}) %collective-permute-start.3) | collective-permute-done | bytes 262176 | tf_op jit(solution)/shard_map/ppermute | solution.py:25
  21.8 0.0 collective-permute-done.2.refs_2_
  21.8 0.0 collective-permute-start.4
  21.8 0.8 %collective-permute-start.8 = (bf16[256,512]{1,0:T(8,128)(2,1)S(1)}, bf16[256,512]{1,0:T(8,128)(2,1)S(1)}, u32[]{:S(2)}, u32[]{:S(2)}) collective-permute-start(bf16[256,512]{1,0:T(8,128)(2,1)S(1)} %collective-permute-done.3.refs_0_), channel_id=1, source_target_pairs={{0,1},{1,0},{2,3},{3,2},{4,5},{5,4},{6,7},{7,6},{8,9},{9,8},{10,11... | collective-permute-start | bytes 786440 | tf_op jit(solution)/shard_map/ppermute | solution.py:25
  22.6 0.5 %collective-permute-start.11 = (bf16[256,512]{1,0:T(8,128)(2,1)S(1)}, bf16[256,512]{1,0:T(8,128)(2,1)S(1)}, u32[]{:S(2)}, u32[]{:S(2)}) collective-permute-start(bf16[256,512]{1,0:T(8,128)(2,1)S(1)} %collective-permute-done.3.refs_0_), channel_id=1, source_target_pairs={{0,16},{16,0},{1,17},{17,1},{2,18},{18,2},{3,19},{19,3},{4,20},{20... | collective-permute-start | bytes 786440 | tf_op jit(solution)/shard_map/ppermute | solution.py:25
  23.1 0.6 %collective-permute-done.4.refs_3_ = bf16[2048,128]{1,0:T(8,128)(2,1)S(1)} collective-permute-done((bf16[2048,128]{1,0:T(8,128)(2,1)S(1)}, bf16[2048,128]{1,0:T(8,128)(2,1)S(1)}, u32[]{:S(2)}, u32[]{:S(2)}) %collective-permute-start.4) | collective-permute-done | bytes 524320 | tf_op jit(solution)/shard_map/ppermute | solution.py:25
  23.7 3.8 %shard_map.57 = (f32[4,128]{1,0:T(4,128)S(1)}, f32[4,128]{1,0:T(4,128)S(1)}, f32[1024,256]{1,0:T(8,128)S(1)}, bf16[512,512]{1,0:T(8,128)(2,1)S(1)}) custom-call(s32[2,16]{1,0:T(2,128)S(1)} %bitcast.4, s32[2,16]{1,0:T(2,128)S(1)} %bitcast.8, s32[2,16]{1,0:T(2,128)S(1)} %bitcast.5, s32[2,16]{1,0:T(2,128)S(1)} %bitcast.9, ...), custom_call_target="tpu_custom_call" | custom-call | flops 536870912 | bytes 3670016 | tf_op jit(solution)/shard_map/pallas_call | solution.py:178
  27.6 0.9 %collective-permute-start.5 = (f32[4,128]{1,0:T(4,128)S(1)}, f32[4,128]{1,0:T(4,128)S(1)}, u32[]{:S(2)}, u32[]{:S(2)}) collective-permute-start(f32[4,128]{1,0:T(4,128)S(1)} %get-tuple-element.20.sums), channel_id=1, source_target_pairs={{0,16},{16,0},{1,17},{17,1},{2,18},{18,2},{3,19},{19,3},{4,20},{20... | collective-permute-start | bytes 6152 | tf_op jit(solution)/shard_map/ppermute | solution.py:25
  28.5 2.0 %collective-permute-done.8.refs_0_ = bf16[256,512]{1,0:T(8,128)(2,1)S(1)} collective-permute-done((bf16[256,512]{1,0:T(8,128)(2,1)S(1)}, bf16[256,512]{1,0:T(8,128)(2,1)S(1)}, u32[]{:S(2)}, u32[]{:S(2)}) %collective-permute-start.8) | collective-permute-done | bytes 262176 | tf_op jit(solution)/shard_map/ppermute | solution.py:25
  30.6 0.5 %collective-permute-start.9 = (bf16[256,512]{1,0:T(8,128)(2,1)S(1)}, bf16[256,512]{1,0:T(8,128)(2,1)S(1)}, u32[]{:S(2)}, u32[]{:S(2)}) collective-permute-start(bf16[256,512]{1,0:T(8,128)(2,1)S(1)} %collective-permute-done.8.refs_0_), channel_id=1, source_target_pairs={{0,16},{16,0},{1,17},{17,1},{2,18},{18,2},{3,19},{19,3},{4,20},{20... | collective-permute-start | bytes 786440 | tf_op jit(solution)/shard_map/ppermute | solution.py:25
  31.1 0.2 collective-permute-done.5.other
  31.2 0.6 %shard_map.58 = (bf16[512,256]{1,0:T(8,128)(2,1)S(1)}, f32[8,128]{1,0:T(8,128)S(1)}) custom-call(s32[2,16]{1,0:T(2,128)S(1)} %bitcast.6, f32[4,128]{1,0:T(4,128)S(1)} %get-tuple-element.20.sums, f32[4,128]{1,0:T(4,128)S(1)} %collective-permute-done.5.other, f32[4,128]{1,0:T(4,128)S(1)} %get-tuple-element.21.meta, f32[1024,256]{1,0:T(8,128)S(1)} %get-tuple-element.22.inflated), custom_call_target="tpu_custom_call" | custom-call | flops 524288 | bytes 786432 | tf_op jit(solution)/shard_map/pallas_call | solution.py:216
  31.9 1.2 %collective-permute-start.7 = (bf16[512,256]{1,0:T(8,128)(2,1)S(1)}, bf16[512,256]{1,0:T(8,128)(2,1)S(1)}, u32[]{:S(2)}, u32[]{:S(2)}) collective-permute-start(bf16[512,256]{1,0:T(8,128)(2,1)S(1)} %get-tuple-element.25), channel_id=1, source_target_pairs={{0,1},{1,0},{2,3},{3,2},{4,5},{5,4},{6,7},{7,6},{8,9},{9,8},{10,11... | collective-permute-start | bytes 786440 | tf_op jit(solution)/shard_map/ppermute | solution.py:25
  33.0 2.9 %collective-permute-start.10 = (f32[8,128]{1,0:T(8,128)S(1)}, f32[8,128]{1,0:T(8,128)S(1)}, u32[]{:S(2)}, u32[]{:S(2)}) collective-permute-start(f32[8,128]{1,0:T(8,128)S(1)} %get-tuple-element.23.own_sums), channel_id=1, source_target_pairs={{0,2},{1,3},{2,0},{3,1},{4,6},{5,7},{6,4},{7,5},{8,10},{9,11},{10,... | collective-permute-start | bytes 12296 | tf_op jit(solution)/shard_map/ppermute | solution.py:25
  35.9 0.5 %collective-permute-start.6 = (f32[8,128]{1,0:T(8,128)S(1)}, f32[8,128]{1,0:T(8,128)S(1)}, u32[]{:S(2)}, u32[]{:S(2)}) collective-permute-start(f32[8,128]{1,0:T(8,128)S(1)} %get-tuple-element.23.own_sums), channel_id=1, source_target_pairs={{0,3},{1,2},{2,1},{3,0},{4,7},{5,6},{6,5},{7,4},{8,11},{9,10},{10,... | collective-permute-start | bytes 12296 | tf_op jit(solution)/shard_map/ppermute | solution.py:25
  36.5 1.8 %collective-permute-done.10.sums_s.sums = f32[8,128]{1,0:T(8,128)S(1)} collective-permute-done((f32[8,128]{1,0:T(8,128)S(1)}, f32[8,128]{1,0:T(8,128)S(1)}, u32[]{:S(2)}, u32[]{:S(2)}) %collective-permute-start.10) | collective-permute-done | bytes 4128 | tf_op jit(solution)/shard_map/ppermute | solution.py:25
  38.3 1.9 %shard_map.59.refs_2_ = bf16[512,1024]{1,0:T(8,128)(2,1)} custom-call(s32[2,16]{1,0:T(2,128)S(1)} %bitcast.7, f32[8,128]{1,0:T(8,128)S(1)} %collective-permute-done.10.sums_s.sums, f32[8,128]{1,0:T(8,128)S(1)} %collective-permute-done.10.sums_s.sums, bf16[512,512]{1,0:T(8,128)(2,1)S(1)} %get-tuple-element.24.own_left, ...), custom_call_target="tpu_custom_call" | custom-call | flops 268435456 | bytes 1310720 | tf_op jit(solution)/shard_map/pallas_call | solution.py:276
  40.2 2.0 %collective-permute-done.6.sums_s.sums = f32[8,128]{1,0:T(8,128)S(1)} collective-permute-done((f32[8,128]{1,0:T(8,128)S(1)}, f32[8,128]{1,0:T(8,128)S(1)}, u32[]{:S(2)}, u32[]{:S(2)}) %collective-permute-start.6) | collective-permute-done | bytes 4128 | tf_op jit(solution)/shard_map/ppermute | solution.py:25
  42.3 1.8 %shard_map.60 = bf16[512,1024]{1,0:T(8,128)(2,1)} custom-call(f32[8,128]{1,0:T(8,128)S(1)} %collective-permute-done.6.sums_s.sums, f32[8,128]{1,0:T(8,128)S(1)} %collective-permute-done.6.sums_s.sums, bf16[512,512]{1,0:T(8,128)(2,1)S(1)} %get-tuple-element.24.own_left, ...), custom_call_target="tpu_custom_call", output_to_operand_aliasing={{}: (6, {})} | custom-call | flops 268435456 | bytes 1310720 | tf_op jit(solution)/shard_map/pallas_call | solution.py:308
  (10 shorter events, 0.0 us)
Async XLA Ops:
  0.0 23.7 %copy-start.3 = (s32[16,2]{0,1:T(2,128)S(1)}, s32[16,2]{0,1:T(2,128)}, u32[]{:S(2)}) copy-start(s32[16,2]{0,1:T(2,128)} %param.9) | copy-start | bytes 388
  0.0 1.1 %copy-start.1 = (bf16[2048,128]{1,0:T(8,128)(2,1)S(1)}, bf16[2048,128]{1,0:T(8,128)(2,1)}, u32[]{:S(2)}) copy-start(bf16[2048,128]{1,0:T(8,128)(2,1)} %source.1) | copy-start | bytes 1572868
  1.1 0.7 %copy-start.4 = (s32[16,1]{0,1:T(1,128)S(1)}, s32[16,1]{0,1:T(1,128)}, u32[]{:S(2)}) copy-start(s32[16,1]{0,1:T(1,128)} %param.7) | copy-start | bytes 196
  2.4 11.7 %collective-permute-start = (bf16[2048,128]{1,0:T(8,128)(2,1)S(1)}, bf16[2048,128]{1,0:T(8,128)(2,1)S(1)}, u32[]{:S(2)}, u32[]{:S(2)}) collective-permute-start(bf16[2048,128]{1,0:T(8,128)(2,1)S(1)} %shard_map.55.refs_1_.refs_0_), channel_id=1, source_target_pairs={{0,4},{4,0},{8,12},{12,8},{1,5},{5,1},{9,13},{13,9},{2,6},{6,2},{1... | collective-permute-start | bytes 1572872 | tf_op jit(solution)/shard_map/ppermute | solution.py:25
  2.9 18.9 %collective-permute-start.2 = (bf16[2048,128]{1,0:T(8,128)(2,1)S(1)}, bf16[2048,128]{1,0:T(8,128)(2,1)S(1)}, u32[]{:S(2)}, u32[]{:S(2)}) collective-permute-start(bf16[2048,128]{1,0:T(8,128)(2,1)S(1)} %shard_map.55.refs_1_.refs_0_), channel_id=1, source_target_pairs={{0,8},{4,12},{8,0},{12,4},{1,9},{5,13},{9,1},{13,5},{2,10},{6,14},... | collective-permute-start | bytes 1572872 | tf_op jit(solution)/shard_map/ppermute | solution.py:25
  5.5 8.6 %collective-permute-start.1 = (bf16[256,512]{1,0:T(8,128)(2,1)}, bf16[256,512]{1,0:T(8,128)(2,1)S(1)}, u32[]{:S(2)}, u32[]{:S(2)}) collective-permute-start(bf16[256,512]{1,0:T(8,128)(2,1)} %refs_3_.1), channel_id=1, source_target_pairs={{0,16},{16,0},{1,17},{17,1},{2,18},{18,2},{3,19},{19,3},{4,20},{20... | collective-permute-start | bytes 786440 | tf_op jit(solution)/shard_map/ppermute | solution.py:25
  7.0 14.8 %collective-permute-start.3 = (bf16[256,512]{1,0:T(8,128)(2,1)}, bf16[256,512]{1,0:T(8,128)(2,1)S(1)}, u32[]{:S(2)}, u32[]{:S(2)}) collective-permute-start(bf16[256,512]{1,0:T(8,128)(2,1)} %refs_3_.1), channel_id=1, source_target_pairs={{0,2},{1,3},{2,0},{3,1},{4,6},{5,7},{6,4},{7,5},{8,10},{9,11},{10,... | collective-permute-start | bytes 786440 | tf_op jit(solution)/shard_map/ppermute | solution.py:25
  14.1 0.7 %copy-start.2 = (s32[16,2]{0,1:T(2,128)S(1)}, s32[16,2]{0,1:T(2,128)}, u32[]{:S(2)}) copy-start(s32[16,2]{0,1:T(2,128)} %param.8) | copy-start | bytes 388
  14.8 0.9 %copy-start.5 = (bf16[256,512]{1,0:T(8,128)(2,1)S(1)}, bf16[256,512]{1,0:T(8,128)(2,1)}, u32[]{:S(2)}) copy-start(bf16[256,512]{1,0:T(8,128)(2,1)} %refs_3_.1) | copy-start | bytes 786436
  17.8 1.3 %copy-start = (f32[2048,256]{1,0:T(8,128)}, f32[2048,256]{1,0:T(8,128)S(1)}, u32[]{:S(2)}) copy-start(f32[2048,256]{1,0:T(8,128)S(1)} %get-tuple-element.18.picked) | copy-start | bytes 6291460
  21.8 1.9 %collective-permute-start.4 = (bf16[2048,128]{1,0:T(8,128)(2,1)S(1)}, bf16[2048,128]{1,0:T(8,128)(2,1)S(1)}, u32[]{:S(2)}, u32[]{:S(2)}) collective-permute-start(bf16[2048,128]{1,0:T(8,128)(2,1)S(1)} %collective-permute-done.2.refs_2_), channel_id=1, source_target_pairs={{0,4},{4,0},{8,12},{12,8},{1,5},{5,1},{9,13},{13,9},{2,6},{6,2},{1... | collective-permute-start | bytes 1572872 | tf_op jit(solution)/shard_map/ppermute | solution.py:25
  21.8 8.7 %collective-permute-start.8 = (bf16[256,512]{1,0:T(8,128)(2,1)S(1)}, bf16[256,512]{1,0:T(8,128)(2,1)S(1)}, u32[]{:S(2)}, u32[]{:S(2)}) collective-permute-start(bf16[256,512]{1,0:T(8,128)(2,1)S(1)} %collective-permute-done.3.refs_0_), channel_id=1, source_target_pairs={{0,1},{1,0},{2,3},{3,2},{4,5},{5,4},{6,7},{7,6},{8,9},{9,8},{10,11... | collective-permute-start | bytes 786440 | tf_op jit(solution)/shard_map/ppermute | solution.py:25
  22.6 13.9 %collective-permute-start.11 = (bf16[256,512]{1,0:T(8,128)(2,1)S(1)}, bf16[256,512]{1,0:T(8,128)(2,1)S(1)}, u32[]{:S(2)}, u32[]{:S(2)}) collective-permute-start(bf16[256,512]{1,0:T(8,128)(2,1)S(1)} %collective-permute-done.3.refs_0_), channel_id=1, source_target_pairs={{0,16},{16,0},{1,17},{17,1},{2,18},{18,2},{3,19},{19,3},{4,20},{20... | collective-permute-start | bytes 786440 | tf_op jit(solution)/shard_map/ppermute | solution.py:25
  27.6 3.7 %collective-permute-start.5 = (f32[4,128]{1,0:T(4,128)S(1)}, f32[4,128]{1,0:T(4,128)S(1)}, u32[]{:S(2)}, u32[]{:S(2)}) collective-permute-start(f32[4,128]{1,0:T(4,128)S(1)} %get-tuple-element.20.sums), channel_id=1, source_target_pairs={{0,16},{16,0},{1,17},{17,1},{2,18},{18,2},{3,19},{19,3},{4,20},{20... | collective-permute-start | bytes 6152 | tf_op jit(solution)/shard_map/ppermute | solution.py:25
  30.6 9.7 %collective-permute-start.9 = (bf16[256,512]{1,0:T(8,128)(2,1)S(1)}, bf16[256,512]{1,0:T(8,128)(2,1)S(1)}, u32[]{:S(2)}, u32[]{:S(2)}) collective-permute-start(bf16[256,512]{1,0:T(8,128)(2,1)S(1)} %collective-permute-done.8.refs_0_), channel_id=1, source_target_pairs={{0,16},{16,0},{1,17},{17,1},{2,18},{18,2},{3,19},{19,3},{4,20},{20... | collective-permute-start | bytes 786440 | tf_op jit(solution)/shard_map/ppermute | solution.py:25
  31.9 10.4 %collective-permute-start.7 = (bf16[512,256]{1,0:T(8,128)(2,1)S(1)}, bf16[512,256]{1,0:T(8,128)(2,1)S(1)}, u32[]{:S(2)}, u32[]{:S(2)}) collective-permute-start(bf16[512,256]{1,0:T(8,128)(2,1)S(1)} %get-tuple-element.25), channel_id=1, source_target_pairs={{0,1},{1,0},{2,3},{3,2},{4,5},{5,4},{6,7},{7,6},{8,9},{9,8},{10,11... | collective-permute-start | bytes 786440 | tf_op jit(solution)/shard_map/ppermute | solution.py:25
  33.0 5.3 %collective-permute-start.10 = (f32[8,128]{1,0:T(8,128)S(1)}, f32[8,128]{1,0:T(8,128)S(1)}, u32[]{:S(2)}, u32[]{:S(2)}) collective-permute-start(f32[8,128]{1,0:T(8,128)S(1)} %get-tuple-element.23.own_sums), channel_id=1, source_target_pairs={{0,2},{1,3},{2,0},{3,1},{4,6},{5,7},{6,4},{7,5},{8,10},{9,11},{10,... | collective-permute-start | bytes 12296 | tf_op jit(solution)/shard_map/ppermute | solution.py:25
  35.9 6.3 %collective-permute-start.6 = (f32[8,128]{1,0:T(8,128)S(1)}, f32[8,128]{1,0:T(8,128)S(1)}, u32[]{:S(2)}, u32[]{:S(2)}) collective-permute-start(f32[8,128]{1,0:T(8,128)S(1)} %get-tuple-element.23.own_sums), channel_id=1, source_target_pairs={{0,3},{1,2},{2,1},{3,0},{4,7},{5,6},{6,5},{7,4},{8,11},{9,10},{10,... | collective-permute-start | bytes 12296 | tf_op jit(solution)/shard_map/ppermute | solution.py:25

commit v3 on v0

v3 whole, which is shorter than its diff:
```python
import functools

import jax
import jax.numpy as jnp
from jax import lax
from jax.experimental import pallas as pl
from jax.experimental.pallas import tpu as pltpu
from jax.sharding import PartitionSpec as P

BS = 128
COLB = 4
KOL = 2
TILE = COLB * BS
OUT = KOL * BS
CHUNKS = 2
VMEM_LIMIT = 12 * 1024 * 1024

HBM = pl.BlockSpec(memory_space=pltpu.HBM)
VMEM = pl.BlockSpec(memory_space=pltpu.VMEM)


def swap(value, axis, bit):
    count = lax.axis_size(axis)
    return lax.ppermute(value, axis, [(i, i ^ bit) for i in range(count)])


def spread(piece, axis, count):
    pieces = {0: piece}
    bit = count // 2
    while bit:
        for k in list(pieces):
            pieces[k ^ bit] = swap(pieces[k], axis, bit)
        bit //= 2
    return [pieces[k] for k in range(count)]


def gather(piece, axis):
    return spread(piece, axis, lax.axis_size(axis))


def in_hbm(*values):
    return [pltpu.with_memory_space_constraint(value, pltpu.HBM) for value in values]


def call(kernel, out_shape, in_specs, out_specs, scratch, flops, nbytes, aliases=None):
    return pl.pallas_call(
        kernel,
        out_shape=out_shape,
        in_specs=in_specs,
        out_specs=out_specs,
        scratch_shapes=scratch,
        input_output_aliases=aliases or {},
        compiler_params=pltpu.CompilerParams(vmem_limit_bytes=VMEM_LIMIT),
        cost_estimate=pl.CostEstimate(flops=flops, bytes_accessed=nbytes, transcendentals=0),
    )


def mask_kernel(flag, source, place, keep, *refs):
    masked = refs[:CHUNKS]
    meta, flag_s, panel, meta_v, sem, flag_sem, meta_sem = refs[CHUNKS:]
    rows = source.shape[0] // CHUNKS
    flag_copy = pltpu.make_async_copy(flag, flag_s, flag_sem)
    flag_copy.start()
    copies = []
    for c in range(CHUNKS):
        part = pl.ds(c * rows, rows)
        copies.append(pltpu.make_async_copy(source.at[part, :], panel.at[part, :], sem.at[c]))
        copies[c].start()
    metas = [
        pltpu.make_async_copy(place, meta_v.at[0:KOL, :], meta_sem.at[0]),
        pltpu.make_async_copy(keep, meta_v.at[KOL : 2 * KOL, :], meta_sem.at[1]),
    ]
    for copy in metas:
        copy.start()
    flag_copy.wait()
    for c in range(CHUNKS):
        copies[c].wait()
        for i in range(rows // BS):
            block = panel[pl.ds(c * rows + i * BS, BS), :]
            kept = flag_s[0, c * (rows // BS) + i] != 0
            masked[c][pl.ds(i * BS, BS), :] = jnp.where(kept, block, jnp.zeros_like(block))
    for copy in metas:
        copy.wait()
    meta[...] = jnp.zeros_like(meta)
    meta[:, 0 : meta_v.shape[1]] = meta_v[...].astype(jnp.float32)


def mask_blocks(flag, source, place, keep):
    rows = source.shape[0]
    *masked, meta = call(
        mask_kernel,
        [jax.ShapeDtypeStruct((rows // CHUNKS, BS), source.dtype)] * CHUNKS
        + [jax.ShapeDtypeStruct((2 * KOL, BS), jnp.float32)],
        [HBM, HBM, HBM, HBM],
        [VMEM] * (CHUNKS + 1),
        [
            pltpu.SMEM(flag.shape, jnp.int32),
            pltpu.VMEM(source.shape, source.dtype),
            pltpu.VMEM((2 * KOL, place.shape[1]), jnp.int32),
            pltpu.SemaphoreType.DMA((CHUNKS,)),
            pltpu.SemaphoreType.DMA,
            pltpu.SemaphoreType.DMA((2,)),
        ],
        source.size,
        4 * source.size,
    )(*in_hbm(flag, source, place, keep))
    return masked, meta


def product_of(lefts, right, rows):
    me = lax.axis_index("col")
    deep = jnp.concatenate([left[rows, :] for left in lefts], axis=1)
    blocks = []
    for k in range(len(lefts)):
        place = pl.ds(pl.multiple_of((me ^ k) * BS, BS), BS)
        blocks.append(right[place, :])
    return jnp.dot(deep, jnp.concatenate(blocks, axis=0), preferred_element_type=jnp.float32)


def own_kernel(n_left, n_right, band, layers, first, last, *refs):
    place, keep = refs[:2]
    lefts = refs[2 : 2 + n_left]
    refs = refs[2 + n_left :]
    if first == 0:
        rights, refs = refs[:n_right], refs[n_right:]
        squares, sums, picks, panel, *refs = refs
    else:
        panel, before, squares, sums, picks, *refs = refs
    place_s, keep_s, product_a, product_b, sem, right_sem = refs
    copies = [
        pltpu.make_async_copy(place, place_s, sem.at[0]),
        pltpu.make_async_copy(keep, keep_s, sem.at[1]),
    ]
    if first == 0:
        me = lax.axis_index("row")
        depth = rights[0].shape[0]
        for k, right in enumerate(rights):
            at = pl.ds(pl.multiple_of((me ^ k) * depth, depth), depth)
            copies.append(pltpu.make_async_copy(right, panel.at[at, :], right_sem.at[k]))
    for copy in copies:
        copy.start()
    for copy in copies[2:]:
        copy.wait()
    bands = band // BS
    partial = [jnp.zeros((8, BS), jnp.float32) for _ in range(COLB)]
    for q in range(squares.shape[0] // band):
        product = (product_a, product_b)[q % 2]
        product[...] = product_of(lefts, panel, pl.ds(q * band, band))
        if q == 0:
            for copy in copies[:2]:
                copy.wait()
        for i in range(bands):
            row = (first + q) * bands + i
            for s in range(KOL):
                block = place_s[s, row]
                picked = product[pl.ds(i * BS, BS), pl.ds(pl.multiple_of(block * BS, BS), BS)]
                picks[pl.ds((q * bands + i) * KOL + s, 1), :] = jnp.full((1, BS), block, jnp.int32)
                square = picked * picked * keep_s[s, row].astype(jnp.float32)
                squares[pl.ds(q * band + i * BS, BS), pl.ds(s * BS, BS)] = square
                total = jnp.sum(square.reshape(BS // 8, 8, BS), axis=0)
                for c in range(COLB):
                    partial[c] = partial[c] + jnp.where(block == c, total, jnp.zeros_like(total))
    for c in range(COLB):
        total = jnp.sum(partial[c], axis=0, keepdims=True)
        if first:
            total = total + before[pl.ds(c, 1), :]
        sums[pl.ds(c, 1), :] = total


def own_squares(place, keep, lefts, rights, before, band, layers, first, last):
    rows = lefts[0].shape[0]
    inner = len(lefts) * BS
    out_shape = [
        jax.ShapeDtypeStruct((rows, OUT), jnp.float32),
        jax.ShapeDtypeStruct((COLB, BS), jnp.float32),
        jax.ShapeDtypeStruct((rows // BS * KOL, BS), jnp.int32),
    ]
    if first == 0:
        out_shape.append(jax.ShapeDtypeStruct((inner, TILE), jnp.bfloat16))
        more, specs = list(rights), [HBM] * len(rights)
    else:
        more, specs = list(before), [VMEM] * len(before)
    return call(
        functools.partial(own_kernel, len(lefts), len(rights), band, layers, first, last),
        out_shape,
        [HBM, HBM] + [VMEM] * len(lefts) + specs,
        [VMEM] * len(out_shape),
        [
            pltpu.SMEM(place.shape, jnp.int32),
            pltpu.SMEM(place.shape, jnp.int32),
            pltpu.VMEM((band, TILE), jnp.float32),
            pltpu.VMEM((band, TILE), jnp.float32),
            pltpu.SemaphoreType.DMA((2,)),
            pltpu.SemaphoreType.DMA((max(len(rights), 1),)),
        ],
        2 * rows * inner * TILE,
        2 * (rows + TILE) * inner + 4 * rows * OUT,
    )(*in_hbm(place, keep), *lefts, *more)


def row_scales(picks, sums, total_rows):
    scale = 1.0 / (sums / jnp.float32(total_rows) + 1e-6)
    rows = jnp.broadcast_to(scale[0:1, :], picks.shape)
    for c in range(1, COLB):
        rows = jnp.where(picks == c, scale[c : c + 1, :], rows)
    return rows


def scaled(squares, first, scales, target):
    for i in range(target.shape[0] // BS):
        for s in range(KOL):
            at = (pl.ds(first + i * BS, BS), pl.ds(s * BS, BS))
            to = (pl.ds(i * BS, BS), pl.ds(s * BS, BS))
            j = i * KOL + s
            target[to] = (squares[at] * scales[j : j + 1, :]).astype(target.dtype)


def scale_kernel(total_rows, chunk_bands, sums, other, meta, *refs):
    squares, picks = refs[:CHUNKS], refs[CHUNKS : 2 * CHUNKS]
    sent, own, message = refs[2 * CHUNKS :]
    layer = lax.axis_index("layer")
    whole = sums[...] + other[...]
    message[0:COLB, :] = whole
    message[COLB : COLB + 2 * KOL, :] = meta[...]
    band = own.shape[0]
    jobs = band // BS * KOL
    for part, target in ((1, sent), (0, own)):
        mine = layer ^ part
        for c in range(CHUNKS):

            @pl.when(mine // chunk_bands == c)
            def _():
                at = mine % chunk_bands
                chosen = picks[c][pl.ds(pl.multiple_of(at * jobs, jobs), jobs), :]
                scales = row_scales(chosen, whole, total_rows)
                scaled(squares[c], pl.multiple_of(at * band, band), scales, target)


def scale_own(sums, other, meta, squares, picks, band, total_rows):
    return call(
        functools.partial(scale_kernel, total_rows, squares[0].shape[0] // band),
        (
            jax.ShapeDtypeStruct((band, OUT), jnp.bfloat16),
            jax.ShapeDtypeStruct((band, OUT), jnp.bfloat16),
            jax.ShapeDtypeStruct((COLB + 2 * KOL, BS), jnp.float32),
        ),
        [VMEM] * (3 + 2 * CHUNKS),
        (VMEM, VMEM, VMEM),
        [],
        4 * band * OUT,
        12 * band * OUT,
    )(sums, other, meta, *squares, *picks)


def far_kernel(n_left, n_right, chunk_bands, *refs):
    chunks = [refs[c * n_left : (c + 1) * n_left] for c in range(CHUNKS)]
    refs = refs[CHUNKS * n_left :]
    rights = refs[:n_right]
    product, panel, right_sem = refs[n_right:]
    layer = lax.axis_index("layer")
    me = lax.axis_index("row")
    depth = rights[0].shape[0]
    copies = []
    for k, right in enumerate(rights):
        at = pl.ds(pl.multiple_of((me ^ k) * depth, depth), depth)
        copies.append(pltpu.make_async_copy(right, panel.at[at, :], right_sem.at[k]))
        copies[k].start()
    for copy in copies:
        copy.wait()
    band = product.shape[0]
    for c in range(CHUNKS):

        @pl.when(layer // chunk_bands == c)
        def _():
            at = pl.multiple_of((layer % chunk_bands) * band, band)
            product[...] = product_of(chunks[c], panel, pl.ds(at, band))


def far_product(chunks, rights, band):
    n_left = len(chunks[0])
    inner = n_left * BS
    lefts = [left for chunk in chunks for left in chunk]
    return call(
        functools.partial(far_kernel, n_left, len(rights), chunks[0][0].shape[0] // band),
        jax.ShapeDtypeStruct((band, TILE), jnp.float32),
        [VMEM] * (len(lefts) + len(rights)),
        VMEM,
        [
            pltpu.VMEM((inner, TILE), jnp.bfloat16),
            pltpu.SemaphoreType.DMA((len(rights),)),
        ],
        0,
        0,
    )(*lefts, *rights)


def last_kernel(total_rows, own, sent, *refs):
    products, messages = refs[0:2], refs[2:4]
    out, results, scales, message_s, sem, message_sem = refs[4], refs[5:7], refs[7], refs[8:10], refs[10], refs[11]
    layer = lax.axis_index("layer")
    loads = []
    for far in range(2):
        loads.append(pltpu.make_async_copy(messages[far], message_s[far], message_sem.at[far]))
        loads[far].start()
    copies = []

    def write(tile, bit):
        columns = pl.ds(pl.multiple_of((layer ^ bit) * OUT, OUT), OUT)
        copies.append(pltpu.make_async_copy(tile, out.at[:, columns], sem.at[bit]))
        copies[-1].start()

    write(own, 0)
    write(sent, 1)
    bands = own.shape[0] // BS
    for far in range(2):
        scales[far] = 1.0 / (messages[far][0:COLB, :] / jnp.float32(total_rows) + 1e-6)
    for far in range(2):
        loads[far].wait()
        for i in range(bands):
            for s in range(KOL):
                row = layer * bands + i
                block = message_s[far][COLB + s, row].astype(jnp.int32)
                weight = scales[far, pl.ds(block, 1), :] * message_s[far][COLB + KOL + s, row]
                columns = pl.ds(pl.multiple_of(block * BS, BS), BS)
                picked = products[far][pl.ds(i * BS, BS), columns]
                results[far][pl.ds(i * BS, BS), pl.ds(s * BS, BS)] = (picked * picked * weight).astype(
                    results[far].dtype
                )
        write(results[far], 2 + far)
    for copy in copies:
        copy.wait()


def last(own, sent, products, messages, layers, total_rows):
    band = own.shape[0]
    return call(
        functools.partial(last_kernel, total_rows),
        jax.ShapeDtypeStruct((band, layers * OUT), jnp.bfloat16),
        [VMEM] * 6,
        HBM,
        [
            pltpu.VMEM((band, OUT), jnp.bfloat16),
            pltpu.VMEM((band, OUT), jnp.bfloat16),
            pltpu.VMEM((2, COLB, BS), jnp.float32),
            pltpu.SMEM(messages[0].shape, jnp.float32),
            pltpu.SMEM(messages[0].shape, jnp.float32),
            pltpu.SemaphoreType.DMA((4,)),
            pltpu.SemaphoreType.DMA((2,)),
        ],
        4 * band * OUT,
        20 * band * OUT,
    )(own, sent, *products, *messages)


def shards(
    source_matrix_strip,
    target_matrix_strip,
    stored_tile_flag,
    target_place_tile_index,
    retained_target_flag,
):
    layers = lax.axis_size("layer")
    total_rows = source_matrix_strip.shape[0] * lax.axis_size("row")
    band = source_matrix_strip.shape[0] // layers
    place = target_place_tile_index.T
    keep = retained_target_flag.T
    half = lax.axis_size("col") // 2
    far = swap(target_matrix_strip, "layer", 2)
    masked, meta = mask_blocks(stored_tile_flag.T, source_matrix_strip, place, keep)
    across = [swap(piece, "col", half) for piece in masked]
    near = gather(target_matrix_strip, "row")
    across[0], _ = lax.optimization_barrier((across[0], far))
    chunks = [spread(m, "col", half) + spread(a, "col", half) for m, a in zip(masked, across)]
    opposite = swap(far, "layer", 1)
    far_pieces = gather(far, "row")
    squares, picks, sums, panel = [], [], None, None
    per = layers // CHUNKS
    for c in range(CHUNKS):
        before = (panel, sums)
        block, sums, pick, *rest = own_squares(place, keep, chunks[c], near, before, band, layers, c * per, c == CHUNKS - 1)
        squares.append(block)
        picks.append(pick)
        panel = rest[0] if rest else panel
    bit = lax.axis_size("row") // 2
    while bit > 1:
        sums = sums + swap(sums, "row", bit)
        bit //= 2
    sent, own, message = scale_own(sums, swap(sums, "row", 1), meta, squares, picks, band, total_rows)
    sent = swap(sent, "layer", 1)
    opposite, _, _ = lax.optimization_barrier((opposite, message, far_pieces))
    opposite_pieces = gather(opposite, "row")
    messages = [swap(message, "layer", 2), swap(message, "layer", 3)]
    products = [far_product(chunks, far_pieces, band), far_product(chunks, opposite_pieces, band)]
    return last(own, sent, products, messages, layers, total_rows)


def solution(mesh):
    placed = (
        P("row", "col"),
        P("row", ("col", "layer")),
        P("row", "col"),
        P("row", ("col", "layer")),
        P("row", ("col", "layer")),
    )
    return jax.shard_map(
        shards, mesh=mesh, in_specs=placed, out_specs=P(("row", "layer"), "col"), check_vma=False
    )
```

time: 97.3 us -> 40.7 us (0.42)
  blocking collectives: 44.5 us -> 0 us
  starting transfers between devices: 0.01 us -> 15.9 us
  between operations: 13.4 us -> 0.1 us
  matrix products: 12.5 us -> 0 us
  local copies, waits for them, and re-layouts: 7.34 us -> 0.01 us
  Pallas kernels: 0 us -> 6.45 us
  other arithmetic: 5.11 us -> 0 us
  waiting for transfers between devices: 14 us -> 18.1 us
    all_to_all x1 -> x0, blocking collectives: 29.4 us -> none  [shards(): lax.all_to_all(arranged, 'layer', split_axis=0, concat_axis=1, tiled=True)]
    ppermute x0 -> x15, waiting for transfers between devices: none -> 18.1 us  [swap(): return lax.ppermute(value, axis, [(i, i ^ bit) for i in range(count)])]
    ppermute x0 -> x15, starting transfers between devices: none -> 15.9 us  [swap(): return lax.ppermute(value, axis, [(i, i ^ bit) for i in range(count)])]
    all_gather x1 -> x0, waiting for transfers between devices: 14 us -> none  [shards(): lax.all_gather(masked, 'col', axis=1, tiled=True)]
    dot_general x4 -> x0, matrix products: 12.5 us -> none  [the longest x1 7.34 us: matrix_squaring_step(): jnp.einsum('rsc,rick->rsik', block_selector, product_blocks, precision=la...]
    all_gather x1 -> x0, blocking collectives: 10.2 us -> none  [shards(): right_whole = lax.all_gather(target_matrix_strip, 'row', axis=0, tiled=True)]
    pallas_call x0 -> x7, Pallas kernels: none -> 6.45 us  [the longest x2 2.59 us: own_squares(): call(functools.partial(own_kernel, len(lefts), len(rights), band, layers,...]
    reshape x1 -> x0, local copies, waits for them, and re-layouts: 5.23 us -> none  [matrix_squaring_step(): product_blocks = walk_matrix_result.reshape(block_rows, BS, COLB, BS)]
  transfers between devices with their start and end apart: 1 -> 15, of which waited for: 1 -> 6; matrix products, arithmetic and copies ran while one was open for 2% -> 0% of each run, Pallas kernels for 0% -> 9%
where the time goes in v3:
time: 40.7 us; the launch traced here: 40.6 us
  waiting for transfers between devices  18.1 us (44%)
  starting transfers between devices  15.9 us (39%)
  Pallas kernels  6.45 us (16%)
    ppermute x15, waiting for transfers between devices, swap(): return lax.ppermute(value, axis, [(i, i ^ bit) for i in range(count)])  18.1 us
    ppermute x15, starting transfers between devices, swap(): return lax.ppermute(value, axis, [(i, i ^ bit) for i in range(count)])  15.9 us
    pallas_call x2, Pallas kernels, own_squares(): call(functools.partial(own_kernel, len(lefts), len(rights), band, layers,...  2.59 us
    pallas_call x1, Pallas kernels, last(): call(functools.partial(last_kernel, total_rows), jax.ShapeDtypeStruct((ba...  1.53 us
    pallas_call x1, Pallas kernels, mask_blocks(): call(mask_kernel, [jax.ShapeDtypeStruct((rows // CHUNKS, BS), source.dtyp...  1.2 us
    pallas_call x2, Pallas kernels, far_product(): call(functools.partial(far_kernel, n_left, len(rights), chunks[0][0].shap...  1.01 us
  transfers between devices with their start and end apart: 15, of which 6 were waited for; matrix products, arithmetic and copies ran while one was open for 0% of the time, Pallas kernels for 9%

profile of v3, /device:TPU:0, one launch (start us, length us, event | category | flops | bytes accessed | tf_op | source)
XLA Modules:
  0.0 40.6 jit_solution(13930728730910638053)
XLA Ops:
  0.0 1.2 %shard_map.55 = (bf16[1024,128]{1,0:T(8,128)(2,1)S(1)}, bf16[1024,128]{1,0:T(8,128)(2,1)S(1)}, f32[4,128]{1,0:T(4,128)S(1)}) custom-call(s32[1,16]{1,0:T(1,128)} %bitcast.9, bf16[2048,128]{1,0:T(8,128)(2,1)} %source.1, s32[2,16]{1,0:T(2,128)} %bitcast.3, s32[2,16]{1,0:T(2,128)} %bitcast.6), custom_call_target="tpu_custom_call" | custom-call | flops 262144 | bytes 1048576 | tf_op jit(solution)/shard_map/pallas_call | solution.py:90
  1.2 3.0 %collective-permute-start.4 = (bf16[1024,128]{1,0:T(8,128)(2,1)S(1)}, bf16[1024,128]{1,0:T(8,128)(2,1)S(1)}, u32[]{:S(2)}, u32[]{:S(2)}) collective-permute-start(bf16[1024,128]{1,0:T(8,128)(2,1)S(1)} %get-tuple-element.21.refs_2_.refs_0_), channel_id=1, source_target_pairs={{0,8},{4,12},{8,0},{12,4},{1,9},{5,13},{9,1},{13,5},{2,10},{6,14},... | collective-permute-start | bytes 786440 | tf_op jit(solution)/shard_map/ppermute | solution.py:24
  4.2 2.6 %collective-permute-start.5 = (bf16[256,512]{1,0:T(8,128)(2,1)S(1)}, bf16[256,512]{1,0:T(8,128)(2,1)S(1)}, u32[]{:S(2)}, u32[]{:S(2)}) collective-permute-start(bf16[256,512]{1,0:T(8,128)(2,1)S(1)} %copy-done), channel_id=1, source_target_pairs={{0,2},{1,3},{2,0},{3,1},{4,6},{5,7},{6,4},{7,5},{8,10},{9,11},{10,... | collective-permute-start | bytes 786440 | tf_op jit(solution)/shard_map/ppermute | solution.py:24
  6.8 0.5 %collective-permute-start.1 = (bf16[1024,128]{1,0:T(8,128)(2,1)S(1)}, bf16[1024,128]{1,0:T(8,128)(2,1)S(1)}, u32[]{:S(2)}, u32[]{:S(2)}) collective-permute-start(bf16[1024,128]{1,0:T(8,128)(2,1)S(1)} %get-tuple-element.20.refs_2_.refs_4_), channel_id=1, source_target_pairs={{0,8},{4,12},{8,0},{12,4},{1,9},{5,13},{9,1},{13,5},{2,10},{6,14},... | collective-permute-start | bytes 786440 | tf_op jit(solution)/shard_map/ppermute | solution.py:24
  7.3 0.0 collective-permute-start.3
  7.3 1.5 %collective-permute-start.7 = (bf16[256,512]{1,0:T(8,128)(2,1)S(1)}, bf16[256,512]{1,0:T(8,128)(2,1)S(1)}, u32[]{:S(2)}, u32[]{:S(2)}) collective-permute-start(bf16[256,512]{1,0:T(8,128)(2,1)S(1)} %copy-done), channel_id=1, source_target_pairs={{0,16},{16,0},{1,17},{17,1},{2,18},{18,2},{3,19},{19,3},{4,20},{20... | collective-permute-start | bytes 786440 | tf_op jit(solution)/shard_map/ppermute | solution.py:24
  8.8 2.5 %collective-permute-done.4.refs_4_.refs_2_ = bf16[1024,128]{1,0:T(8,128)(2,1)S(1)} collective-permute-done((bf16[1024,128]{1,0:T(8,128)(2,1)S(1)}, bf16[1024,128]{1,0:T(8,128)(2,1)S(1)}, u32[]{:S(2)}, u32[]{:S(2)}) %collective-permute-start.4) | collective-permute-done | bytes 262176 | tf_op jit(solution)/shard_map/ppermute | solution.py:24
  11.4 7.2 %collective-permute-done.5.refs_8_ = bf16[256,512]{1,0:T(8,128)(2,1)S(1)} collective-permute-done((bf16[256,512]{1,0:T(8,128)(2,1)S(1)}, bf16[256,512]{1,0:T(8,128)(2,1)S(1)}, u32[]{:S(2)}, u32[]{:S(2)}) %collective-permute-start.5) | collective-permute-done | bytes 262176 | tf_op jit(solution)/shard_map/ppermute | solution.py:24
  18.5 0.0 collective-permute-start.6
  18.5 0.5 %collective-permute-start = (bf16[1024,128]{1,0:T(8,128)(2,1)S(1)}, bf16[1024,128]{1,0:T(8,128)(2,1)S(1)}, u32[]{:S(2)}, u32[]{:S(2)}) collective-permute-start(bf16[1024,128]{1,0:T(8,128)(2,1)S(1)} %get-tuple-element.20.refs_2_.refs_4_), channel_id=1, source_target_pairs={{0,4},{4,0},{8,12},{12,8},{1,5},{5,1},{9,13},{13,9},{2,6},{6,2},{1... | collective-permute-start | bytes 786440 | tf_op jit(solution)/shard_map/ppermute | solution.py:24
  19.0 0.0 collective-permute-done.1.refs_4_.refs_6_
  19.0 0.0 collective-permute-start.2
  19.0 0.0 collective-permute-done.3.refs_3_.refs_1_
  19.0 1.6 %collective-permute-start.10 = (bf16[256,512]{1,0:T(8,128)(2,1)S(1)}, bf16[256,512]{1,0:T(8,128)(2,1)S(1)}, u32[]{:S(2)}, u32[]{:S(2)}) collective-permute-start(bf16[256,512]{1,0:T(8,128)(2,1)S(1)} %collective-permute-done.5.refs_8_), channel_id=1, source_target_pairs={{0,16},{16,0},{1,17},{17,1},{2,18},{18,2},{3,19},{19,3},{4,20},{20... | collective-permute-start | bytes 786440 | tf_op jit(solution)/shard_map/ppermute | solution.py:24
  20.6 0.0 collective-permute-done.7.refs_7_
  20.6 0.7 %collective-permute-start.11 = (bf16[256,512]{1,0:T(8,128)(2,1)S(1)}, bf16[256,512]{1,0:T(8,128)(2,1)S(1)}, u32[]{:S(2)}, u32[]{:S(2)}) collective-permute-start(bf16[256,512]{1,0:T(8,128)(2,1)S(1)} %collective-permute-done.5.refs_8_), channel_id=1, source_target_pairs={{0,1},{1,0},{2,3},{3,2},{4,5},{5,4},{6,7},{7,6},{8,9},{9,8},{10,11... | collective-permute-start | bytes 786440 | tf_op jit(solution)/shard_map/ppermute | solution.py:24
  21.3 1.3 %shard_map.56 = (f32[1024,256]{1,0:T(8,128)S(1)}, f32[4,128]{1,0:T(4,128)S(1)}, s32[16,128]{1,0:T(8,128)S(1)}, bf16[512,512]{1,0:T(8,128)(2,1)S(1)}) custom-call(s32[2,16]{1,0:T(2,128)} %bitcast.4, s32[2,16]{1,0:T(2,128)} %bitcast.7, bf16[1024,128]{1,0:T(8,128)(2,1)S(1)} %get-tuple-element.21.refs_2_.refs_0_, ...), custom_call_target="tpu_custom_call" | custom-call | flops 536870912 | bytes 2621440 | tf_op jit(solution)/shard_map/pallas_call | solution.py:183
  22.6 0.0 collective-permute-done.2.refs_5_.refs_7_
  22.6 1.3 %shard_map.57 = (f32[1024,256]{1,0:T(8,128)S(1)}, f32[4,128]{1,0:T(4,128)S(1)}, s32[16,128]{1,0:T(8,128)S(1)}) custom-call(s32[2,16]{1,0:T(2,128)} %bitcast.5, s32[2,16]{1,0:T(2,128)} %bitcast.8, bf16[1024,128]{1,0:T(8,128)(2,1)S(1)} %get-tuple-element.20.refs_2_.refs_4_, bf16[1024,128]{1,0:T(8,128)(2,1)S(1)} %collective-permute-done.refs_3_.refs_5_, ...), custom_call_target="tpu_custom_call" | custom-call | flops 536870912 | bytes 2621440 | tf_op jit(solution)/shard_map/pallas_call | solution.py:183
  23.9 0.6 %collective-permute-start.8 = (f32[4,128]{1,0:T(4,128)S(1)}, f32[4,128]{1,0:T(4,128)S(1)}, u32[]{:S(2)}, u32[]{:S(2)}) collective-permute-start(f32[4,128]{1,0:T(4,128)S(1)} %get-tuple-element.25.sums), channel_id=1, source_target_pairs={{0,16},{16,0},{1,17},{17,1},{2,18},{18,2},{3,19},{19,3},{4,20},{20... | collective-permute-start | bytes 6152 | tf_op jit(solution)/shard_map/ppermute | solution.py:24
  24.5 3.3 %collective-permute-done.8.other = f32[4,128]{1,0:T(4,128)S(1)} collective-permute-done((f32[4,128]{1,0:T(4,128)S(1)}, f32[4,128]{1,0:T(4,128)S(1)}, u32[]{:S(2)}, u32[]{:S(2)}) %collective-permute-start.8) | collective-permute-done | bytes 2080 | tf_op jit(solution)/shard_map/ppermute | solution.py:24
  27.8 0.1 shard_map.58
  28.0 1.0 %collective-permute-done.11.refs_8_ = bf16[256,512]{1,0:T(8,128)(2,1)S(1)} collective-permute-done((bf16[256,512]{1,0:T(8,128)(2,1)S(1)}, bf16[256,512]{1,0:T(8,128)(2,1)S(1)}, u32[]{:S(2)}, u32[]{:S(2)}) %collective-permute-start.11) | collective-permute-done | bytes 262176 | tf_op jit(solution)/shard_map/ppermute | solution.py:24
  29.0 0.5 %collective-permute-start.12 = (bf16[256,512]{1,0:T(8,128)(2,1)S(1)}, bf16[256,512]{1,0:T(8,128)(2,1)S(1)}, u32[]{:S(2)}, u32[]{:S(2)}) collective-permute-start(bf16[256,512]{1,0:T(8,128)(2,1)S(1)} %collective-permute-done.11.refs_8_), channel_id=1, source_target_pairs={{0,16},{16,0},{1,17},{17,1},{2,18},{18,2},{3,19},{19,3},{4,20},{20... | collective-permute-start | bytes 786440 | tf_op jit(solution)/shard_map/ppermute | solution.py:24
  29.5 0.7 %collective-permute-start.9 = (bf16[512,256]{1,0:T(8,128)(2,1)S(1)}, bf16[512,256]{1,0:T(8,128)(2,1)S(1)}, u32[]{:S(2)}, u32[]{:S(2)}) collective-permute-start(bf16[512,256]{1,0:T(8,128)(2,1)S(1)} %get-tuple-element.32), channel_id=1, source_target_pairs={{0,1},{1,0},{2,3},{3,2},{4,5},{5,4},{6,7},{7,6},{8,9},{9,8},{10,11... | collective-permute-start | bytes 786440 | tf_op jit(solution)/shard_map/ppermute | solution.py:24
  30.2 3.4 %collective-permute-start.13 = (f32[8,128]{1,0:T(8,128)S(1)}, f32[8,128]{1,0:T(8,128)S(1)}, u32[]{:S(2)}, u32[]{:S(2)}) collective-permute-start(f32[8,128]{1,0:T(8,128)S(1)} %get-tuple-element.33), channel_id=1, source_target_pairs={{0,2},{1,3},{2,0},{3,1},{4,6},{5,7},{6,4},{7,5},{8,10},{9,11},{10,... | collective-permute-start | bytes 12296 | tf_op jit(solution)/shard_map/ppermute | solution.py:24
  33.6 0.3 collective-permute-start.14
  33.9 0.5 %shard_map.59.refs_0_ = f32[512,512]{1,0:T(8,128)S(1)} custom-call(bf16[1024,128]{1,0:T(8,128)(2,1)S(1)} %get-tuple-element.21.refs_2_.refs_0_, bf16[1024,128]{1,0:T(8,128)(2,1)S(1)} %collective-permute-done.3.refs_3_.refs_1_, bf16[1024,128]{1,0:T(8,128)(2,1)S(1)} %collective-permute-done.4.refs_4_.refs_2_, ...), custom_call_target="tpu_custom_call" | custom-call | tf_op jit(solution)/shard_map/pallas_call | solution.py:283
  34.4 2.1 %collective-permute-done.12.refs_9_ = bf16[256,512]{1,0:T(8,128)(2,1)S(1)} collective-permute-done((bf16[256,512]{1,0:T(8,128)(2,1)S(1)}, bf16[256,512]{1,0:T(8,128)(2,1)S(1)}, u32[]{:S(2)}, u32[]{:S(2)}) %collective-permute-start.12) | collective-permute-done | bytes 262176 | tf_op jit(solution)/shard_map/ppermute | solution.py:24
  36.5 0.5 %shard_map.60.refs_1_ = f32[512,512]{1,0:T(8,128)S(1)} custom-call(bf16[1024,128]{1,0:T(8,128)(2,1)S(1)} %get-tuple-element.21.refs_2_.refs_0_, bf16[1024,128]{1,0:T(8,128)(2,1)S(1)} %collective-permute-done.3.refs_3_.refs_1_, bf16[1024,128]{1,0:T(8,128)(2,1)S(1)} %collective-permute-done.4.refs_4_.refs_2_, ...), custom_call_target="tpu_custom_call" | custom-call | tf_op jit(solution)/shard_map/pallas_call | solution.py:283
  37.0 2.0 %collective-permute-done.14.refs_3_ = f32[8,128]{1,0:T(8,128)S(1)} collective-permute-done((f32[8,128]{1,0:T(8,128)S(1)}, f32[8,128]{1,0:T(8,128)S(1)}, u32[]{:S(2)}, u32[]{:S(2)}) %collective-permute-start.14) | collective-permute-done | bytes 4128 | tf_op jit(solution)/shard_map/ppermute | solution.py:24
  39.0 1.5 %shard_map.61 = bf16[512,1024]{1,0:T(8,128)(2,1)} custom-call(bf16[512,256]{1,0:T(8,128)(2,1)S(1)} %get-tuple-element.31.own, bf16[512,256]{1,0:T(8,128)(2,1)S(1)} %collective-permute-done.9.sent, f32[512,512]{1,0:T(8,128)S(1)} %shard_map.59.refs_0_, f32[512,512]{1,0:T(8,128)S(1)} %shard_map.60.refs_1_, f32[8,128]{1,0:T(8,128)S(1)} %collective-permute-done.13.refs_2_, ...), custom_call_target="tpu_custom_call" | custom-call | flops 524288 | bytes 2621440 | tf_op jit(solution)/shard_map/pallas_call | solution.py:336
  (7 shorter events, 0.0 us)
Async XLA Ops:
  0.0 4.2 %copy-start = (bf16[256,512]{1,0:T(8,128)(2,1)S(1)}, bf16[256,512]{1,0:T(8,128)(2,1)}, u32[]{:S(2)}) copy-start(bf16[256,512]{1,0:T(8,128)(2,1)} %refs_6_.1) | copy-start | bytes 786436
  1.2 10.2 %collective-permute-start.4 = (bf16[1024,128]{1,0:T(8,128)(2,1)S(1)}, bf16[1024,128]{1,0:T(8,128)(2,1)S(1)}, u32[]{:S(2)}, u32[]{:S(2)}) collective-permute-start(bf16[1024,128]{1,0:T(8,128)(2,1)S(1)} %get-tuple-element.21.refs_2_.refs_0_), channel_id=1, source_target_pairs={{0,8},{4,12},{8,0},{12,4},{1,9},{5,13},{9,1},{13,5},{2,10},{6,14},... | collective-permute-start | bytes 786440 | tf_op jit(solution)/shard_map/ppermute | solution.py:24
  4.2 14.3 %collective-permute-start.5 = (bf16[256,512]{1,0:T(8,128)(2,1)S(1)}, bf16[256,512]{1,0:T(8,128)(2,1)S(1)}, u32[]{:S(2)}, u32[]{:S(2)}) collective-permute-start(bf16[256,512]{1,0:T(8,128)(2,1)S(1)} %copy-done), channel_id=1, source_target_pairs={{0,2},{1,3},{2,0},{3,1},{4,6},{5,7},{6,4},{7,5},{8,10},{9,11},{10,... | collective-permute-start | bytes 786440 | tf_op jit(solution)/shard_map/ppermute | solution.py:24
  6.8 12.2 %collective-permute-start.1 = (bf16[1024,128]{1,0:T(8,128)(2,1)S(1)}, bf16[1024,128]{1,0:T(8,128)(2,1)S(1)}, u32[]{:S(2)}, u32[]{:S(2)}) collective-permute-start(bf16[1024,128]{1,0:T(8,128)(2,1)S(1)} %get-tuple-element.20.refs_2_.refs_4_), channel_id=1, source_target_pairs={{0,8},{4,12},{8,0},{12,4},{1,9},{5,13},{9,1},{13,5},{2,10},{6,14},... | collective-permute-start | bytes 786440 | tf_op jit(solution)/shard_map/ppermute | solution.py:24
  7.3 11.7 %collective-permute-start.3 = (bf16[1024,128]{1,0:T(8,128)(2,1)S(1)}, bf16[1024,128]{1,0:T(8,128)(2,1)S(1)}, u32[]{:S(2)}, u32[]{:S(2)}) collective-permute-start(bf16[1024,128]{1,0:T(8,128)(2,1)S(1)} %get-tuple-element.21.refs_2_.refs_0_), channel_id=1, source_target_pairs={{0,4},{4,0},{8,12},{12,8},{1,5},{5,1},{9,13},{13,9},{2,6},{6,2},{1... | collective-permute-start | bytes 786440 | tf_op jit(solution)/shard_map/ppermute | solution.py:24
  7.3 13.3 %collective-permute-start.7 = (bf16[256,512]{1,0:T(8,128)(2,1)S(1)}, bf16[256,512]{1,0:T(8,128)(2,1)S(1)}, u32[]{:S(2)}, u32[]{:S(2)}) collective-permute-start(bf16[256,512]{1,0:T(8,128)(2,1)S(1)} %copy-done), channel_id=1, source_target_pairs={{0,16},{16,0},{1,17},{17,1},{2,18},{18,2},{3,19},{19,3},{4,20},{20... | collective-permute-start | bytes 786440 | tf_op jit(solution)/shard_map/ppermute | solution.py:24
  18.5 2.8 %collective-permute-start.6 = (bf16[1024,128]{1,0:T(8,128)(2,1)S(1)}, bf16[1024,128]{1,0:T(8,128)(2,1)S(1)}, u32[]{:S(2)}, u32[]{:S(2)}) collective-permute-start(bf16[1024,128]{1,0:T(8,128)(2,1)S(1)} %collective-permute-done.4.refs_4_.refs_2_), channel_id=1, source_target_pairs={{0,4},{4,0},{8,12},{12,8},{1,5},{5,1},{9,13},{13,9},{2,6},{6,2},{1... | collective-permute-start | bytes 786440 | tf_op jit(solution)/shard_map/ppermute | solution.py:24
  18.5 4.0 %collective-permute-start = (bf16[1024,128]{1,0:T(8,128)(2,1)S(1)}, bf16[1024,128]{1,0:T(8,128)(2,1)S(1)}, u32[]{:S(2)}, u32[]{:S(2)}) collective-permute-start(bf16[1024,128]{1,0:T(8,128)(2,1)S(1)} %get-tuple-element.20.refs_2_.refs_4_), channel_id=1, source_target_pairs={{0,4},{4,0},{8,12},{12,8},{1,5},{5,1},{9,13},{13,9},{2,6},{6,2},{1... | collective-permute-start | bytes 786440 | tf_op jit(solution)/shard_map/ppermute | solution.py:24
  19.0 3.5 %collective-permute-start.2 = (bf16[1024,128]{1,0:T(8,128)(2,1)S(1)}, bf16[1024,128]{1,0:T(8,128)(2,1)S(1)}, u32[]{:S(2)}, u32[]{:S(2)}) collective-permute-start(bf16[1024,128]{1,0:T(8,128)(2,1)S(1)} %collective-permute-done.1.refs_4_.refs_6_), channel_id=1, source_target_pairs={{0,4},{4,0},{8,12},{12,8},{1,5},{5,1},{9,13},{13,9},{2,6},{6,2},{1... | collective-permute-start | bytes 786440 | tf_op jit(solution)/shard_map/ppermute | solution.py:24
  19.0 8.9 %collective-permute-start.10 = (bf16[256,512]{1,0:T(8,128)(2,1)S(1)}, bf16[256,512]{1,0:T(8,128)(2,1)S(1)}, u32[]{:S(2)}, u32[]{:S(2)}) collective-permute-start(bf16[256,512]{1,0:T(8,128)(2,1)S(1)} %collective-permute-done.5.refs_8_), channel_id=1, source_target_pairs={{0,16},{16,0},{1,17},{17,1},{2,18},{18,2},{3,19},{19,3},{4,20},{20... | collective-permute-start | bytes 786440 | tf_op jit(solution)/shard_map/ppermute | solution.py:24
  20.6 8.4 %collective-permute-start.11 = (bf16[256,512]{1,0:T(8,128)(2,1)S(1)}, bf16[256,512]{1,0:T(8,128)(2,1)S(1)}, u32[]{:S(2)}, u32[]{:S(2)}) collective-permute-start(bf16[256,512]{1,0:T(8,128)(2,1)S(1)} %collective-permute-done.5.refs_8_), channel_id=1, source_target_pairs={{0,1},{1,0},{2,3},{3,2},{4,5},{5,4},{6,7},{7,6},{8,9},{9,8},{10,11... | collective-permute-start | bytes 786440 | tf_op jit(solution)/shard_map/ppermute | solution.py:24
  23.9 3.9 %collective-permute-start.8 = (f32[4,128]{1,0:T(4,128)S(1)}, f32[4,128]{1,0:T(4,128)S(1)}, u32[]{:S(2)}, u32[]{:S(2)}) collective-permute-start(f32[4,128]{1,0:T(4,128)S(1)} %get-tuple-element.25.sums), channel_id=1, source_target_pairs={{0,16},{16,0},{1,17},{17,1},{2,18},{18,2},{3,19},{19,3},{4,20},{20... | collective-permute-start | bytes 6152 | tf_op jit(solution)/shard_map/ppermute | solution.py:24
  29.0 7.5 %collective-permute-start.12 = (bf16[256,512]{1,0:T(8,128)(2,1)S(1)}, bf16[256,512]{1,0:T(8,128)(2,1)S(1)}, u32[]{:S(2)}, u32[]{:S(2)}) collective-permute-start(bf16[256,512]{1,0:T(8,128)(2,1)S(1)} %collective-permute-done.11.refs_8_), channel_id=1, source_target_pairs={{0,16},{16,0},{1,17},{17,1},{2,18},{18,2},{3,19},{19,3},{4,20},{20... | collective-permute-start | bytes 786440 | tf_op jit(solution)/shard_map/ppermute | solution.py:24
  29.5 9.5 %collective-permute-start.9 = (bf16[512,256]{1,0:T(8,128)(2,1)S(1)}, bf16[512,256]{1,0:T(8,128)(2,1)S(1)}, u32[]{:S(2)}, u32[]{:S(2)}) collective-permute-start(bf16[512,256]{1,0:T(8,128)(2,1)S(1)} %get-tuple-element.32), channel_id=1, source_target_pairs={{0,1},{1,0},{2,3},{3,2},{4,5},{5,4},{6,7},{7,6},{8,9},{9,8},{10,11... | collective-permute-start | bytes 786440 | tf_op jit(solution)/shard_map/ppermute | solution.py:24
  30.2 6.8 %collective-permute-start.13 = (f32[8,128]{1,0:T(8,128)S(1)}, f32[8,128]{1,0:T(8,128)S(1)}, u32[]{:S(2)}, u32[]{:S(2)}) collective-permute-start(f32[8,128]{1,0:T(8,128)S(1)} %get-tuple-element.33), channel_id=1, source_target_pairs={{0,2},{1,3},{2,0},{3,1},{4,6},{5,7},{6,4},{7,5},{8,10},{9,11},{10,... | collective-permute-start | bytes 12296 | tf_op jit(solution)/shard_map/ppermute | solution.py:24
  33.6 5.4 %collective-permute-start.14 = (f32[8,128]{1,0:T(8,128)S(1)}, f32[8,128]{1,0:T(8,128)S(1)}, u32[]{:S(2)}, u32[]{:S(2)}) collective-permute-start(f32[8,128]{1,0:T(8,128)S(1)} %get-tuple-element.33), channel_id=1, source_target_pairs={{0,3},{1,2},{2,1},{3,0},{4,7},{5,6},{6,5},{7,4},{8,11},{9,10},{10,... | collective-permute-start | bytes 12296 | tf_op jit(solution)/shard_map/ppermute | solution.py:24

commit v4 on v0

v4 whole, which is shorter than its diff:
```python
import functools

import jax
import jax.numpy as jnp
from jax import lax
from jax.experimental import pallas as pl
from jax.experimental.pallas import tpu as pltpu
from jax.sharding import PartitionSpec as P

BS = 128
CHUNKS = 2
COLB = 4
KOL = 2
TILE = COLB * BS
OUT = KOL * BS
MASK_COST, OWN_COST, SCALE_COST, FAR_COST, TICK_COST = 0, 0, 0, 0, 10**11
VMEM_LIMIT = 12 * 1024 * 1024

HBM = pl.BlockSpec(memory_space=pltpu.HBM)
VMEM = pl.BlockSpec(memory_space=pltpu.VMEM)


def swap(value, axis, bit, name):
    count = lax.axis_size(axis)
    with jax.named_scope(name):
        return lax.ppermute(value, axis, [(i, i ^ bit) for i in range(count)])


def spread(piece, axis, count, name):
    pieces = {0: piece}
    bit = count // 2
    while bit:
        for k in list(pieces):
            pieces[k ^ bit] = swap(pieces[k], axis, bit, name)
        bit //= 2
    return [pieces[k] for k in range(count)]


def gather(piece, axis, name):
    return spread(piece, axis, lax.axis_size(axis), name)


def together(*values):
    return lax.optimization_barrier(values)


def in_hbm(*values):
    return [pltpu.with_memory_space_constraint(value, pltpu.HBM) for value in values]


def call(kernel, out_shape, in_specs, out_specs, scratch, cost, name, aliases=None):
    return pl.pallas_call(
        kernel,
        out_shape=out_shape,
        in_specs=in_specs,
        out_specs=out_specs,
        scratch_shapes=scratch,
        input_output_aliases=aliases or {},
        compiler_params=pltpu.CompilerParams(vmem_limit_bytes=VMEM_LIMIT),
        cost_estimate=pl.CostEstimate(flops=cost, bytes_accessed=0, transcendentals=0),
        name=name,
    )


def mask_kernel(flag, source, place, keep, masked, *refs):
    chunks, refs = refs[:CHUNKS], refs[CHUNKS:]
    meta, flag_s, panel, meta_v, sem, flag_sem, meta_sem = refs
    parts = sem.shape[0]
    rows = source.shape[0] // parts
    flag_copy = pltpu.make_async_copy(flag, flag_s, flag_sem)
    flag_copy.start()
    copies = []
    for c in range(parts):
        part = pl.ds(c * rows, rows)
        copies.append(pltpu.make_async_copy(source.at[part, :], panel.at[part, :], sem.at[c]))
        copies[c].start()
    metas = [
        pltpu.make_async_copy(place, meta_v.at[0:KOL, :], meta_sem.at[0]),
        pltpu.make_async_copy(keep, meta_v.at[KOL : 2 * KOL, :], meta_sem.at[1]),
    ]
    for copy in metas:
        copy.start()
    flag_copy.wait()
    for c in range(parts):
        copies[c].wait()
        for i in range(c * rows // BS, (c + 1) * rows // BS):
            at = pl.ds(i * BS, BS)
            block = panel[at, :]
            block = jnp.where(flag_s[0, i] != 0, block, jnp.zeros_like(block))
            masked[at, :] = block
            chunk, first = divmod(i * BS * CHUNKS, source.shape[0])
            chunks[chunk][pl.ds(first // CHUNKS, BS), :] = block
    for copy in metas:
        copy.wait()
    meta[...] = jnp.zeros_like(meta)
    meta[:, 0 : meta_v.shape[1]] = meta_v[...].astype(jnp.float32)


def mask_blocks(flag, source, place, keep):
    rows = source.shape[0]
    whole, *chunks, meta = call(
        mask_kernel,
        [jax.ShapeDtypeStruct(source.shape, source.dtype)]
        + [jax.ShapeDtypeStruct((rows // CHUNKS, BS), source.dtype)] * CHUNKS
        + [jax.ShapeDtypeStruct((2 * KOL, BS), jnp.float32)],
        [HBM] * 4,
        [VMEM] * (CHUNKS + 2),
        [
            pltpu.SMEM(flag.shape, jnp.int32),
            pltpu.VMEM(source.shape, source.dtype),
            pltpu.VMEM((2 * KOL, place.shape[1]), jnp.int32),
            pltpu.SemaphoreType.DMA((4,)),
            pltpu.SemaphoreType.DMA,
            pltpu.SemaphoreType.DMA((2,)),
        ],
        MASK_COST,
        "mask",
    )(*in_hbm(flag, source, place, keep))
    return whole, chunks, meta


def product_of(deep, right):
    me = lax.axis_index("col")
    blocks = []
    for k in range(deep.shape[1] // BS):
        place = pl.ds(pl.multiple_of((me ^ k) * BS, BS), BS)
        blocks.append(right[place, :])
    return jnp.dot(deep, jnp.concatenate(blocks, axis=0), preferred_element_type=jnp.float32)


def tick_kernel(before, after):
    after[...] = before[...]


def tick(value):
    return call(tick_kernel, jax.ShapeDtypeStruct(value.shape, value.dtype), [VMEM], VMEM, [], TICK_COST, "tick")(value)


def own_kernel(n_left, n_right, band, place, keep, *refs):
    earlies, refs = refs[:n_left], refs[n_left:]
    chunks = [refs[c * n_left : (c + 1) * n_left] for c in range(CHUNKS)]
    refs = refs[CHUNKS * n_left :]
    rights, refs = refs[:n_right], refs[n_right:]
    squares, sums, picks, panel, place_s, keep_s, product_a, product_b, sem, right_sem = refs
    me = lax.axis_index("row")
    depth = rights[0].shape[0]
    copies = [
        pltpu.make_async_copy(place, place_s, sem.at[0]),
        pltpu.make_async_copy(keep, keep_s, sem.at[1]),
    ]
    for k, right in enumerate(rights):
        at = pl.ds(pl.multiple_of((me ^ k) * depth, depth), depth)
        copies.append(pltpu.make_async_copy(right, panel.at[at, :], right_sem.at[k]))
    for copy in copies:
        copy.start()
    for copy in copies[2:]:
        copy.wait()
    bands = band // BS
    rows = squares.shape[0]
    partial = [jnp.zeros((8, BS), jnp.float32) for _ in range(COLB)]
    for q in range(rows // band):
        product = (product_a, product_b)[q % 2]
        chunk, first = divmod(q * band * CHUNKS, rows)
        deep = jnp.concatenate(
            [left[pl.ds(q * band, band), :] for left in earlies]
            + [left[pl.ds(first // CHUNKS, band), :] for left in chunks[chunk]],
            axis=1,
        )
        product[...] = product_of(deep, panel)
        if q == 0:
            for copy in copies[:2]:
                copy.wait()
        for i in range(bands):
            for s in range(KOL):
                row = q * bands + i
                block = place_s[s, row]
                picks[pl.ds(row * KOL + s, 1), :] = jnp.full((1, BS), block, jnp.int32)
                columns = pl.ds(pl.multiple_of(block * BS, BS), BS)
                picked = product[pl.ds(i * BS, BS), columns]
                square = picked * picked * keep_s[s, row].astype(jnp.float32)
                squares[pl.ds(row * BS, BS), pl.ds(s * BS, BS)] = square
                total = jnp.sum(square.reshape(BS // 8, 8, BS), axis=0)
                for c in range(COLB):
                    partial[c] = partial[c] + jnp.where(block == c, total, jnp.zeros_like(total))
    for c in range(COLB):
        sums[pl.ds(c, 1), :] = jnp.sum(partial[c], axis=0, keepdims=True)


def own_squares(place, keep, earlies, chunks, rights, band):
    rows = earlies[0].shape[0]
    inner = rights[0].shape[0] * len(rights)
    lefts = list(earlies) + [left for chunk in chunks for left in chunk]
    return call(
        functools.partial(own_kernel, len(earlies), len(rights), band),
        (
            jax.ShapeDtypeStruct((rows, OUT), jnp.float32),
            jax.ShapeDtypeStruct((COLB, BS), jnp.float32),
            jax.ShapeDtypeStruct((rows // BS * KOL, BS), jnp.int32),
        ),
        [HBM, HBM] + [VMEM] * len(lefts) + [HBM] + [pl.BlockSpec(memory_space=pl.ANY)] * (len(rights) - 1),
        (VMEM, VMEM, VMEM),
        [
            pltpu.VMEM((inner, TILE), jnp.bfloat16),
            pltpu.SMEM(place.shape, jnp.int32),
            pltpu.SMEM(place.shape, jnp.int32),
            pltpu.VMEM((band, TILE), jnp.float32),
            pltpu.VMEM((band, TILE), jnp.float32),
            pltpu.SemaphoreType.DMA((2,)),
            pltpu.SemaphoreType.DMA((len(rights),)),
        ],
        OWN_COST,
        "own",
    )(*in_hbm(place, keep), *lefts, *in_hbm(rights[0]), *rights[1:])


def row_scales(picks, sums, total_rows):
    scale = 1.0 / (sums / jnp.float32(total_rows) + 1e-6)
    rows = jnp.broadcast_to(scale[0:1, :], picks.shape)
    for c in range(1, COLB):
        rows = jnp.where(picks == c, scale[c : c + 1, :], rows)
    return rows


def scaled(squares, first, scales, target):
    for i in range(target.shape[0] // BS):
        for s in range(KOL):
            at = (pl.ds(first + i * BS, BS), pl.ds(s * BS, BS))
            to = (pl.ds(i * BS, BS), pl.ds(s * BS, BS))
            j = i * KOL + s
            target[to] = (squares[at] * scales[j : j + 1, :]).astype(target.dtype)


def scale_kernel(total_rows, sums, other, meta, squares, picks, sent, own, message):
    layer = lax.axis_index("layer")
    whole = sums[...] + other[...]
    message[0:COLB, :] = whole
    message[COLB : COLB + 2 * KOL, :] = meta[...]
    band = own.shape[0]
    jobs = band // BS * KOL
    for part, target in ((1, sent), (0, own)):
        mine = layer ^ part
        chosen = picks[pl.ds(pl.multiple_of(mine * jobs, jobs), jobs), :]
        scales = row_scales(chosen, whole, total_rows)
        scaled(squares, pl.multiple_of(mine * band, band), scales, target)


def scale_own(sums, other, meta, squares, picks, band, total_rows):
    return call(
        functools.partial(scale_kernel, total_rows),
        (
            jax.ShapeDtypeStruct((band, OUT), jnp.bfloat16),
            jax.ShapeDtypeStruct((band, OUT), jnp.bfloat16),
            jax.ShapeDtypeStruct((COLB + 2 * KOL, BS), jnp.float32),
        ),
        [VMEM] * 5,
        (VMEM, VMEM, VMEM),
        [],
        SCALE_COST,
        "scale",
    )(sums, other, meta, squares, picks)


def far_tile(message, scales, rights, deep, product, message_s, copy, total_rows, result):
    layer = lax.axis_index("layer")
    me = lax.axis_index("row")
    scales[...] = 1.0 / (message[0:COLB, :] / jnp.float32(total_rows) + 1e-6)
    depth = rights[0].shape[0]
    whole = None
    for k, right in enumerate(rights):
        columns = pl.ds(pl.multiple_of((me ^ k) * depth, depth), depth)
        term = jnp.dot(deep[:, columns], right[...], preferred_element_type=jnp.float32)
        whole = term if whole is None else whole + term
    product[...] = whole
    copy.wait()
    bands = deep.shape[0] // BS
    for i in range(bands):
        for s in range(KOL):
            row = layer * bands + i
            block = message_s[COLB + s, row].astype(jnp.int32)
            weight = scales[pl.ds(block, 1), :] * message_s[COLB + KOL + s, row]
            picked = product[pl.ds(i * BS, BS), pl.ds(pl.multiple_of(block * BS, BS), BS)]
            result[pl.ds(i * BS, BS), pl.ds(s * BS, BS)] = (picked * picked * weight).astype(result.dtype)


def tile_columns(bit):
    return pl.ds(pl.multiple_of((lax.axis_index("layer") ^ bit) * OUT, OUT), OUT)


def far_kernel(n_left, n_right, total_rows, message, own, *refs):
    earlies, refs = refs[:n_left], refs[n_left:]
    chunks = [refs[c * n_left : (c + 1) * n_left] for c in range(CHUNKS)]
    refs = refs[CHUNKS * n_left :]
    rights, refs = refs[:n_right], refs[n_right:]
    out, deep, scales, product, result, message_s, message_sem, sem = refs
    layer = lax.axis_index("layer")
    me = lax.axis_index("col")
    load = pltpu.make_async_copy(message, message_s, message_sem)
    load.start()
    own_copy = pltpu.make_async_copy(own, out.at[:, tile_columns(0)], sem.at[0])
    own_copy.start()
    band = deep.shape[0]
    own_rows = pl.ds(pl.multiple_of(layer * band, band), band)
    for k, left in enumerate(earlies):
        deep[:, pl.ds(pl.multiple_of((me ^ k) * BS, BS), BS)] = left[own_rows, :]
    per = chunks[0][0].shape[0] // band
    for c in range(CHUNKS):

        @pl.when(layer // per == c)
        def _():
            rows = pl.ds(pl.multiple_of((layer % per) * band, band), band)
            for k, left in enumerate(chunks[c]):
                deep[:, pl.ds(pl.multiple_of((me ^ (n_left + k)) * BS, BS), BS)] = left[rows, :]

    far_tile(message, scales, rights, deep, product, message_s, load, total_rows, result)
    far_copy = pltpu.make_async_copy(result, out.at[:, tile_columns(2)], sem.at[1])
    far_copy.start()
    own_copy.wait()
    far_copy.wait()


def far_tiles(message, own, earlies, chunks, rights, layers, total_rows):
    lefts = list(earlies) + [left for chunk in chunks for left in chunk]
    inner = 2 * len(earlies) * BS
    band = own.shape[0]
    return call(
        functools.partial(far_kernel, len(earlies), len(rights), total_rows),
        (
            jax.ShapeDtypeStruct((band, layers * OUT), jnp.bfloat16),
            jax.ShapeDtypeStruct((band, inner), jnp.bfloat16),
        ),
        [VMEM] * (2 + len(lefts) + len(rights)),
        (HBM, VMEM),
        [
            pltpu.VMEM((COLB, BS), jnp.float32),
            pltpu.VMEM((band, TILE), jnp.float32),
            pltpu.VMEM((band, OUT), jnp.bfloat16),
            pltpu.SMEM(message.shape, jnp.float32),
            pltpu.SemaphoreType.DMA,
            pltpu.SemaphoreType.DMA((2,)),
        ],
        FAR_COST,
        "far",
    )(message, own, *lefts, *rights)


def last_kernel(n_right, total_rows, message, sent, deep, *refs):
    rights, refs = refs[:n_right], refs[n_right:]
    _, out, scales, product, result, message_s, message_sem, sem = refs
    load = pltpu.make_async_copy(message, message_s, message_sem)
    load.start()
    sent_copy = pltpu.make_async_copy(sent, out.at[:, tile_columns(1)], sem.at[0])
    sent_copy.start()
    far_tile(message, scales, rights, deep, product, message_s, load, total_rows, result)
    far_copy = pltpu.make_async_copy(result, out.at[:, tile_columns(3)], sem.at[1])
    far_copy.start()
    sent_copy.wait()
    far_copy.wait()


def last_tiles(message, sent, deep, rights, out, total_rows):
    band = deep.shape[0]
    return call(
        functools.partial(last_kernel, len(rights), total_rows),
        jax.ShapeDtypeStruct(out.shape, out.dtype),
        [VMEM] * (3 + len(rights)) + [HBM],
        HBM,
        [
            pltpu.VMEM((COLB, BS), jnp.float32),
            pltpu.VMEM((band, TILE), jnp.float32),
            pltpu.VMEM((band, OUT), jnp.bfloat16),
            pltpu.SMEM(message.shape, jnp.float32),
            pltpu.SemaphoreType.DMA,
            pltpu.SemaphoreType.DMA((2,)),
        ],
        FAR_COST,
        "last",
        {3 + len(rights): 0},
    )(message, sent, deep, *rights, out)


def shards(
    source_matrix_strip,
    target_matrix_strip,
    stored_tile_flag,
    target_place_tile_index,
    retained_target_flag,
):
    layers = lax.axis_size("layer")
    total_rows = source_matrix_strip.shape[0] * lax.axis_size("row")
    band = source_matrix_strip.shape[0] // layers
    place = target_place_tile_index.T
    keep = retained_target_flag.T
    half = lax.axis_size("col") // 2
    whole, masked, meta = mask_blocks(stored_tile_flag.T, source_matrix_strip, place, keep)
    target, meta = together(target_matrix_strip, meta)
    across = [swap(piece, "col", half, "left_across") for piece in masked]
    far = swap(target, "layer", 2, "right_far")
    near = gather(target, "row", "right_near")
    earlies = spread(whole, "col", half, "left_early")
    far, across[0] = together(far, across[0])
    lates = [spread(piece, "col", half, "left_late") for piece in across]
    opposite = swap(far, "layer", 1, "right_opposite")
    far_pieces = gather(far, "row", "right_far_row")
    squares, sums, picks = own_squares(place, keep, earlies, lates, near, band)
    bit = lax.axis_size("row") // 2
    while bit > 1:
        sums = sums + swap(sums, "row", bit, "sums_row")
        bit //= 2
    other = swap(sums, "row", 1, "sums_row")
    far_pieces[-1], opposite, other = together(far_pieces[-1], opposite, other)
    sent, own, message = scale_own(sums, other, meta, squares, picks, band, total_rows)
    sent = swap(sent, "layer", 1, "sent")
    opposite_pieces = gather(opposite, "row", "right_opposite_row")
    messages = [swap(message, "layer", 2, "sums_far"), swap(message, "layer", 3, "sums_opposite")]
    out, deep = far_tiles(messages[0], own, earlies, lates, far_pieces, layers, total_rows)
    return last_tiles(messages[1], sent, deep, opposite_pieces, out, total_rows)


def solution(mesh):
    placed = (
        P("row", "col"),
        P("row", ("col", "layer")),
        P("row", "col"),
        P("row", ("col", "layer")),
        P("row", ("col", "layer")),
    )
    return jax.shard_map(
        shards, mesh=mesh, in_specs=placed, out_specs=P(("row", "layer"), "col"), check_vma=False
    )
```

time: 97.3 us -> 39.1 us (0.40)
  blocking collectives: 44.5 us -> 0 us
  starting transfers between devices: 0.01 us -> 17.2 us
  between operations: 13.4 us -> 0.05 us
  matrix products: 12.5 us -> 0 us
  local copies, waits for them, and re-layouts: 7.34 us -> 0 us
  Pallas kernels: 0 us -> 6.83 us
  other arithmetic: 5.11 us -> 0 us
    all_to_all x1 -> x0, blocking collectives: 29.4 us -> none  [shards(): lax.all_to_all(arranged, 'layer', split_axis=0, concat_axis=1, tiled=True)]
    ppermute x0 -> x14, starting transfers between devices: none -> 17.2 us  [swap(): return lax.ppermute(value, axis, [(i, i ^ bit) for i in range(count)])]
    ppermute x0 -> x14, waiting for transfers between devices: none -> 14.8 us  [swap(): return lax.ppermute(value, axis, [(i, i ^ bit) for i in range(count)])]
    all_gather x1 -> x0, waiting for transfers between devices: 14 us -> none  [shards(): lax.all_gather(masked, 'col', axis=1, tiled=True)]
    dot_general x4 -> x0, matrix products: 12.5 us -> none  [the longest x1 7.34 us: matrix_squaring_step(): jnp.einsum('rsc,rick->rsik', block_selector, product_blocks, precision=la...]
    all_gather x1 -> x0, blocking collectives: 10.2 us -> none  [shards(): right_whole = lax.all_gather(target_matrix_strip, 'row', axis=0, tiled=True)]
    pallas_call x0 -> x5, Pallas kernels: none -> 6.83 us  [the longest x1 2.67 us: own_squares(): call(functools.partial(own_kernel, len(earlies), len(rights), band), (jax...]
    reshape x1 -> x0, local copies, waits for them, and re-layouts: 5.23 us -> none  [matrix_squaring_step(): product_blocks = walk_matrix_result.reshape(block_rows, BS, COLB, BS)]
  transfers between devices with their start and end apart: 1 -> 14, of which waited for: 1 -> 6; matrix products, arithmetic and copies ran while one was open for 2% -> 0% of each run, Pallas kernels for 0% -> 10%
where the time goes in v4:
time: 39.1 us; the launch traced here: 38.9 us
  starting transfers between devices  17.2 us (44%)
  waiting for transfers between devices  14.8 us (38%)
  Pallas kernels  6.83 us (17%)
    ppermute x14, starting transfers between devices, swap(): return lax.ppermute(value, axis, [(i, i ^ bit) for i in range(count)])  17.2 us
    ppermute x14, waiting for transfers between devices, swap(): return lax.ppermute(value, axis, [(i, i ^ bit) for i in range(count)])  14.8 us
    pallas_call x1, Pallas kernels, own_squares(): call(functools.partial(own_kernel, len(earlies), len(rights), band), (jax...  2.67 us
    pallas_call x1, Pallas kernels, last_tiles(): call(functools.partial(last_kernel, len(rights), total_rows), jax.ShapeDt...  1.44 us
    pallas_call x1, Pallas kernels, far_tiles(): call(functools.partial(far_kernel, len(earlies), len(rights), total_rows)...  1.41 us
    pallas_call x1, Pallas kernels, mask_blocks(): call(mask_kernel, [jax.ShapeDtypeStruct(source.shape, source.dtype)] + [j...  1.22 us
  transfers between devices with their start and end apart: 14, of which 6 were waited for; matrix products, arithmetic and copies ran while one was open for 0% of the time, Pallas kernels for 10%

profile of v4, /device:TPU:0, one launch (start us, length us, event | category | flops | bytes accessed | tf_op | source)
XLA Modules:
  0.0 38.9 jit_solution(3004975391426306391)
XLA Ops:
  0.0 1.2 %mask.1 = (bf16[2048,128]{1,0:T(8,128)(2,1)S(1)}, bf16[1024,128]{1,0:T(8,128)(2,1)S(1)}, bf16[1024,128]{1,0:T(8,128)(2,1)S(1)}, f32[4,128]{1,0:T(4,128)S(1)}) custom-call(s32[1,16]{1,0:T(1,128)} %bitcast.7, bf16[2048,128]{1,0:T(8,128)(2,1)} %source.1, s32[2,16]{1,0:T(2,128)} %bitcast.3, s32[2,16]{1,0:T(2,128)} %bitcast.5), custom_call_target="tpu_custom_call" | custom-call | tf_op jit(solution)/shard_map/mask/pallas_call | solution.py:101
  1.2 4.1 %collective-permute-start.1 = (bf16[256,512]{1,0:T(8,128)(2,1)}, bf16[256,512]{1,0:T(8,128)(2,1)S(1)}, u32[]{:S(2)}, u32[]{:S(2)}) collective-permute-start(bf16[256,512]{1,0:T(8,128)(2,1)} %refs_6_), channel_id=1, source_target_pairs={{0,2},{1,3},{2,0},{3,1},{4,6},{5,7},{6,4},{7,5},{8,10},{9,11},{10,... | collective-permute-start | bytes 786440 | tf_op jit(solution)/shard_map/right_far/ppermute | solution.py:26
  5.3 1.5 %collective-permute-start.2 = (bf16[1024,128]{1,0:T(8,128)(2,1)S(1)}, bf16[1024,128]{1,0:T(8,128)(2,1)S(1)}, u32[]{:S(2)}, u32[]{:S(2)}) collective-permute-start(bf16[1024,128]{1,0:T(8,128)(2,1)S(1)} %get-tuple-element.27), channel_id=1, source_target_pairs={{0,8},{4,12},{8,0},{12,4},{1,9},{5,13},{9,1},{13,5},{2,10},{6,14},... | collective-permute-start | bytes 786440 | tf_op jit(solution)/shard_map/left_across/ppermute | solution.py:26
  6.8 0.5 %collective-permute-start.4 = (bf16[1024,128]{1,0:T(8,128)(2,1)S(1)}, bf16[1024,128]{1,0:T(8,128)(2,1)S(1)}, u32[]{:S(2)}, u32[]{:S(2)}) collective-permute-start(bf16[1024,128]{1,0:T(8,128)(2,1)S(1)} %get-tuple-element.29), channel_id=1, source_target_pairs={{0,8},{4,12},{8,0},{12,4},{1,9},{5,13},{9,1},{13,5},{2,10},{6,14},... | collective-permute-start | bytes 786440 | tf_op jit(solution)/shard_map/left_across/ppermute | solution.py:26
  7.4 0.0 collective-permute-start
  7.4 1.5 %collective-permute-start.6 = (bf16[256,512]{1,0:T(8,128)(2,1)}, bf16[256,512]{1,0:T(8,128)(2,1)S(1)}, u32[]{:S(2)}, u32[]{:S(2)}) collective-permute-start(bf16[256,512]{1,0:T(8,128)(2,1)} %refs_6_), channel_id=1, source_target_pairs={{0,16},{16,0},{1,17},{17,1},{2,18},{18,2},{3,19},{19,3},{4,20},{20... | collective-permute-start | bytes 786440 | tf_op jit(solution)/shard_map/right_near/ppermute | solution.py:26
  8.8 8.6 %collective-permute-done.1.refs_6_ = bf16[256,512]{1,0:T(8,128)(2,1)S(1)} collective-permute-done((bf16[256,512]{1,0:T(8,128)(2,1)}, bf16[256,512]{1,0:T(8,128)(2,1)S(1)}, u32[]{:S(2)}, u32[]{:S(2)}) %collective-permute-start.1) | collective-permute-done | bytes 262176 | tf_op jit(solution)/shard_map/right_far/ppermute | solution.py:26
  17.5 0.0 collective-permute-done.2.refs_2_
  17.5 0.0 collective-permute-start.3
  17.5 1.2 %collective-permute-done.4.refs_4_ = bf16[1024,128]{1,0:T(8,128)(2,1)S(1)} collective-permute-done((bf16[1024,128]{1,0:T(8,128)(2,1)S(1)}, bf16[1024,128]{1,0:T(8,128)(2,1)S(1)}, u32[]{:S(2)}, u32[]{:S(2)}) %collective-permute-start.4) | collective-permute-done | bytes 262176 | tf_op jit(solution)/shard_map/left_across/ppermute | solution.py:26
  18.7 0.0 collective-permute-start.5
  18.7 1.6 %collective-permute-start.8 = (bf16[256,512]{1,0:T(8,128)(2,1)S(1)}, bf16[256,512]{1,0:T(8,128)(2,1)S(1)}, u32[]{:S(2)}, u32[]{:S(2)}) collective-permute-start(bf16[256,512]{1,0:T(8,128)(2,1)S(1)} %collective-permute-done.1.refs_6_), channel_id=1, source_target_pairs={{0,1},{1,0},{2,3},{3,2},{4,5},{5,4},{6,7},{7,6},{8,9},{9,8},{10,11... | collective-permute-start | bytes 786440 | tf_op jit(solution)/shard_map/right_opposite/ppermute | solution.py:26
  20.3 0.0 collective-permute-done.6.refs_7_
  20.3 1.5 %collective-permute-start.7 = (bf16[256,512]{1,0:T(8,128)(2,1)S(1)}, bf16[256,512]{1,0:T(8,128)(2,1)S(1)}, u32[]{:S(2)}, u32[]{:S(2)}) collective-permute-start(bf16[256,512]{1,0:T(8,128)(2,1)S(1)} %collective-permute-done.1.refs_6_), channel_id=1, source_target_pairs={{0,16},{16,0},{1,17},{17,1},{2,18},{18,2},{3,19},{19,3},{4,20},{20... | collective-permute-start | bytes 786440 | tf_op jit(solution)/shard_map/right_far_row/ppermute | solution.py:26
  21.8 0.0 collective-permute-done.3.refs_3_
  21.8 0.0 collective-permute-done.refs_1_
  21.8 2.7 %own.1 = (f32[2048,256]{1,0:T(8,128)S(1)}, f32[4,128]{1,0:T(4,128)S(1)}, s32[32,128]{1,0:T(8,128)S(1)}) custom-call(s32[2,16]{1,0:T(2,128)} %bitcast.4, s32[2,16]{1,0:T(2,128)} %bitcast.6, bf16[2048,128]{1,0:T(8,128)(2,1)S(1)} %get-tuple-element.24.refs_0_, bf16[2048,128]{1,0:T(8,128)(2,1)S(1)} %collective-permute-done.refs_1_, ...), custom_call_target="tpu_custom_call" | custom-call | tf_op jit(solution)/shard_map/own/pallas_call | solution.py:193
  24.5 0.6 %collective-permute-start.9 = (f32[4,128]{1,0:T(4,128)S(1)}, f32[4,128]{1,0:T(4,128)S(1)}, u32[]{:S(2)}, u32[]{:S(2)}) collective-permute-start(f32[4,128]{1,0:T(4,128)S(1)} %get-tuple-element.30.sums), channel_id=1, source_target_pairs={{0,16},{16,0},{1,17},{17,1},{2,18},{18,2},{3,19},{19,3},{4,20},{20... | collective-permute-start | bytes 6152 | tf_op jit(solution)/shard_map/sums_row/ppermute | solution.py:26
  25.1 2.4 %collective-permute-done.8.refs_0_ = bf16[256,512]{1,0:T(8,128)(2,1)S(1)} collective-permute-done((bf16[256,512]{1,0:T(8,128)(2,1)S(1)}, bf16[256,512]{1,0:T(8,128)(2,1)S(1)}, u32[]{:S(2)}, u32[]{:S(2)}) %collective-permute-start.8) | collective-permute-done | bytes 262176 | tf_op jit(solution)/shard_map/right_opposite/ppermute | solution.py:26
  27.4 1.3 %collective-permute-done.7.refs_7_ = bf16[256,512]{1,0:T(8,128)(2,1)S(1)} collective-permute-done((bf16[256,512]{1,0:T(8,128)(2,1)S(1)}, bf16[256,512]{1,0:T(8,128)(2,1)S(1)}, u32[]{:S(2)}, u32[]{:S(2)}) %collective-permute-start.7) | collective-permute-done | bytes 262176 | tf_op jit(solution)/shard_map/right_far_row/ppermute | solution.py:26
  28.8 0.0 collective-permute-done.9.other
  28.8 0.1 scale.1
  28.9 0.5 %collective-permute-start.11 = (bf16[512,256]{1,0:T(8,128)(2,1)S(1)}, bf16[512,256]{1,0:T(8,128)(2,1)S(1)}, u32[]{:S(2)}, u32[]{:S(2)}) collective-permute-start(bf16[512,256]{1,0:T(8,128)(2,1)S(1)} %get-tuple-element.37), channel_id=1, source_target_pairs={{0,1},{1,0},{2,3},{3,2},{4,5},{5,4},{6,7},{7,6},{8,9},{9,8},{10,11... | collective-permute-start | bytes 786440 | tf_op jit(solution)/shard_map/sent/ppermute | solution.py:26
  29.4 1.5 %collective-permute-start.13 = (bf16[256,512]{1,0:T(8,128)(2,1)S(1)}, bf16[256,512]{1,0:T(8,128)(2,1)S(1)}, u32[]{:S(2)}, u32[]{:S(2)}) collective-permute-start(bf16[256,512]{1,0:T(8,128)(2,1)S(1)} %collective-permute-done.8.refs_0_), channel_id=1, source_target_pairs={{0,16},{16,0},{1,17},{17,1},{2,18},{18,2},{3,19},{19,3},{4,20},{20... | collective-permute-start | bytes 786440 | tf_op jit(solution)/shard_map/right_opposite_row/ppermute | solution.py:26
  30.9 1.2 %collective-permute-start.12 = (f32[8,128]{1,0:T(8,128)S(1)}, f32[8,128]{1,0:T(8,128)S(1)}, u32[]{:S(2)}, u32[]{:S(2)}) collective-permute-start(f32[8,128]{1,0:T(8,128)S(1)} %get-tuple-element.36), channel_id=1, source_target_pairs={{0,2},{1,3},{2,0},{3,1},{4,6},{5,7},{6,4},{7,5},{8,10},{9,11},{10,... | collective-permute-start | bytes 12296 | tf_op jit(solution)/shard_map/sums_far/ppermute | solution.py:26
  32.1 2.7 %collective-permute-start.10 = (f32[8,128]{1,0:T(8,128)S(1)}, f32[8,128]{1,0:T(8,128)S(1)}, u32[]{:S(2)}, u32[]{:S(2)}) collective-permute-start(f32[8,128]{1,0:T(8,128)S(1)} %get-tuple-element.36), channel_id=1, source_target_pairs={{0,3},{1,2},{2,1},{3,0},{4,7},{5,6},{6,5},{7,4},{8,11},{9,10},{10,... | collective-permute-start | bytes 12296 | tf_op jit(solution)/shard_map/sums_opposite/ppermute | solution.py:26
  34.8 0.7 %collective-permute-done.12.message = f32[8,128]{1,0:T(8,128)S(1)} collective-permute-done((f32[8,128]{1,0:T(8,128)S(1)}, f32[8,128]{1,0:T(8,128)S(1)}, u32[]{:S(2)}, u32[]{:S(2)}) %collective-permute-start.12) | collective-permute-done | bytes 4128 | tf_op jit(solution)/shard_map/sums_far/ppermute | solution.py:26
  35.5 1.4 %far.1 = (bf16[512,1024]{1,0:T(8,128)(2,1)}, bf16[512,512]{1,0:T(8,128)(2,1)S(1)}) custom-call(f32[8,128]{1,0:T(8,128)S(1)} %collective-permute-done.12.message, bf16[512,256]{1,0:T(8,128)(2,1)S(1)} %get-tuple-element.38.own, bf16[2048,128]{1,0:T(8,128)(2,1)S(1)} %get-tuple-element.24.refs_0_, bf16[2048,128]{1,0:T(8,128)(2,1)S(1)} %collective-permute-done.refs_1_, ...), custom_call_target="tpu_custom_call" | custom-call | tf_op jit(solution)/shard_map/far/pallas_call | solution.py:325
  36.9 0.6 %collective-permute-done.10.message = f32[8,128]{1,0:T(8,128)S(1)} collective-permute-done((f32[8,128]{1,0:T(8,128)S(1)}, f32[8,128]{1,0:T(8,128)S(1)}, u32[]{:S(2)}, u32[]{:S(2)}) %collective-permute-start.10) | collective-permute-done | bytes 4128 | tf_op jit(solution)/shard_map/sums_opposite/ppermute | solution.py:26
  37.5 0.0 collective-permute-done.11.sent
  37.5 0.0 collective-permute-done.13.refs_1_
  37.5 1.4 %last.1 = bf16[512,1024]{1,0:T(8,128)(2,1)} custom-call(f32[8,128]{1,0:T(8,128)S(1)} %collective-permute-done.10.message, bf16[512,256]{1,0:T(8,128)(2,1)S(1)} %collective-permute-done.11.sent, bf16[512,512]{1,0:T(8,128)(2,1)S(1)} %get-tuple-element.40.deep, bf16[256,512]{1,0:T(8,128)(2,1)S(1)} %collective-permute-done.8.refs_0_, ...), custom_call_target="tpu_custom_call", output_to_operand_aliasing={{}: (5, {})} | custom-call | tf_op jit(solution)/shard_map/last/pallas_call | solution.py:362
  (1 shorter events, 0.0 us)
Async XLA Ops:
  1.2 16.2 %collective-permute-start.1 = (bf16[256,512]{1,0:T(8,128)(2,1)}, bf16[256,512]{1,0:T(8,128)(2,1)S(1)}, u32[]{:S(2)}, u32[]{:S(2)}) collective-permute-start(bf16[256,512]{1,0:T(8,128)(2,1)} %refs_6_), channel_id=1, source_target_pairs={{0,2},{1,3},{2,0},{3,1},{4,6},{5,7},{6,4},{7,5},{8,10},{9,11},{10,... | collective-permute-start | bytes 786440 | tf_op jit(solution)/shard_map/right_far/ppermute | solution.py:26
  5.3 12.1 %collective-permute-start.2 = (bf16[1024,128]{1,0:T(8,128)(2,1)S(1)}, bf16[1024,128]{1,0:T(8,128)(2,1)S(1)}, u32[]{:S(2)}, u32[]{:S(2)}) collective-permute-start(bf16[1024,128]{1,0:T(8,128)(2,1)S(1)} %get-tuple-element.27), channel_id=1, source_target_pairs={{0,8},{4,12},{8,0},{12,4},{1,9},{5,13},{9,1},{13,5},{2,10},{6,14},... | collective-permute-start | bytes 786440 | tf_op jit(solution)/shard_map/left_across/ppermute | solution.py:26
  6.8 11.9 %collective-permute-start.4 = (bf16[1024,128]{1,0:T(8,128)(2,1)S(1)}, bf16[1024,128]{1,0:T(8,128)(2,1)S(1)}, u32[]{:S(2)}, u32[]{:S(2)}) collective-permute-start(bf16[1024,128]{1,0:T(8,128)(2,1)S(1)} %get-tuple-element.29), channel_id=1, source_target_pairs={{0,8},{4,12},{8,0},{12,4},{1,9},{5,13},{9,1},{13,5},{2,10},{6,14},... | collective-permute-start | bytes 786440 | tf_op jit(solution)/shard_map/left_across/ppermute | solution.py:26
  7.4 14.4 %collective-permute-start = (bf16[2048,128]{1,0:T(8,128)(2,1)S(1)}, bf16[2048,128]{1,0:T(8,128)(2,1)S(1)}, u32[]{:S(2)}, u32[]{:S(2)}) collective-permute-start(bf16[2048,128]{1,0:T(8,128)(2,1)S(1)} %get-tuple-element.24.refs_0_), channel_id=1, source_target_pairs={{0,4},{4,0},{8,12},{12,8},{1,5},{5,1},{9,13},{13,9},{2,6},{6,2},{1... | collective-permute-start | bytes 1572872 | tf_op jit(solution)/shard_map/left_early/ppermute | solution.py:26
  7.4 12.9 %collective-permute-start.6 = (bf16[256,512]{1,0:T(8,128)(2,1)}, bf16[256,512]{1,0:T(8,128)(2,1)S(1)}, u32[]{:S(2)}, u32[]{:S(2)}) collective-permute-start(bf16[256,512]{1,0:T(8,128)(2,1)} %refs_6_), channel_id=1, source_target_pairs={{0,16},{16,0},{1,17},{17,1},{2,18},{18,2},{3,19},{19,3},{4,20},{20... | collective-permute-start | bytes 786440 | tf_op jit(solution)/shard_map/right_near/ppermute | solution.py:26
  17.5 4.3 %collective-permute-start.3 = (bf16[1024,128]{1,0:T(8,128)(2,1)S(1)}, bf16[1024,128]{1,0:T(8,128)(2,1)S(1)}, u32[]{:S(2)}, u32[]{:S(2)}) collective-permute-start(bf16[1024,128]{1,0:T(8,128)(2,1)S(1)} %collective-permute-done.2.refs_2_), channel_id=1, source_target_pairs={{0,4},{4,0},{8,12},{12,8},{1,5},{5,1},{9,13},{13,9},{2,6},{6,2},{1... | collective-permute-start | bytes 786440 | tf_op jit(solution)/shard_map/left_late/ppermute | solution.py:26
  18.7 3.1 %collective-permute-start.5 = (bf16[1024,128]{1,0:T(8,128)(2,1)S(1)}, bf16[1024,128]{1,0:T(8,128)(2,1)S(1)}, u32[]{:S(2)}, u32[]{:S(2)}) collective-permute-start(bf16[1024,128]{1,0:T(8,128)(2,1)S(1)} %collective-permute-done.4.refs_4_), channel_id=1, source_target_pairs={{0,4},{4,0},{8,12},{12,8},{1,5},{5,1},{9,13},{13,9},{2,6},{6,2},{1... | collective-permute-start | bytes 786440 | tf_op jit(solution)/shard_map/left_late/ppermute | solution.py:26
  18.7 8.7 %collective-permute-start.8 = (bf16[256,512]{1,0:T(8,128)(2,1)S(1)}, bf16[256,512]{1,0:T(8,128)(2,1)S(1)}, u32[]{:S(2)}, u32[]{:S(2)}) collective-permute-start(bf16[256,512]{1,0:T(8,128)(2,1)S(1)} %collective-permute-done.1.refs_6_), channel_id=1, source_target_pairs={{0,1},{1,0},{2,3},{3,2},{4,5},{5,4},{6,7},{7,6},{8,9},{9,8},{10,11... | collective-permute-start | bytes 786440 | tf_op jit(solution)/shard_map/right_opposite/ppermute | solution.py:26
  20.3 8.5 %collective-permute-start.7 = (bf16[256,512]{1,0:T(8,128)(2,1)S(1)}, bf16[256,512]{1,0:T(8,128)(2,1)S(1)}, u32[]{:S(2)}, u32[]{:S(2)}) collective-permute-start(bf16[256,512]{1,0:T(8,128)(2,1)S(1)} %collective-permute-done.1.refs_6_), channel_id=1, source_target_pairs={{0,16},{16,0},{1,17},{17,1},{2,18},{18,2},{3,19},{19,3},{4,20},{20... | collective-permute-start | bytes 786440 | tf_op jit(solution)/shard_map/right_far_row/ppermute | solution.py:26
  24.5 4.3 %collective-permute-start.9 = (f32[4,128]{1,0:T(4,128)S(1)}, f32[4,128]{1,0:T(4,128)S(1)}, u32[]{:S(2)}, u32[]{:S(2)}) collective-permute-start(f32[4,128]{1,0:T(4,128)S(1)} %get-tuple-element.30.sums), channel_id=1, source_target_pairs={{0,16},{16,0},{1,17},{17,1},{2,18},{18,2},{3,19},{19,3},{4,20},{20... | collective-permute-start | bytes 6152 | tf_op jit(solution)/shard_map/sums_row/ppermute | solution.py:26
  28.9 8.6 %collective-permute-start.11 = (bf16[512,256]{1,0:T(8,128)(2,1)S(1)}, bf16[512,256]{1,0:T(8,128)(2,1)S(1)}, u32[]{:S(2)}, u32[]{:S(2)}) collective-permute-start(bf16[512,256]{1,0:T(8,128)(2,1)S(1)} %get-tuple-element.37), channel_id=1, source_target_pairs={{0,1},{1,0},{2,3},{3,2},{4,5},{5,4},{6,7},{7,6},{8,9},{9,8},{10,11... | collective-permute-start | bytes 786440 | tf_op jit(solution)/shard_map/sent/ppermute | solution.py:26
  29.4 8.1 %collective-permute-start.13 = (bf16[256,512]{1,0:T(8,128)(2,1)S(1)}, bf16[256,512]{1,0:T(8,128)(2,1)S(1)}, u32[]{:S(2)}, u32[]{:S(2)}) collective-permute-start(bf16[256,512]{1,0:T(8,128)(2,1)S(1)} %collective-permute-done.8.refs_0_), channel_id=1, source_target_pairs={{0,16},{16,0},{1,17},{17,1},{2,18},{18,2},{3,19},{19,3},{4,20},{20... | collective-permute-start | bytes 786440 | tf_op jit(solution)/shard_map/right_opposite_row/ppermute | solution.py:26
  30.9 4.6 %collective-permute-start.12 = (f32[8,128]{1,0:T(8,128)S(1)}, f32[8,128]{1,0:T(8,128)S(1)}, u32[]{:S(2)}, u32[]{:S(2)}) collective-permute-start(f32[8,128]{1,0:T(8,128)S(1)} %get-tuple-element.36), channel_id=1, source_target_pairs={{0,2},{1,3},{2,0},{3,1},{4,6},{5,7},{6,4},{7,5},{8,10},{9,11},{10,... | collective-permute-start | bytes 12296 | tf_op jit(solution)/shard_map/sums_far/ppermute | solution.py:26
  32.1 5.4 %collective-permute-start.10 = (f32[8,128]{1,0:T(8,128)S(1)}, f32[8,128]{1,0:T(8,128)S(1)}, u32[]{:S(2)}, u32[]{:S(2)}) collective-permute-start(f32[8,128]{1,0:T(8,128)S(1)} %get-tuple-element.36), channel_id=1, source_target_pairs={{0,3},{1,2},{2,1},{3,0},{4,7},{5,6},{6,5},{7,4},{8,11},{9,10},{10,... | collective-permute-start | bytes 12296 | tf_op jit(solution)/shard_map/sums_opposite/ppermute | solution.py:26

commit v5 on v4

--- a/solution.py
+++ b/solution.py
@@ -392,7 +392,7 @@
     keep = retained_target_flag.T
     half = lax.axis_size("col") // 2
     whole, masked, meta = mask_blocks(stored_tile_flag.T, source_matrix_strip, place, keep)
-    target, meta = together(target_matrix_strip, meta)
+    target = target_matrix_strip
     across = [swap(piece, "col", half, "left_across") for piece in masked]
     far = swap(target, "layer", 2, "right_far")
     near = gather(target, "row", "right_near")

time: 39.1 us -> 38.5 us (0.985)
  waiting for transfers between devices: 14.8 us -> 14.2 us
    ppermute x14, waiting for transfers between devices: 14.8 us -> 14.2 us  [swap(): return lax.ppermute(value, axis, [(i, i ^ bit) for i in range(count)])]
  transfers between devices with their start and end apart: 14 -> 14, of which waited for: 6 -> 5; matrix products, arithmetic and copies ran while one was open for 0% -> 0% of each run, Pallas kernels for 10% -> 14%
where the time goes in v5:
time: 38.5 us; the launch traced here: 38.4 us
  starting transfers between devices  17.2 us (45%)
  waiting for transfers between devices  14.2 us (37%)
  Pallas kernels  6.83 us (18%)
    ppermute x14, starting transfers between devices, swap(): return lax.ppermute(value, axis, [(i, i ^ bit) for i in range(count)])  17.2 us
    ppermute x14, waiting for transfers between devices, swap(): return lax.ppermute(value, axis, [(i, i ^ bit) for i in range(count)])  14.2 us
    pallas_call x1, Pallas kernels, own_squares(): call(functools.partial(own_kernel, len(earlies), len(rights), band), (jax...  2.66 us
    pallas_call x1, Pallas kernels, last_tiles(): call(functools.partial(last_kernel, len(rights), total_rows), jax.ShapeDt...  1.44 us
    pallas_call x1, Pallas kernels, far_tiles(): call(functools.partial(far_kernel, len(earlies), len(rights), total_rows)...  1.41 us
    pallas_call x1, Pallas kernels, mask_blocks(): call(mask_kernel, [jax.ShapeDtypeStruct(source.shape, source.dtype)] + [j...  1.22 us
  transfers between devices with their start and end apart: 14, of which 5 were waited for; matrix products, arithmetic and copies ran while one was open for 0% of the time, Pallas kernels for 14%

profile of v5, /device:TPU:0, one launch (start us, length us, event | category | flops | bytes accessed | tf_op | source)
XLA Modules:
  0.0 38.4 jit_solution(45876984014273685)
XLA Ops:
  0.0 4.0 %collective-permute-start.1 = (bf16[256,512]{1,0:T(8,128)(2,1)}, bf16[256,512]{1,0:T(8,128)(2,1)S(1)}, u32[]{:S(2)}, u32[]{:S(2)}) collective-permute-start(bf16[256,512]{1,0:T(8,128)(2,1)} %refs_6_.1), channel_id=1, source_target_pairs={{0,2},{1,3},{2,0},{3,1},{4,6},{5,7},{6,4},{7,5},{8,10},{9,11},{10,... | collective-permute-start | bytes 786440 | tf_op jit(solution)/shard_map/right_far/ppermute | solution.py:26
  4.0 1.2 %mask.1 = (bf16[2048,128]{1,0:T(8,128)(2,1)S(1)}, bf16[1024,128]{1,0:T(8,128)(2,1)S(1)}, bf16[1024,128]{1,0:T(8,128)(2,1)S(1)}, f32[4,128]{1,0:T(4,128)S(1)}) custom-call(s32[1,16]{1,0:T(1,128)} %bitcast.7, bf16[2048,128]{1,0:T(8,128)(2,1)} %source.1, s32[2,16]{1,0:T(2,128)} %bitcast.3, s32[2,16]{1,0:T(2,128)} %bitcast.5), custom_call_target="tpu_custom_call" | custom-call | tf_op jit(solution)/shard_map/mask/pallas_call | solution.py:101
  5.3 1.6 %collective-permute-start.2 = (bf16[1024,128]{1,0:T(8,128)(2,1)S(1)}, bf16[1024,128]{1,0:T(8,128)(2,1)S(1)}, u32[]{:S(2)}, u32[]{:S(2)}) collective-permute-start(bf16[1024,128]{1,0:T(8,128)(2,1)S(1)} %get-tuple-element.23), channel_id=1, source_target_pairs={{0,8},{4,12},{8,0},{12,4},{1,9},{5,13},{9,1},{13,5},{2,10},{6,14},... | collective-permute-start | bytes 786440 | tf_op jit(solution)/shard_map/left_across/ppermute | solution.py:26
  6.8 0.5 %collective-permute-start.4 = (bf16[1024,128]{1,0:T(8,128)(2,1)S(1)}, bf16[1024,128]{1,0:T(8,128)(2,1)S(1)}, u32[]{:S(2)}, u32[]{:S(2)}) collective-permute-start(bf16[1024,128]{1,0:T(8,128)(2,1)S(1)} %get-tuple-element.25), channel_id=1, source_target_pairs={{0,8},{4,12},{8,0},{12,4},{1,9},{5,13},{9,1},{13,5},{2,10},{6,14},... | collective-permute-start | bytes 786440 | tf_op jit(solution)/shard_map/left_across/ppermute | solution.py:26
  7.4 0.0 collective-permute-start
  7.4 1.5 %collective-permute-start.6 = (bf16[256,512]{1,0:T(8,128)(2,1)}, bf16[256,512]{1,0:T(8,128)(2,1)S(1)}, u32[]{:S(2)}, u32[]{:S(2)}) collective-permute-start(bf16[256,512]{1,0:T(8,128)(2,1)} %refs_6_.1), channel_id=1, source_target_pairs={{0,16},{16,0},{1,17},{17,1},{2,18},{18,2},{3,19},{19,3},{4,20},{20... | collective-permute-start | bytes 786440 | tf_op jit(solution)/shard_map/right_near/ppermute | solution.py:26
  8.8 7.3 %collective-permute-done.1.refs_6_ = bf16[256,512]{1,0:T(8,128)(2,1)S(1)} collective-permute-done((bf16[256,512]{1,0:T(8,128)(2,1)}, bf16[256,512]{1,0:T(8,128)(2,1)S(1)}, u32[]{:S(2)}, u32[]{:S(2)}) %collective-permute-start.1) | collective-permute-done | bytes 262176 | tf_op jit(solution)/shard_map/right_far/ppermute | solution.py:26
  16.2 0.0 collective-permute-done.2.refs_2_
  16.2 0.0 collective-permute-start.3
  16.2 2.5 %collective-permute-done.4.refs_4_ = bf16[1024,128]{1,0:T(8,128)(2,1)S(1)} collective-permute-done((bf16[1024,128]{1,0:T(8,128)(2,1)S(1)}, bf16[1024,128]{1,0:T(8,128)(2,1)S(1)}, u32[]{:S(2)}, u32[]{:S(2)}) %collective-permute-start.4) | collective-permute-done | bytes 262176 | tf_op jit(solution)/shard_map/left_across/ppermute | solution.py:26
  18.7 0.0 collective-permute-start.5
  18.7 1.6 %collective-permute-start.8 = (bf16[256,512]{1,0:T(8,128)(2,1)S(1)}, bf16[256,512]{1,0:T(8,128)(2,1)S(1)}, u32[]{:S(2)}, u32[]{:S(2)}) collective-permute-start(bf16[256,512]{1,0:T(8,128)(2,1)S(1)} %collective-permute-done.1.refs_6_), channel_id=1, source_target_pairs={{0,1},{1,0},{2,3},{3,2},{4,5},{5,4},{6,7},{7,6},{8,9},{9,8},{10,11... | collective-permute-start | bytes 786440 | tf_op jit(solution)/shard_map/right_opposite/ppermute | solution.py:26
  20.3 0.0 collective-permute-done.6.refs_7_
  20.3 1.5 %collective-permute-start.7 = (bf16[256,512]{1,0:T(8,128)(2,1)S(1)}, bf16[256,512]{1,0:T(8,128)(2,1)S(1)}, u32[]{:S(2)}, u32[]{:S(2)}) collective-permute-start(bf16[256,512]{1,0:T(8,128)(2,1)S(1)} %collective-permute-done.1.refs_6_), channel_id=1, source_target_pairs={{0,16},{16,0},{1,17},{17,1},{2,18},{18,2},{3,19},{19,3},{4,20},{20... | collective-permute-start | bytes 786440 | tf_op jit(solution)/shard_map/right_far_row/ppermute | solution.py:26
  21.8 0.0 collective-permute-done.3.refs_3_
  21.8 0.0 collective-permute-done.5.refs_5_
  21.8 0.0 collective-permute-done.refs_1_
  21.8 2.7 %own.1 = (f32[2048,256]{1,0:T(8,128)S(1)}, f32[4,128]{1,0:T(4,128)S(1)}, s32[32,128]{1,0:T(8,128)S(1)}) custom-call(s32[2,16]{1,0:T(2,128)} %bitcast.4, s32[2,16]{1,0:T(2,128)} %bitcast.6, bf16[2048,128]{1,0:T(8,128)(2,1)S(1)} %get-tuple-element.22.refs_0_, bf16[2048,128]{1,0:T(8,128)(2,1)S(1)} %collective-permute-done.refs_1_, ...), custom_call_target="tpu_custom_call" | custom-call | tf_op jit(solution)/shard_map/own/pallas_call | solution.py:193
  24.5 0.6 %collective-permute-start.9 = (f32[4,128]{1,0:T(4,128)S(1)}, f32[4,128]{1,0:T(4,128)S(1)}, u32[]{:S(2)}, u32[]{:S(2)}) collective-permute-start(f32[4,128]{1,0:T(4,128)S(1)} %get-tuple-element.26.sums), channel_id=1, source_target_pairs={{0,16},{16,0},{1,17},{17,1},{2,18},{18,2},{3,19},{19,3},{4,20},{20... | collective-permute-start | bytes 6152 | tf_op jit(solution)/shard_map/sums_row/ppermute | solution.py:26
  25.1 2.4 %collective-permute-done.8.refs_0_ = bf16[256,512]{1,0:T(8,128)(2,1)S(1)} collective-permute-done((bf16[256,512]{1,0:T(8,128)(2,1)S(1)}, bf16[256,512]{1,0:T(8,128)(2,1)S(1)}, u32[]{:S(2)}, u32[]{:S(2)}) %collective-permute-start.8) | collective-permute-done | bytes 262176 | tf_op jit(solution)/shard_map/right_opposite/ppermute | solution.py:26
  27.4 1.3 %collective-permute-done.7.refs_7_ = bf16[256,512]{1,0:T(8,128)(2,1)S(1)} collective-permute-done((bf16[256,512]{1,0:T(8,128)(2,1)S(1)}, bf16[256,512]{1,0:T(8,128)(2,1)S(1)}, u32[]{:S(2)}, u32[]{:S(2)}) %collective-permute-start.7) | collective-permute-done | bytes 262176 | tf_op jit(solution)/shard_map/right_far_row/ppermute | solution.py:26
  28.8 0.0 collective-permute-done.9.other
  28.8 0.1 scale.1
  28.9 0.5 %collective-permute-start.11 = (bf16[512,256]{1,0:T(8,128)(2,1)S(1)}, bf16[512,256]{1,0:T(8,128)(2,1)S(1)}, u32[]{:S(2)}, u32[]{:S(2)}) collective-permute-start(bf16[512,256]{1,0:T(8,128)(2,1)S(1)} %get-tuple-element.33), channel_id=1, source_target_pairs={{0,1},{1,0},{2,3},{3,2},{4,5},{5,4},{6,7},{7,6},{8,9},{9,8},{10,11... | collective-permute-start | bytes 786440 | tf_op jit(solution)/shard_map/sent/ppermute | solution.py:26
  29.4 1.5 %collective-permute-start.13 = (bf16[256,512]{1,0:T(8,128)(2,1)S(1)}, bf16[256,512]{1,0:T(8,128)(2,1)S(1)}, u32[]{:S(2)}, u32[]{:S(2)}) collective-permute-start(bf16[256,512]{1,0:T(8,128)(2,1)S(1)} %collective-permute-done.8.refs_0_), channel_id=1, source_target_pairs={{0,16},{16,0},{1,17},{17,1},{2,18},{18,2},{3,19},{19,3},{4,20},{20... | collective-permute-start | bytes 786440 | tf_op jit(solution)/shard_map/right_opposite_row/ppermute | solution.py:26
  30.9 0.3 collective-permute-start.12
  31.2 3.6 %collective-permute-start.10 = (f32[8,128]{1,0:T(8,128)S(1)}, f32[8,128]{1,0:T(8,128)S(1)}, u32[]{:S(2)}, u32[]{:S(2)}) collective-permute-start(f32[8,128]{1,0:T(8,128)S(1)} %get-tuple-element.32), channel_id=1, source_target_pairs={{0,3},{1,2},{2,1},{3,0},{4,7},{5,6},{6,5},{7,4},{8,11},{9,10},{10,... | collective-permute-start | bytes 12296 | tf_op jit(solution)/shard_map/sums_opposite/ppermute | solution.py:26
  34.8 0.7 %collective-permute-done.12.message = f32[8,128]{1,0:T(8,128)S(1)} collective-permute-done((f32[8,128]{1,0:T(8,128)S(1)}, f32[8,128]{1,0:T(8,128)S(1)}, u32[]{:S(2)}, u32[]{:S(2)}) %collective-permute-start.12) | collective-permute-done | bytes 4128 | tf_op jit(solution)/shard_map/sums_far/ppermute | solution.py:26
  35.5 1.4 %far.1 = (bf16[512,1024]{1,0:T(8,128)(2,1)}, bf16[512,512]{1,0:T(8,128)(2,1)S(1)}) custom-call(f32[8,128]{1,0:T(8,128)S(1)} %collective-permute-done.12.message, bf16[512,256]{1,0:T(8,128)(2,1)S(1)} %get-tuple-element.34.own, bf16[2048,128]{1,0:T(8,128)(2,1)S(1)} %get-tuple-element.22.refs_0_, bf16[2048,128]{1,0:T(8,128)(2,1)S(1)} %collective-permute-done.refs_1_, ...), custom_call_target="tpu_custom_call" | custom-call | tf_op jit(solution)/shard_map/far/pallas_call | solution.py:325
  36.9 0.0 collective-permute-done.11.sent
  36.9 0.0 collective-permute-done.13.refs_1_
  36.9 1.4 %last.1 = bf16[512,1024]{1,0:T(8,128)(2,1)} custom-call(f32[8,128]{1,0:T(8,128)S(1)} %collective-permute-done.10.message, bf16[512,256]{1,0:T(8,128)(2,1)S(1)} %collective-permute-done.11.sent, bf16[512,512]{1,0:T(8,128)(2,1)S(1)} %get-tuple-element.36.deep, bf16[256,512]{1,0:T(8,128)(2,1)S(1)} %collective-permute-done.8.refs_0_, ...), custom_call_target="tpu_custom_call", output_to_operand_aliasing={{}: (5, {})} | custom-call | tf_op jit(solution)/shard_map/last/pallas_call | solution.py:362
  (1 shorter events, 0.0 us)
Async XLA Ops:
  0.0 16.2 %collective-permute-start.1 = (bf16[256,512]{1,0:T(8,128)(2,1)}, bf16[256,512]{1,0:T(8,128)(2,1)S(1)}, u32[]{:S(2)}, u32[]{:S(2)}) collective-permute-start(bf16[256,512]{1,0:T(8,128)(2,1)} %refs_6_.1), channel_id=1, source_target_pairs={{0,2},{1,3},{2,0},{3,1},{4,6},{5,7},{6,4},{7,5},{8,10},{9,11},{10,... | collective-permute-start | bytes 786440 | tf_op jit(solution)/shard_map/right_far/ppermute | solution.py:26
  5.3 10.9 %collective-permute-start.2 = (bf16[1024,128]{1,0:T(8,128)(2,1)S(1)}, bf16[1024,128]{1,0:T(8,128)(2,1)S(1)}, u32[]{:S(2)}, u32[]{:S(2)}) collective-permute-start(bf16[1024,128]{1,0:T(8,128)(2,1)S(1)} %get-tuple-element.23), channel_id=1, source_target_pairs={{0,8},{4,12},{8,0},{12,4},{1,9},{5,13},{9,1},{13,5},{2,10},{6,14},... | collective-permute-start | bytes 786440 | tf_op jit(solution)/shard_map/left_across/ppermute | solution.py:26
  6.8 11.9 %collective-permute-start.4 = (bf16[1024,128]{1,0:T(8,128)(2,1)S(1)}, bf16[1024,128]{1,0:T(8,128)(2,1)S(1)}, u32[]{:S(2)}, u32[]{:S(2)}) collective-permute-start(bf16[1024,128]{1,0:T(8,128)(2,1)S(1)} %get-tuple-element.25), channel_id=1, source_target_pairs={{0,8},{4,12},{8,0},{12,4},{1,9},{5,13},{9,1},{13,5},{2,10},{6,14},... | collective-permute-start | bytes 786440 | tf_op jit(solution)/shard_map/left_across/ppermute | solution.py:26
  7.4 14.4 %collective-permute-start = (bf16[2048,128]{1,0:T(8,128)(2,1)S(1)}, bf16[2048,128]{1,0:T(8,128)(2,1)S(1)}, u32[]{:S(2)}, u32[]{:S(2)}) collective-permute-start(bf16[2048,128]{1,0:T(8,128)(2,1)S(1)} %get-tuple-element.22.refs_0_), channel_id=1, source_target_pairs={{0,4},{4,0},{8,12},{12,8},{1,5},{5,1},{9,13},{13,9},{2,6},{6,2},{1... | collective-permute-start | bytes 1572872 | tf_op jit(solution)/shard_map/left_early/ppermute | solution.py:26
  7.4 12.9 %collective-permute-start.6 = (bf16[256,512]{1,0:T(8,128)(2,1)}, bf16[256,512]{1,0:T(8,128)(2,1)S(1)}, u32[]{:S(2)}, u32[]{:S(2)}) collective-permute-start(bf16[256,512]{1,0:T(8,128)(2,1)} %refs_6_.1), channel_id=1, source_target_pairs={{0,16},{16,0},{1,17},{17,1},{2,18},{18,2},{3,19},{19,3},{4,20},{20... | collective-permute-start | bytes 786440 | tf_op jit(solution)/shard_map/right_near/ppermute | solution.py:26
  16.2 5.6 %collective-permute-start.3 = (bf16[1024,128]{1,0:T(8,128)(2,1)S(1)}, bf16[1024,128]{1,0:T(8,128)(2,1)S(1)}, u32[]{:S(2)}, u32[]{:S(2)}) collective-permute-start(bf16[1024,128]{1,0:T(8,128)(2,1)S(1)} %collective-permute-done.2.refs_2_), channel_id=1, source_target_pairs={{0,4},{4,0},{8,12},{12,8},{1,5},{5,1},{9,13},{13,9},{2,6},{6,2},{1... | collective-permute-start | bytes 786440 | tf_op jit(solution)/shard_map/left_late/ppermute | solution.py:26
  18.7 3.1 %collective-permute-start.5 = (bf16[1024,128]{1,0:T(8,128)(2,1)S(1)}, bf16[1024,128]{1,0:T(8,128)(2,1)S(1)}, u32[]{:S(2)}, u32[]{:S(2)}) collective-permute-start(bf16[1024,128]{1,0:T(8,128)(2,1)S(1)} %collective-permute-done.4.refs_4_), channel_id=1, source_target_pairs={{0,4},{4,0},{8,12},{12,8},{1,5},{5,1},{9,13},{13,9},{2,6},{6,2},{1... | collective-permute-start | bytes 786440 | tf_op jit(solution)/shard_map/left_late/ppermute | solution.py:26
  18.7 8.7 %collective-permute-start.8 = (bf16[256,512]{1,0:T(8,128)(2,1)S(1)}, bf16[256,512]{1,0:T(8,128)(2,1)S(1)}, u32[]{:S(2)}, u32[]{:S(2)}) collective-permute-start(bf16[256,512]{1,0:T(8,128)(2,1)S(1)} %collective-permute-done.1.refs_6_), channel_id=1, source_target_pairs={{0,1},{1,0},{2,3},{3,2},{4,5},{5,4},{6,7},{7,6},{8,9},{9,8},{10,11... | collective-permute-start | bytes 786440 | tf_op jit(solution)/shard_map/right_opposite/ppermute | solution.py:26
  20.3 8.5 %collective-permute-start.7 = (bf16[256,512]{1,0:T(8,128)(2,1)S(1)}, bf16[256,512]{1,0:T(8,128)(2,1)S(1)}, u32[]{:S(2)}, u32[]{:S(2)}) collective-permute-start(bf16[256,512]{1,0:T(8,128)(2,1)S(1)} %collective-permute-done.1.refs_6_), channel_id=1, source_target_pairs={{0,16},{16,0},{1,17},{17,1},{2,18},{18,2},{3,19},{19,3},{4,20},{20... | collective-permute-start | bytes 786440 | tf_op jit(solution)/shard_map/right_far_row/ppermute | solution.py:26
  24.5 4.3 %collective-permute-start.9 = (f32[4,128]{1,0:T(4,128)S(1)}, f32[4,128]{1,0:T(4,128)S(1)}, u32[]{:S(2)}, u32[]{:S(2)}) collective-permute-start(f32[4,128]{1,0:T(4,128)S(1)} %get-tuple-element.26.sums), channel_id=1, source_target_pairs={{0,16},{16,0},{1,17},{17,1},{2,18},{18,2},{3,19},{19,3},{4,20},{20... | collective-permute-start | bytes 6152 | tf_op jit(solution)/shard_map/sums_row/ppermute | solution.py:26
  28.9 8.0 %collective-permute-start.11 = (bf16[512,256]{1,0:T(8,128)(2,1)S(1)}, bf16[512,256]{1,0:T(8,128)(2,1)S(1)}, u32[]{:S(2)}, u32[]{:S(2)}) collective-permute-start(bf16[512,256]{1,0:T(8,128)(2,1)S(1)} %get-tuple-element.33), channel_id=1, source_target_pairs={{0,1},{1,0},{2,3},{3,2},{4,5},{5,4},{6,7},{7,6},{8,9},{9,8},{10,11... | collective-permute-start | bytes 786440 | tf_op jit(solution)/shard_map/sent/ppermute | solution.py:26
  29.4 7.5 %collective-permute-start.13 = (bf16[256,512]{1,0:T(8,128)(2,1)S(1)}, bf16[256,512]{1,0:T(8,128)(2,1)S(1)}, u32[]{:S(2)}, u32[]{:S(2)}) collective-permute-start(bf16[256,512]{1,0:T(8,128)(2,1)S(1)} %collective-permute-done.8.refs_0_), channel_id=1, source_target_pairs={{0,16},{16,0},{1,17},{17,1},{2,18},{18,2},{3,19},{19,3},{4,20},{20... | collective-permute-start | bytes 786440 | tf_op jit(solution)/shard_map/right_opposite_row/ppermute | solution.py:26
  30.9 4.6 %collective-permute-start.12 = (f32[8,128]{1,0:T(8,128)S(1)}, f32[8,128]{1,0:T(8,128)S(1)}, u32[]{:S(2)}, u32[]{:S(2)}) collective-permute-start(f32[8,128]{1,0:T(8,128)S(1)} %get-tuple-element.32), channel_id=1, source_target_pairs={{0,2},{1,3},{2,0},{3,1},{4,6},{5,7},{6,4},{7,5},{8,10},{9,11},{10,... | collective-permute-start | bytes 12296 | tf_op jit(solution)/shard_map/sums_far/ppermute | solution.py:26
  31.2 5.7 %collective-permute-start.10 = (f32[8,128]{1,0:T(8,128)S(1)}, f32[8,128]{1,0:T(8,128)S(1)}, u32[]{:S(2)}, u32[]{:S(2)}) collective-permute-start(f32[8,128]{1,0:T(8,128)S(1)} %get-tuple-element.32), channel_id=1, source_target_pairs={{0,3},{1,2},{2,1},{3,0},{4,7},{5,6},{6,5},{7,4},{8,11},{9,10},{10,... | collective-permute-start | bytes 12296 | tf_op jit(solution)/shard_map/sums_opposite/ppermute | solution.py:26

commit v6 on v5

--- a/solution.py
+++ b/solution.py
@@ -260,11 +260,12 @@
     )(sums, other, meta, squares, picks)
 
 
-def far_tile(message, scales, rights, deep, product, message_s, copy, total_rows, result):
+def far_tile(message, scales, rights, deep, product, message_s, copy, total_rows, result, writes):
     layer = lax.axis_index("layer")
     me = lax.axis_index("row")
     scales[...] = 1.0 / (message[0:COLB, :] / jnp.float32(total_rows) + 1e-6)
     depth = rights[0].shape[0]
+    bands = deep.shape[0] // BS
     whole = None
     for k, right in enumerate(rights):
         columns = pl.ds(pl.multiple_of((me ^ k) * depth, depth), depth)
@@ -272,14 +273,23 @@
         whole = term if whole is None else whole + term
     product[...] = whole
     copy.wait()
-    bands = deep.shape[0] // BS
     for i in range(bands):
+        rows = pl.ds(i * BS, BS)
         for s in range(KOL):
             row = layer * bands + i
             block = message_s[COLB + s, row].astype(jnp.int32)
             weight = scales[pl.ds(block, 1), :] * message_s[COLB + KOL + s, row]
-            picked = product[pl.ds(i * BS, BS), pl.ds(pl.multiple_of(block * BS, BS), BS)]
-            result[pl.ds(i * BS, BS), pl.ds(s * BS, BS)] = (picked * picked * weight).astype(result.dtype)
+            picked = product[rows, pl.ds(pl.multiple_of(block * BS, BS), BS)]
+            result[rows, pl.ds(s * BS, BS)] = (picked * picked * weight).astype(result.dtype)
+        writes[i].start()
+
+
+def band_writes(result, out, bit, sem):
+    writes = []
+    for i in range(result.shape[0] // BS):
+        rows = pl.ds(i * BS, BS)
+        writes.append(pltpu.make_async_copy(result.at[rows, :], out.at[rows, tile_columns(bit)], sem.at[i]))
+    return writes
 
 
 def tile_columns(bit):
@@ -291,12 +301,12 @@
     chunks = [refs[c * n_left : (c + 1) * n_left] for c in range(CHUNKS)]
     refs = refs[CHUNKS * n_left :]
     rights, refs = refs[:n_right], refs[n_right:]
-    out, deep, scales, product, result, message_s, message_sem, sem = refs
+    out, deep, scales, product, result, message_s, message_sem, sem, write_sem = refs
     layer = lax.axis_index("layer")
     me = lax.axis_index("col")
     load = pltpu.make_async_copy(message, message_s, message_sem)
     load.start()
-    own_copy = pltpu.make_async_copy(own, out.at[:, tile_columns(0)], sem.at[0])
+    own_copy = pltpu.make_async_copy(own, out.at[:, tile_columns(0)], sem)
     own_copy.start()
     band = deep.shape[0]
     own_rows = pl.ds(pl.multiple_of(layer * band, band), band)
@@ -311,11 +321,11 @@
             for k, left in enumerate(chunks[c]):
                 deep[:, pl.ds(pl.multiple_of((me ^ (n_left + k)) * BS, BS), BS)] = left[rows, :]
 
-    far_tile(message, scales, rights, deep, product, message_s, load, total_rows, result)
-    far_copy = pltpu.make_async_copy(result, out.at[:, tile_columns(2)], sem.at[1])
-    far_copy.start()
+    writes = band_writes(result, out, 2, write_sem)
+    far_tile(message, scales, rights, deep, product, message_s, load, total_rows, result, writes)
     own_copy.wait()
-    far_copy.wait()
+    for write in writes:
+        write.wait()
 
 
 def far_tiles(message, own, earlies, chunks, rights, layers, total_rows):
@@ -336,7 +346,8 @@
             pltpu.VMEM((band, OUT), jnp.bfloat16),
             pltpu.SMEM(message.shape, jnp.float32),
             pltpu.SemaphoreType.DMA,
-            pltpu.SemaphoreType.DMA((2,)),
+            pltpu.SemaphoreType.DMA,
+            pltpu.SemaphoreType.DMA((band // BS,)),
         ],
         FAR_COST,
         "far",
@@ -345,16 +356,16 @@
 
 def last_kernel(n_right, total_rows, message, sent, deep, *refs):
     rights, refs = refs[:n_right], refs[n_right:]
-    _, out, scales, product, result, message_s, message_sem, sem = refs
+    _, out, scales, product, result, message_s, message_sem, sem, write_sem = refs
     load = pltpu.make_async_copy(message, message_s, message_sem)
     load.start()
-    sent_copy = pltpu.make_async_copy(sent, out.at[:, tile_columns(1)], sem.at[0])
+    sent_copy = pltpu.make_async_copy(sent, out.at[:, tile_columns(1)], sem)
     sent_copy.start()
-    far_tile(message, scales, rights, deep, product, message_s, load, total_rows, result)
-    far_copy = pltpu.make_async_copy(result, out.at[:, tile_columns(3)], sem.at[1])
-    far_copy.start()
+    writes = band_writes(result, out, 3, write_sem)
+    far_tile(message, scales, rights, deep, product, message_s, load, total_rows, result, writes)
     sent_copy.wait()
-    far_copy.wait()
+    for write in writes:
+        write.wait()
 
 
 def last_tiles(message, sent, deep, rights, out, total_rows):
@@ -370,7 +381,8 @@
             pltpu.VMEM((band, OUT), jnp.bfloat16),
             pltpu.SMEM(message.shape, jnp.float32),
             pltpu.SemaphoreType.DMA,
-            pltpu.SemaphoreType.DMA((2,)),
+            pltpu.SemaphoreType.DMA,
+            pltpu.SemaphoreType.DMA((band // BS,)),
         ],
         FAR_COST,
         "last",

time: 38.5 us -> 38.5 us (level)
  no operation moved by 1% of the time
where the time goes in v6:
time: 38.5 us; the launch traced here: 38.3 us
  starting transfers between devices  17.2 us (45%)
  waiting for transfers between devices  14.2 us (37%)
  Pallas kernels  6.77 us (18%)
    ppermute x14, starting transfers between devices, swap(): return lax.ppermute(value, axis, [(i, i ^ bit) for i in range(count)])  17.2 us
    ppermute x14, waiting for transfers between devices, swap(): return lax.ppermute(value, axis, [(i, i ^ bit) for i in range(count)])  14.2 us
    pallas_call x1, Pallas kernels, own_squares(): call(functools.partial(own_kernel, len(earlies), len(rights), band), (jax...  2.66 us
    pallas_call x1, Pallas kernels, last_tiles(): call(functools.partial(last_kernel, len(rights), total_rows), jax.ShapeDt...  1.41 us
    pallas_call x1, Pallas kernels, far_tiles(): call(functools.partial(far_kernel, len(earlies), len(rights), total_rows)...  1.38 us
    pallas_call x1, Pallas kernels, mask_blocks(): call(mask_kernel, [jax.ShapeDtypeStruct(source.shape, source.dtype)] + [j...  1.22 us
  transfers between devices with their start and end apart: 14, of which 5 were waited for; matrix products, arithmetic and copies ran while one was open for 0% of the time, Pallas kernels for 14%

profile of v6, /device:TPU:0, one launch (start us, length us, event | category | flops | bytes accessed | tf_op | source)
XLA Modules:
  0.0 38.3 jit_solution(2481691923764939238)
XLA Ops:
  0.0 4.0 %collective-permute-start.1 = (bf16[256,512]{1,0:T(8,128)(2,1)}, bf16[256,512]{1,0:T(8,128)(2,1)S(1)}, u32[]{:S(2)}, u32[]{:S(2)}) collective-permute-start(bf16[256,512]{1,0:T(8,128)(2,1)} %refs_6_.1), channel_id=1, source_target_pairs={{0,2},{1,3},{2,0},{3,1},{4,6},{5,7},{6,4},{7,5},{8,10},{9,11},{10,... | collective-permute-start | bytes 786440 | tf_op jit(solution)/shard_map/right_far/ppermute | solution.py:26
  4.0 1.2 %mask.1 = (bf16[2048,128]{1,0:T(8,128)(2,1)S(1)}, bf16[1024,128]{1,0:T(8,128)(2,1)S(1)}, bf16[1024,128]{1,0:T(8,128)(2,1)S(1)}, f32[4,128]{1,0:T(4,128)S(1)}) custom-call(s32[1,16]{1,0:T(1,128)} %bitcast.7, bf16[2048,128]{1,0:T(8,128)(2,1)} %source.1, s32[2,16]{1,0:T(2,128)} %bitcast.3, s32[2,16]{1,0:T(2,128)} %bitcast.5), custom_call_target="tpu_custom_call" | custom-call | tf_op jit(solution)/shard_map/mask/pallas_call | solution.py:101
  5.3 1.6 %collective-permute-start.2 = (bf16[1024,128]{1,0:T(8,128)(2,1)S(1)}, bf16[1024,128]{1,0:T(8,128)(2,1)S(1)}, u32[]{:S(2)}, u32[]{:S(2)}) collective-permute-start(bf16[1024,128]{1,0:T(8,128)(2,1)S(1)} %get-tuple-element.23), channel_id=1, source_target_pairs={{0,8},{4,12},{8,0},{12,4},{1,9},{5,13},{9,1},{13,5},{2,10},{6,14},... | collective-permute-start | bytes 786440 | tf_op jit(solution)/shard_map/left_across/ppermute | solution.py:26
  6.8 0.5 %collective-permute-start.4 = (bf16[1024,128]{1,0:T(8,128)(2,1)S(1)}, bf16[1024,128]{1,0:T(8,128)(2,1)S(1)}, u32[]{:S(2)}, u32[]{:S(2)}) collective-permute-start(bf16[1024,128]{1,0:T(8,128)(2,1)S(1)} %get-tuple-element.25), channel_id=1, source_target_pairs={{0,8},{4,12},{8,0},{12,4},{1,9},{5,13},{9,1},{13,5},{2,10},{6,14},... | collective-permute-start | bytes 786440 | tf_op jit(solution)/shard_map/left_across/ppermute | solution.py:26
  7.4 0.0 collective-permute-start
  7.4 1.5 %collective-permute-start.6 = (bf16[256,512]{1,0:T(8,128)(2,1)}, bf16[256,512]{1,0:T(8,128)(2,1)S(1)}, u32[]{:S(2)}, u32[]{:S(2)}) collective-permute-start(bf16[256,512]{1,0:T(8,128)(2,1)} %refs_6_.1), channel_id=1, source_target_pairs={{0,16},{16,0},{1,17},{17,1},{2,18},{18,2},{3,19},{19,3},{4,20},{20... | collective-permute-start | bytes 786440 | tf_op jit(solution)/shard_map/right_near/ppermute | solution.py:26
  8.8 7.3 %collective-permute-done.1.refs_6_ = bf16[256,512]{1,0:T(8,128)(2,1)S(1)} collective-permute-done((bf16[256,512]{1,0:T(8,128)(2,1)}, bf16[256,512]{1,0:T(8,128)(2,1)S(1)}, u32[]{:S(2)}, u32[]{:S(2)}) %collective-permute-start.1) | collective-permute-done | bytes 262176 | tf_op jit(solution)/shard_map/right_far/ppermute | solution.py:26
  16.2 0.0 collective-permute-done.2.refs_2_
  16.2 0.0 collective-permute-start.3
  16.2 2.5 %collective-permute-done.4.refs_4_ = bf16[1024,128]{1,0:T(8,128)(2,1)S(1)} collective-permute-done((bf16[1024,128]{1,0:T(8,128)(2,1)S(1)}, bf16[1024,128]{1,0:T(8,128)(2,1)S(1)}, u32[]{:S(2)}, u32[]{:S(2)}) %collective-permute-start.4) | collective-permute-done | bytes 262176 | tf_op jit(solution)/shard_map/left_across/ppermute | solution.py:26
  18.7 0.0 collective-permute-start.5
  18.7 1.6 %collective-permute-start.8 = (bf16[256,512]{1,0:T(8,128)(2,1)S(1)}, bf16[256,512]{1,0:T(8,128)(2,1)S(1)}, u32[]{:S(2)}, u32[]{:S(2)}) collective-permute-start(bf16[256,512]{1,0:T(8,128)(2,1)S(1)} %collective-permute-done.1.refs_6_), channel_id=1, source_target_pairs={{0,1},{1,0},{2,3},{3,2},{4,5},{5,4},{6,7},{7,6},{8,9},{9,8},{10,11... | collective-permute-start | bytes 786440 | tf_op jit(solution)/shard_map/right_opposite/ppermute | solution.py:26
  20.3 0.0 collective-permute-done.6.refs_7_
  20.3 1.5 %collective-permute-start.7 = (bf16[256,512]{1,0:T(8,128)(2,1)S(1)}, bf16[256,512]{1,0:T(8,128)(2,1)S(1)}, u32[]{:S(2)}, u32[]{:S(2)}) collective-permute-start(bf16[256,512]{1,0:T(8,128)(2,1)S(1)} %collective-permute-done.1.refs_6_), channel_id=1, source_target_pairs={{0,16},{16,0},{1,17},{17,1},{2,18},{18,2},{3,19},{19,3},{4,20},{20... | collective-permute-start | bytes 786440 | tf_op jit(solution)/shard_map/right_far_row/ppermute | solution.py:26
  21.8 0.0 collective-permute-done.3.refs_3_
  21.8 0.0 collective-permute-done.5.refs_5_
  21.8 0.0 collective-permute-done.refs_1_
  21.8 2.7 %own.1 = (f32[2048,256]{1,0:T(8,128)S(1)}, f32[4,128]{1,0:T(4,128)S(1)}, s32[32,128]{1,0:T(8,128)S(1)}) custom-call(s32[2,16]{1,0:T(2,128)} %bitcast.4, s32[2,16]{1,0:T(2,128)} %bitcast.6, bf16[2048,128]{1,0:T(8,128)(2,1)S(1)} %get-tuple-element.22.refs_0_, bf16[2048,128]{1,0:T(8,128)(2,1)S(1)} %collective-permute-done.refs_1_, ...), custom_call_target="tpu_custom_call" | custom-call | tf_op jit(solution)/shard_map/own/pallas_call | solution.py:193
  24.5 0.6 %collective-permute-start.9 = (f32[4,128]{1,0:T(4,128)S(1)}, f32[4,128]{1,0:T(4,128)S(1)}, u32[]{:S(2)}, u32[]{:S(2)}) collective-permute-start(f32[4,128]{1,0:T(4,128)S(1)} %get-tuple-element.26.sums), channel_id=1, source_target_pairs={{0,16},{16,0},{1,17},{17,1},{2,18},{18,2},{3,19},{19,3},{4,20},{20... | collective-permute-start | bytes 6152 | tf_op jit(solution)/shard_map/sums_row/ppermute | solution.py:26
  25.1 2.4 %collective-permute-done.8.refs_0_ = bf16[256,512]{1,0:T(8,128)(2,1)S(1)} collective-permute-done((bf16[256,512]{1,0:T(8,128)(2,1)S(1)}, bf16[256,512]{1,0:T(8,128)(2,1)S(1)}, u32[]{:S(2)}, u32[]{:S(2)}) %collective-permute-start.8) | collective-permute-done | bytes 262176 | tf_op jit(solution)/shard_map/right_opposite/ppermute | solution.py:26
  27.4 1.3 %collective-permute-done.7.refs_7_ = bf16[256,512]{1,0:T(8,128)(2,1)S(1)} collective-permute-done((bf16[256,512]{1,0:T(8,128)(2,1)S(1)}, bf16[256,512]{1,0:T(8,128)(2,1)S(1)}, u32[]{:S(2)}, u32[]{:S(2)}) %collective-permute-start.7) | collective-permute-done | bytes 262176 | tf_op jit(solution)/shard_map/right_far_row/ppermute | solution.py:26
  28.8 0.0 collective-permute-done.9.other
  28.8 0.1 scale.1
  28.9 0.5 %collective-permute-start.11 = (bf16[512,256]{1,0:T(8,128)(2,1)S(1)}, bf16[512,256]{1,0:T(8,128)(2,1)S(1)}, u32[]{:S(2)}, u32[]{:S(2)}) collective-permute-start(bf16[512,256]{1,0:T(8,128)(2,1)S(1)} %get-tuple-element.33), channel_id=1, source_target_pairs={{0,1},{1,0},{2,3},{3,2},{4,5},{5,4},{6,7},{7,6},{8,9},{9,8},{10,11... | collective-permute-start | bytes 786440 | tf_op jit(solution)/shard_map/sent/ppermute | solution.py:26
  29.4 1.5 %collective-permute-start.13 = (bf16[256,512]{1,0:T(8,128)(2,1)S(1)}, bf16[256,512]{1,0:T(8,128)(2,1)S(1)}, u32[]{:S(2)}, u32[]{:S(2)}) collective-permute-start(bf16[256,512]{1,0:T(8,128)(2,1)S(1)} %collective-permute-done.8.refs_0_), channel_id=1, source_target_pairs={{0,16},{16,0},{1,17},{17,1},{2,18},{18,2},{3,19},{19,3},{4,20},{20... | collective-permute-start | bytes 786440 | tf_op jit(solution)/shard_map/right_opposite_row/ppermute | solution.py:26
  30.9 0.3 collective-permute-start.12
  31.2 3.6 %collective-permute-start.10 = (f32[8,128]{1,0:T(8,128)S(1)}, f32[8,128]{1,0:T(8,128)S(1)}, u32[]{:S(2)}, u32[]{:S(2)}) collective-permute-start(f32[8,128]{1,0:T(8,128)S(1)} %get-tuple-element.32), channel_id=1, source_target_pairs={{0,3},{1,2},{2,1},{3,0},{4,7},{5,6},{6,5},{7,4},{8,11},{9,10},{10,... | collective-permute-start | bytes 12296 | tf_op jit(solution)/shard_map/sums_opposite/ppermute | solution.py:26
  34.8 0.7 %collective-permute-done.12.message = f32[8,128]{1,0:T(8,128)S(1)} collective-permute-done((f32[8,128]{1,0:T(8,128)S(1)}, f32[8,128]{1,0:T(8,128)S(1)}, u32[]{:S(2)}, u32[]{:S(2)}) %collective-permute-start.12) | collective-permute-done | bytes 4128 | tf_op jit(solution)/shard_map/sums_far/ppermute | solution.py:26
  35.5 1.4 %far.1 = (bf16[512,1024]{1,0:T(8,128)(2,1)}, bf16[512,512]{1,0:T(8,128)(2,1)S(1)}) custom-call(f32[8,128]{1,0:T(8,128)S(1)} %collective-permute-done.12.message, bf16[512,256]{1,0:T(8,128)(2,1)S(1)} %get-tuple-element.34.own, bf16[2048,128]{1,0:T(8,128)(2,1)S(1)} %get-tuple-element.22.refs_0_, bf16[2048,128]{1,0:T(8,128)(2,1)S(1)} %collective-permute-done.refs_1_, ...), custom_call_target="tpu_custom_call" | custom-call | tf_op jit(solution)/shard_map/far/pallas_call | solution.py:335
  36.9 0.0 collective-permute-done.11.sent
  36.9 0.0 collective-permute-done.13.refs_1_
  36.9 1.4 %last.1 = bf16[512,1024]{1,0:T(8,128)(2,1)} custom-call(f32[8,128]{1,0:T(8,128)S(1)} %collective-permute-done.10.message, bf16[512,256]{1,0:T(8,128)(2,1)S(1)} %collective-permute-done.11.sent, bf16[512,512]{1,0:T(8,128)(2,1)S(1)} %get-tuple-element.36.deep, bf16[256,512]{1,0:T(8,128)(2,1)S(1)} %collective-permute-done.8.refs_0_, ...), custom_call_target="tpu_custom_call", output_to_operand_aliasing={{}: (5, {})} | custom-call | tf_op jit(solution)/shard_map/last/pallas_call | solution.py:373
  (1 shorter events, 0.0 us)
Async XLA Ops:
  0.0 16.2 %collective-permute-start.1 = (bf16[256,512]{1,0:T(8,128)(2,1)}, bf16[256,512]{1,0:T(8,128)(2,1)S(1)}, u32[]{:S(2)}, u32[]{:S(2)}) collective-permute-start(bf16[256,512]{1,0:T(8,128)(2,1)} %refs_6_.1), channel_id=1, source_target_pairs={{0,2},{1,3},{2,0},{3,1},{4,6},{5,7},{6,4},{7,5},{8,10},{9,11},{10,... | collective-permute-start | bytes 786440 | tf_op jit(solution)/shard_map/right_far/ppermute | solution.py:26
  5.3 10.9 %collective-permute-start.2 = (bf16[1024,128]{1,0:T(8,128)(2,1)S(1)}, bf16[1024,128]{1,0:T(8,128)(2,1)S(1)}, u32[]{:S(2)}, u32[]{:S(2)}) collective-permute-start(bf16[1024,128]{1,0:T(8,128)(2,1)S(1)} %get-tuple-element.23), channel_id=1, source_target_pairs={{0,8},{4,12},{8,0},{12,4},{1,9},{5,13},{9,1},{13,5},{2,10},{6,14},... | collective-permute-start | bytes 786440 | tf_op jit(solution)/shard_map/left_across/ppermute | solution.py:26
  6.8 11.9 %collective-permute-start.4 = (bf16[1024,128]{1,0:T(8,128)(2,1)S(1)}, bf16[1024,128]{1,0:T(8,128)(2,1)S(1)}, u32[]{:S(2)}, u32[]{:S(2)}) collective-permute-start(bf16[1024,128]{1,0:T(8,128)(2,1)S(1)} %get-tuple-element.25), channel_id=1, source_target_pairs={{0,8},{4,12},{8,0},{12,4},{1,9},{5,13},{9,1},{13,5},{2,10},{6,14},... | collective-permute-start | bytes 786440 | tf_op jit(solution)/shard_map/left_across/ppermute | solution.py:26
  7.4 14.4 %collective-permute-start = (bf16[2048,128]{1,0:T(8,128)(2,1)S(1)}, bf16[2048,128]{1,0:T(8,128)(2,1)S(1)}, u32[]{:S(2)}, u32[]{:S(2)}) collective-permute-start(bf16[2048,128]{1,0:T(8,128)(2,1)S(1)} %get-tuple-element.22.refs_0_), channel_id=1, source_target_pairs={{0,4},{4,0},{8,12},{12,8},{1,5},{5,1},{9,13},{13,9},{2,6},{6,2},{1... | collective-permute-start | bytes 1572872 | tf_op jit(solution)/shard_map/left_early/ppermute | solution.py:26
  7.4 12.9 %collective-permute-start.6 = (bf16[256,512]{1,0:T(8,128)(2,1)}, bf16[256,512]{1,0:T(8,128)(2,1)S(1)}, u32[]{:S(2)}, u32[]{:S(2)}) collective-permute-start(bf16[256,512]{1,0:T(8,128)(2,1)} %refs_6_.1), channel_id=1, source_target_pairs={{0,16},{16,0},{1,17},{17,1},{2,18},{18,2},{3,19},{19,3},{4,20},{20... | collective-permute-start | bytes 786440 | tf_op jit(solution)/shard_map/right_near/ppermute | solution.py:26
  16.2 5.6 %collective-permute-start.3 = (bf16[1024,128]{1,0:T(8,128)(2,1)S(1)}, bf16[1024,128]{1,0:T(8,128)(2,1)S(1)}, u32[]{:S(2)}, u32[]{:S(2)}) collective-permute-start(bf16[1024,128]{1,0:T(8,128)(2,1)S(1)} %collective-permute-done.2.refs_2_), channel_id=1, source_target_pairs={{0,4},{4,0},{8,12},{12,8},{1,5},{5,1},{9,13},{13,9},{2,6},{6,2},{1... | collective-permute-start | bytes 786440 | tf_op jit(solution)/shard_map/left_late/ppermute | solution.py:26
  18.7 3.1 %collective-permute-start.5 = (bf16[1024,128]{1,0:T(8,128)(2,1)S(1)}, bf16[1024,128]{1,0:T(8,128)(2,1)S(1)}, u32[]{:S(2)}, u32[]{:S(2)}) collective-permute-start(bf16[1024,128]{1,0:T(8,128)(2,1)S(1)} %collective-permute-done.4.refs_4_), channel_id=1, source_target_pairs={{0,4},{4,0},{8,12},{12,8},{1,5},{5,1},{9,13},{13,9},{2,6},{6,2},{1... | collective-permute-start | bytes 786440 | tf_op jit(solution)/shard_map/left_late/ppermute | solution.py:26
  18.7 8.7 %collective-permute-start.8 = (bf16[256,512]{1,0:T(8,128)(2,1)S(1)}, bf16[256,512]{1,0:T(8,128)(2,1)S(1)}, u32[]{:S(2)}, u32[]{:S(2)}) collective-permute-start(bf16[256,512]{1,0:T(8,128)(2,1)S(1)} %collective-permute-done.1.refs_6_), channel_id=1, source_target_pairs={{0,1},{1,0},{2,3},{3,2},{4,5},{5,4},{6,7},{7,6},{8,9},{9,8},{10,11... | collective-permute-start | bytes 786440 | tf_op jit(solution)/shard_map/right_opposite/ppermute | solution.py:26
  20.3 8.5 %collective-permute-start.7 = (bf16[256,512]{1,0:T(8,128)(2,1)S(1)}, bf16[256,512]{1,0:T(8,128)(2,1)S(1)}, u32[]{:S(2)}, u32[]{:S(2)}) collective-permute-start(bf16[256,512]{1,0:T(8,128)(2,1)S(1)} %collective-permute-done.1.refs_6_), channel_id=1, source_target_pairs={{0,16},{16,0},{1,17},{17,1},{2,18},{18,2},{3,19},{19,3},{4,20},{20... | collective-permute-start | bytes 786440 | tf_op jit(solution)/shard_map/right_far_row/ppermute | solution.py:26
  24.5 4.3 %collective-permute-start.9 = (f32[4,128]{1,0:T(4,128)S(1)}, f32[4,128]{1,0:T(4,128)S(1)}, u32[]{:S(2)}, u32[]{:S(2)}) collective-permute-start(f32[4,128]{1,0:T(4,128)S(1)} %get-tuple-element.26.sums), channel_id=1, source_target_pairs={{0,16},{16,0},{1,17},{17,1},{2,18},{18,2},{3,19},{19,3},{4,20},{20... | collective-permute-start | bytes 6152 | tf_op jit(solution)/shard_map/sums_row/ppermute | solution.py:26
  28.9 8.0 %collective-permute-start.11 = (bf16[512,256]{1,0:T(8,128)(2,1)S(1)}, bf16[512,256]{1,0:T(8,128)(2,1)S(1)}, u32[]{:S(2)}, u32[]{:S(2)}) collective-permute-start(bf16[512,256]{1,0:T(8,128)(2,1)S(1)} %get-tuple-element.33), channel_id=1, source_target_pairs={{0,1},{1,0},{2,3},{3,2},{4,5},{5,4},{6,7},{7,6},{8,9},{9,8},{10,11... | collective-permute-start | bytes 786440 | tf_op jit(solution)/shard_map/sent/ppermute | solution.py:26
  29.4 7.5 %collective-permute-start.13 = (bf16[256,512]{1,0:T(8,128)(2,1)S(1)}, bf16[256,512]{1,0:T(8,128)(2,1)S(1)}, u32[]{:S(2)}, u32[]{:S(2)}) collective-permute-start(bf16[256,512]{1,0:T(8,128)(2,1)S(1)} %collective-permute-done.8.refs_0_), channel_id=1, source_target_pairs={{0,16},{16,0},{1,17},{17,1},{2,18},{18,2},{3,19},{19,3},{4,20},{20... | collective-permute-start | bytes 786440 | tf_op jit(solution)/shard_map/right_opposite_row/ppermute | solution.py:26
  30.9 4.6 %collective-permute-start.12 = (f32[8,128]{1,0:T(8,128)S(1)}, f32[8,128]{1,0:T(8,128)S(1)}, u32[]{:S(2)}, u32[]{:S(2)}) collective-permute-start(f32[8,128]{1,0:T(8,128)S(1)} %get-tuple-element.32), channel_id=1, source_target_pairs={{0,2},{1,3},{2,0},{3,1},{4,6},{5,7},{6,4},{7,5},{8,10},{9,11},{10,... | collective-permute-start | bytes 12296 | tf_op jit(solution)/shard_map/sums_far/ppermute | solution.py:26
  31.2 5.7 %collective-permute-start.10 = (f32[8,128]{1,0:T(8,128)S(1)}, f32[8,128]{1,0:T(8,128)S(1)}, u32[]{:S(2)}, u32[]{:S(2)}) collective-permute-start(f32[8,128]{1,0:T(8,128)S(1)} %get-tuple-element.32), channel_id=1, source_target_pairs={{0,3},{1,2},{2,1},{3,0},{4,7},{5,6},{6,5},{7,4},{8,11},{9,10},{10,... | collective-permute-start | bytes 12296 | tf_op jit(solution)/shard_map/sums_opposite/ppermute | solution.py:26

commit v7 on v6

--- a/solution.py
+++ b/solution.py
@@ -62,9 +62,9 @@
     )
 
 
-def mask_kernel(flag, source, place, keep, masked, *refs):
+def mask_kernel(flag, source, target, place, keep, masked, *refs):
     chunks, refs = refs[:CHUNKS], refs[CHUNKS:]
-    meta, flag_s, panel, meta_v, sem, flag_sem, meta_sem = refs
+    target_v, meta, flag_s, panel, meta_v, sem, flag_sem, meta_sem = refs
     parts = sem.shape[0]
     rows = source.shape[0] // parts
     flag_copy = pltpu.make_async_copy(flag, flag_s, flag_sem)
@@ -77,6 +77,7 @@
     metas = [
         pltpu.make_async_copy(place, meta_v.at[0:KOL, :], meta_sem.at[0]),
         pltpu.make_async_copy(keep, meta_v.at[KOL : 2 * KOL, :], meta_sem.at[1]),
+        pltpu.make_async_copy(target, target_v, meta_sem.at[2]),
     ]
     for copy in metas:
         copy.start()
@@ -96,36 +97,44 @@
     meta[:, 0 : meta_v.shape[1]] = meta_v[...].astype(jnp.float32)
 
 
-def mask_blocks(flag, source, place, keep):
+def mask_blocks(flag, source, target, place, keep):
     rows = source.shape[0]
-    whole, *chunks, meta = call(
+    whole, *chunks, target_v, meta = call(
         mask_kernel,
         [jax.ShapeDtypeStruct(source.shape, source.dtype)]
         + [jax.ShapeDtypeStruct((rows // CHUNKS, BS), source.dtype)] * CHUNKS
-        + [jax.ShapeDtypeStruct((2 * KOL, BS), jnp.float32)],
-        [HBM] * 4,
-        [VMEM] * (CHUNKS + 2),
+        + [
+            jax.ShapeDtypeStruct(target.shape, target.dtype),
+            jax.ShapeDtypeStruct((2 * KOL, BS), jnp.float32),
+        ],
+        [HBM] * 5,
+        [VMEM] * (CHUNKS + 3),
         [
             pltpu.SMEM(flag.shape, jnp.int32),
             pltpu.VMEM(source.shape, source.dtype),
             pltpu.VMEM((2 * KOL, place.shape[1]), jnp.int32),
             pltpu.SemaphoreType.DMA((4,)),
             pltpu.SemaphoreType.DMA,
-            pltpu.SemaphoreType.DMA((2,)),
+            pltpu.SemaphoreType.DMA((3,)),
         ],
         MASK_COST,
         "mask",
-    )(*in_hbm(flag, source, place, keep))
-    return whole, chunks, meta
-
-
-def product_of(deep, right):
+    )(*in_hbm(flag, source, target, place, keep))
+    return whole, chunks, target_v, meta
+
+
+def right_blocks(rights, inner):
     me = lax.axis_index("col")
+    depth = rights[0].shape[0]
+    per = depth // BS
     blocks = []
-    for k in range(deep.shape[1] // BS):
-        place = pl.ds(pl.multiple_of((me ^ k) * BS, BS), BS)
-        blocks.append(right[place, :])
-    return jnp.dot(deep, jnp.concatenate(blocks, axis=0), preferred_element_type=jnp.float32)
+    for group in range(inner // depth):
+        piece = (me // per) ^ group ^ lax.axis_index("row")
+        chosen = rights[0][...]
+        for k in range(1, len(rights)):
+            chosen = jnp.where(piece == k, rights[k][...], chosen)
+        blocks.append(chosen)
+    return blocks
 
 
 def tick_kernel(before, after):
@@ -136,25 +145,25 @@
     return call(tick_kernel, jax.ShapeDtypeStruct(value.shape, value.dtype), [VMEM], VMEM, [], TICK_COST, "tick")(value)
 
 
-def own_kernel(n_left, n_right, band, place, keep, *refs):
+def own_kernel(n_left, n_right, band, meta, *refs):
     earlies, refs = refs[:n_left], refs[n_left:]
     chunks = [refs[c * n_left : (c + 1) * n_left] for c in range(CHUNKS)]
     refs = refs[CHUNKS * n_left :]
     rights, refs = refs[:n_right], refs[n_right:]
-    squares, sums, picks, panel, place_s, keep_s, product_a, product_b, sem, right_sem = refs
-    me = lax.axis_index("row")
+    squares, sums, picks, panel, meta_s, product_a, product_b, sem = refs
+    load = pltpu.make_async_copy(meta, meta_s, sem)
+    load.start()
+    inner = panel.shape[0]
     depth = rights[0].shape[0]
-    copies = [
-        pltpu.make_async_copy(place, place_s, sem.at[0]),
-        pltpu.make_async_copy(keep, keep_s, sem.at[1]),
-    ]
-    for k, right in enumerate(rights):
-        at = pl.ds(pl.multiple_of((me ^ k) * depth, depth), depth)
-        copies.append(pltpu.make_async_copy(right, panel.at[at, :], right_sem.at[k]))
-    for copy in copies:
-        copy.start()
-    for copy in copies[2:]:
-        copy.wait()
+    me = lax.axis_index("col")
+    for group, piece in enumerate(right_blocks(rights, inner)):
+        panel[pl.ds(group * depth, depth), :] = piece
+    per = depth // BS
+    ordered = []
+    for k in range(inner // BS):
+        place = (k // per) * depth + ((me ^ k) % per) * BS
+        ordered.append(panel[pl.ds(pl.multiple_of(place, BS), BS), :])
+    right = jnp.concatenate(ordered, axis=0)
     bands = band // BS
     rows = squares.shape[0]
     partial = [jnp.zeros((8, BS), jnp.float32) for _ in range(COLB)]
@@ -166,18 +175,17 @@
             + [left[pl.ds(first // CHUNKS, band), :] for left in chunks[chunk]],
             axis=1,
         )
-        product[...] = product_of(deep, panel)
+        product[...] = jnp.dot(deep, right, preferred_element_type=jnp.float32)
         if q == 0:
-            for copy in copies[:2]:
-                copy.wait()
+            load.wait()
         for i in range(bands):
             for s in range(KOL):
                 row = q * bands + i
-                block = place_s[s, row]
+                block = meta_s[s, row].astype(jnp.int32)
                 picks[pl.ds(row * KOL + s, 1), :] = jnp.full((1, BS), block, jnp.int32)
                 columns = pl.ds(pl.multiple_of(block * BS, BS), BS)
                 picked = product[pl.ds(i * BS, BS), columns]
-                square = picked * picked * keep_s[s, row].astype(jnp.float32)
+                square = picked * picked * meta_s[KOL + s, row]
                 squares[pl.ds(row * BS, BS), pl.ds(s * BS, BS)] = square
                 total = jnp.sum(square.reshape(BS // 8, 8, BS), axis=0)
                 for c in range(COLB):
@@ -186,7 +194,7 @@
         sums[pl.ds(c, 1), :] = jnp.sum(partial[c], axis=0, keepdims=True)
 
 
-def own_squares(place, keep, earlies, chunks, rights, band):
+def own_squares(meta, earlies, chunks, rights, band):
     rows = earlies[0].shape[0]
     inner = rights[0].shape[0] * len(rights)
     lefts = list(earlies) + [left for chunk in chunks for left in chunk]
@@ -197,20 +205,18 @@
             jax.ShapeDtypeStruct((COLB, BS), jnp.float32),
             jax.ShapeDtypeStruct((rows // BS * KOL, BS), jnp.int32),
         ),
-        [HBM, HBM] + [VMEM] * len(lefts) + [HBM] + [pl.BlockSpec(memory_space=pl.ANY)] * (len(rights) - 1),
+        [VMEM] * (1 + len(lefts) + len(rights)),
         (VMEM, VMEM, VMEM),
         [
             pltpu.VMEM((inner, TILE), jnp.bfloat16),
-            pltpu.SMEM(place.shape, jnp.int32),
-            pltpu.SMEM(place.shape, jnp.int32),
+            pltpu.SMEM(meta.shape, jnp.float32),
             pltpu.VMEM((band, TILE), jnp.float32),
             pltpu.VMEM((band, TILE), jnp.float32),
-            pltpu.SemaphoreType.DMA((2,)),
-            pltpu.SemaphoreType.DMA((len(rights),)),
+            pltpu.SemaphoreType.DMA,
         ],
         OWN_COST,
         "own",
-    )(*in_hbm(place, keep), *lefts, *in_hbm(rights[0]), *rights[1:])
+    )(meta, *lefts, *rights)
 
 
 def row_scales(picks, sums, total_rows):
@@ -403,17 +409,19 @@
     place = target_place_tile_index.T
     keep = retained_target_flag.T
     half = lax.axis_size("col") // 2
-    whole, masked, meta = mask_blocks(stored_tile_flag.T, source_matrix_strip, place, keep)
+    whole, masked, near_own, meta = mask_blocks(
+        stored_tile_flag.T, source_matrix_strip, target_matrix_strip, place, keep
+    )
     target = target_matrix_strip
     across = [swap(piece, "col", half, "left_across") for piece in masked]
     far = swap(target, "layer", 2, "right_far")
-    near = gather(target, "row", "right_near")
+    near = [near_own, *gather(target, "row", "right_near")[1:]]
     earlies = spread(whole, "col", half, "left_early")
     far, across[0] = together(far, across[0])
     lates = [spread(piece, "col", half, "left_late") for piece in across]
     opposite = swap(far, "layer", 1, "right_opposite")
     far_pieces = gather(far, "row", "right_far_row")
-    squares, sums, picks = own_squares(place, keep, earlies, lates, near, band)
+    squares, sums, picks = own_squares(meta, earlies, lates, near, band)
     bit = lax.axis_size("row") // 2
     while bit > 1:
         sums = sums + swap(sums, "row", bit, "sums_row")

time: 38.5 us -> 38.6 us (level)
  waiting for transfers between devices: 14.2 us -> 15 us
  Pallas kernels: 6.77 us -> 6.08 us
    ppermute x14, waiting for transfers between devices: 14.2 us -> 15 us  [swap(): return lax.ppermute(value, axis, [(i, i ^ bit) for i in range(count)])]
    pallas_call x1, Pallas kernels: 2.66 us -> 1.88 us  [own_squares(): call(functools.partial(own_kernel, len(earlies), len(rights), band), (jax...]
  transfers between devices with their start and end apart: 14 -> 14, of which waited for: 5 -> 5; matrix products, arithmetic and copies ran while one was open for 0% -> 0% of each run, Pallas kernels for 14% -> 12%
where the time goes in v7:
time: 38.6 us; the launch traced here: 38.4 us
  starting transfers between devices  17.2 us (45%)
  waiting for transfers between devices  15 us (39%)
  Pallas kernels  6.08 us (16%)
    ppermute x14, starting transfers between devices, swap(): return lax.ppermute(value, axis, [(i, i ^ bit) for i in range(count)])  17.2 us
    ppermute x14, waiting for transfers between devices, swap(): return lax.ppermute(value, axis, [(i, i ^ bit) for i in range(count)])  15 us
    pallas_call x1, Pallas kernels, own_squares(): call(functools.partial(own_kernel, len(earlies), len(rights), band), (jax...  1.88 us
    pallas_call x1, Pallas kernels, last_tiles(): call(functools.partial(last_kernel, len(rights), total_rows), jax.ShapeDt...  1.41 us
    pallas_call x1, Pallas kernels, far_tiles(): call(functools.partial(far_kernel, len(earlies), len(rights), total_rows)...  1.38 us
    pallas_call x1, Pallas kernels, mask_blocks(): call(mask_kernel, [jax.ShapeDtypeStruct(source.shape, source.dtype)] + [j...  1.31 us
  transfers between devices with their start and end apart: 14, of which 5 were waited for; matrix products, arithmetic and copies ran while one was open for 0% of the time, Pallas kernels for 12%

profile of v7, /device:TPU:0, one launch (start us, length us, event | category | flops | bytes accessed | tf_op | source)
XLA Modules:
  0.0 38.4 jit_solution(14191167974172948711)
XLA Ops:
  0.0 4.0 %collective-permute-start.1 = (bf16[256,512]{1,0:T(8,128)(2,1)}, bf16[256,512]{1,0:T(8,128)(2,1)S(1)}, u32[]{:S(2)}, u32[]{:S(2)}) collective-permute-start(bf16[256,512]{1,0:T(8,128)(2,1)} %target.1), channel_id=1, source_target_pairs={{0,2},{1,3},{2,0},{3,1},{4,6},{5,7},{6,4},{7,5},{8,10},{9,11},{10,... | collective-permute-start | bytes 786440 | tf_op jit(solution)/shard_map/right_far/ppermute | solution.py:26
  4.0 1.3 %mask.1 = (bf16[2048,128]{1,0:T(8,128)(2,1)S(1)}, bf16[1024,128]{1,0:T(8,128)(2,1)S(1)}, bf16[1024,128]{1,0:T(8,128)(2,1)S(1)}, bf16[256,512]{1,0:T(8,128)(2,1)S(1)}, f32[4,128]{1,0:T(4,128)S(1)}) custom-call(s32[1,16]{1,0:T(1,128)} %bitcast.5, bf16[2048,128]{1,0:T(8,128)(2,1)} %source.1, bf16[256,512]{1,0:T(8,128)(2,1)} %target.1, s32[2,16]{1,0:T(2,128)} %bitcast.3, ...), custom_call_target="tpu_custom_call" | custom-call | tf_op jit(solution)/shard_map/mask/pallas_call | solution.py:102
  5.4 1.6 %collective-permute-start.2 = (bf16[1024,128]{1,0:T(8,128)(2,1)S(1)}, bf16[1024,128]{1,0:T(8,128)(2,1)S(1)}, u32[]{:S(2)}, u32[]{:S(2)}) collective-permute-start(bf16[1024,128]{1,0:T(8,128)(2,1)S(1)} %get-tuple-element.25), channel_id=1, source_target_pairs={{0,8},{4,12},{8,0},{12,4},{1,9},{5,13},{9,1},{13,5},{2,10},{6,14},... | collective-permute-start | bytes 786440 | tf_op jit(solution)/shard_map/left_across/ppermute | solution.py:26
  6.9 0.5 %collective-permute-start.4 = (bf16[1024,128]{1,0:T(8,128)(2,1)S(1)}, bf16[1024,128]{1,0:T(8,128)(2,1)S(1)}, u32[]{:S(2)}, u32[]{:S(2)}) collective-permute-start(bf16[1024,128]{1,0:T(8,128)(2,1)S(1)} %get-tuple-element.27), channel_id=1, source_target_pairs={{0,8},{4,12},{8,0},{12,4},{1,9},{5,13},{9,1},{13,5},{2,10},{6,14},... | collective-permute-start | bytes 786440 | tf_op jit(solution)/shard_map/left_across/ppermute | solution.py:26
  7.4 0.0 collective-permute-start
  7.5 1.5 %collective-permute-start.6 = (bf16[256,512]{1,0:T(8,128)(2,1)}, bf16[256,512]{1,0:T(8,128)(2,1)S(1)}, u32[]{:S(2)}, u32[]{:S(2)}) collective-permute-start(bf16[256,512]{1,0:T(8,128)(2,1)} %target.1), channel_id=1, source_target_pairs={{0,16},{16,0},{1,17},{17,1},{2,18},{18,2},{3,19},{19,3},{4,20},{20... | collective-permute-start | bytes 786440 | tf_op jit(solution)/shard_map/right_near/ppermute | solution.py:26
  8.9 7.2 %collective-permute-done.1.refs_6_ = bf16[256,512]{1,0:T(8,128)(2,1)S(1)} collective-permute-done((bf16[256,512]{1,0:T(8,128)(2,1)}, bf16[256,512]{1,0:T(8,128)(2,1)S(1)}, u32[]{:S(2)}, u32[]{:S(2)}) %collective-permute-start.1) | collective-permute-done | bytes 262176 | tf_op jit(solution)/shard_map/right_far/ppermute | solution.py:26
  16.2 0.0 collective-permute-done.2.refs_2_
  16.2 0.0 collective-permute-start.3
  16.2 2.6 %collective-permute-done.4.refs_4_ = bf16[1024,128]{1,0:T(8,128)(2,1)S(1)} collective-permute-done((bf16[1024,128]{1,0:T(8,128)(2,1)S(1)}, bf16[1024,128]{1,0:T(8,128)(2,1)S(1)}, u32[]{:S(2)}, u32[]{:S(2)}) %collective-permute-start.4) | collective-permute-done | bytes 262176 | tf_op jit(solution)/shard_map/left_across/ppermute | solution.py:26
  18.8 0.0 collective-permute-start.5
  18.8 1.6 %collective-permute-start.8 = (bf16[256,512]{1,0:T(8,128)(2,1)S(1)}, bf16[256,512]{1,0:T(8,128)(2,1)S(1)}, u32[]{:S(2)}, u32[]{:S(2)}) collective-permute-start(bf16[256,512]{1,0:T(8,128)(2,1)S(1)} %collective-permute-done.1.refs_6_), channel_id=1, source_target_pairs={{0,1},{1,0},{2,3},{3,2},{4,5},{5,4},{6,7},{7,6},{8,9},{9,8},{10,11... | collective-permute-start | bytes 786440 | tf_op jit(solution)/shard_map/right_opposite/ppermute | solution.py:26
  20.4 0.0 collective-permute-done.6.refs_7_
  20.4 1.5 %collective-permute-start.7 = (bf16[256,512]{1,0:T(8,128)(2,1)S(1)}, bf16[256,512]{1,0:T(8,128)(2,1)S(1)}, u32[]{:S(2)}, u32[]{:S(2)}) collective-permute-start(bf16[256,512]{1,0:T(8,128)(2,1)S(1)} %collective-permute-done.1.refs_6_), channel_id=1, source_target_pairs={{0,16},{16,0},{1,17},{17,1},{2,18},{18,2},{3,19},{19,3},{4,20},{20... | collective-permute-start | bytes 786440 | tf_op jit(solution)/shard_map/right_far_row/ppermute | solution.py:26
  21.9 0.0 collective-permute-done.3.refs_3_
  21.9 0.0 collective-permute-done.5.refs_5_
  21.9 0.0 collective-permute-done.refs_1_
  21.9 1.9 %own.1 = (f32[2048,256]{1,0:T(8,128)S(1)}, f32[4,128]{1,0:T(4,128)S(1)}, s32[32,128]{1,0:T(8,128)S(1)}) custom-call(f32[4,128]{1,0:T(4,128)S(1)} %get-tuple-element.23.meta, bf16[2048,128]{1,0:T(8,128)(2,1)S(1)} %get-tuple-element.24.refs_0_, bf16[2048,128]{1,0:T(8,128)(2,1)S(1)} %collective-permute-done.refs_1_, ...), custom_call_target="tpu_custom_call" | custom-call | tf_op jit(solution)/shard_map/own/pallas_call | solution.py:201
  23.8 0.6 %collective-permute-start.9 = (f32[4,128]{1,0:T(4,128)S(1)}, f32[4,128]{1,0:T(4,128)S(1)}, u32[]{:S(2)}, u32[]{:S(2)}) collective-permute-start(f32[4,128]{1,0:T(4,128)S(1)} %get-tuple-element.29.sums), channel_id=1, source_target_pairs={{0,16},{16,0},{1,17},{17,1},{2,18},{18,2},{3,19},{19,3},{4,20},{20... | collective-permute-start | bytes 6152 | tf_op jit(solution)/shard_map/sums_row/ppermute | solution.py:26
  24.4 3.2 %collective-permute-done.8.refs_0_ = bf16[256,512]{1,0:T(8,128)(2,1)S(1)} collective-permute-done((bf16[256,512]{1,0:T(8,128)(2,1)S(1)}, bf16[256,512]{1,0:T(8,128)(2,1)S(1)}, u32[]{:S(2)}, u32[]{:S(2)}) %collective-permute-start.8) | collective-permute-done | bytes 262176 | tf_op jit(solution)/shard_map/right_opposite/ppermute | solution.py:26
  27.5 1.3 %collective-permute-done.7.refs_7_ = bf16[256,512]{1,0:T(8,128)(2,1)S(1)} collective-permute-done((bf16[256,512]{1,0:T(8,128)(2,1)S(1)}, bf16[256,512]{1,0:T(8,128)(2,1)S(1)}, u32[]{:S(2)}, u32[]{:S(2)}) %collective-permute-start.7) | collective-permute-done | bytes 262176 | tf_op jit(solution)/shard_map/right_far_row/ppermute | solution.py:26
  28.9 0.0 collective-permute-done.9.other
  28.9 0.1 scale.1
  29.0 0.5 %collective-permute-start.11 = (bf16[512,256]{1,0:T(8,128)(2,1)S(1)}, bf16[512,256]{1,0:T(8,128)(2,1)S(1)}, u32[]{:S(2)}, u32[]{:S(2)}) collective-permute-start(bf16[512,256]{1,0:T(8,128)(2,1)S(1)} %get-tuple-element.35), channel_id=1, source_target_pairs={{0,1},{1,0},{2,3},{3,2},{4,5},{5,4},{6,7},{7,6},{8,9},{9,8},{10,11... | collective-permute-start | bytes 786440 | tf_op jit(solution)/shard_map/sent/ppermute | solution.py:26
  29.5 1.5 %collective-permute-start.13 = (bf16[256,512]{1,0:T(8,128)(2,1)S(1)}, bf16[256,512]{1,0:T(8,128)(2,1)S(1)}, u32[]{:S(2)}, u32[]{:S(2)}) collective-permute-start(bf16[256,512]{1,0:T(8,128)(2,1)S(1)} %collective-permute-done.8.refs_0_), channel_id=1, source_target_pairs={{0,16},{16,0},{1,17},{17,1},{2,18},{18,2},{3,19},{19,3},{4,20},{20... | collective-permute-start | bytes 786440 | tf_op jit(solution)/shard_map/right_opposite_row/ppermute | solution.py:26
  31.0 0.3 collective-permute-start.12
  31.3 3.6 %collective-permute-start.10 = (f32[8,128]{1,0:T(8,128)S(1)}, f32[8,128]{1,0:T(8,128)S(1)}, u32[]{:S(2)}, u32[]{:S(2)}) collective-permute-start(f32[8,128]{1,0:T(8,128)S(1)} %get-tuple-element.34), channel_id=1, source_target_pairs={{0,3},{1,2},{2,1},{3,0},{4,7},{5,6},{6,5},{7,4},{8,11},{9,10},{10,... | collective-permute-start | bytes 12296 | tf_op jit(solution)/shard_map/sums_opposite/ppermute | solution.py:26
  34.9 0.7 %collective-permute-done.12.message = f32[8,128]{1,0:T(8,128)S(1)} collective-permute-done((f32[8,128]{1,0:T(8,128)S(1)}, f32[8,128]{1,0:T(8,128)S(1)}, u32[]{:S(2)}, u32[]{:S(2)}) %collective-permute-start.12) | collective-permute-done | bytes 4128 | tf_op jit(solution)/shard_map/sums_far/ppermute | solution.py:26
  35.6 1.4 %far.1 = (bf16[512,1024]{1,0:T(8,128)(2,1)}, bf16[512,512]{1,0:T(8,128)(2,1)S(1)}) custom-call(f32[8,128]{1,0:T(8,128)S(1)} %collective-permute-done.12.message, bf16[512,256]{1,0:T(8,128)(2,1)S(1)} %get-tuple-element.36.own, bf16[2048,128]{1,0:T(8,128)(2,1)S(1)} %get-tuple-element.24.refs_0_, bf16[2048,128]{1,0:T(8,128)(2,1)S(1)} %collective-permute-done.refs_1_, ...), custom_call_target="tpu_custom_call" | custom-call | tf_op jit(solution)/shard_map/far/pallas_call | solution.py:341
  37.0 0.0 collective-permute-done.10.message
  37.0 0.0 collective-permute-done.13.refs_1_
  37.0 1.4 %last.1 = bf16[512,1024]{1,0:T(8,128)(2,1)} custom-call(f32[8,128]{1,0:T(8,128)S(1)} %collective-permute-done.10.message, bf16[512,256]{1,0:T(8,128)(2,1)S(1)} %collective-permute-done.11.sent, bf16[512,512]{1,0:T(8,128)(2,1)S(1)} %get-tuple-element.38.deep, bf16[256,512]{1,0:T(8,128)(2,1)S(1)} %collective-permute-done.8.refs_0_, ...), custom_call_target="tpu_custom_call", output_to_operand_aliasing={{}: (5, {})} | custom-call | tf_op jit(solution)/shard_map/last/pallas_call | solution.py:379
  (1 shorter events, 0.0 us)
Async XLA Ops:
  0.0 16.2 %collective-permute-start.1 = (bf16[256,512]{1,0:T(8,128)(2,1)}, bf16[256,512]{1,0:T(8,128)(2,1)S(1)}, u32[]{:S(2)}, u32[]{:S(2)}) collective-permute-start(bf16[256,512]{1,0:T(8,128)(2,1)} %target.1), channel_id=1, source_target_pairs={{0,2},{1,3},{2,0},{3,1},{4,6},{5,7},{6,4},{7,5},{8,10},{9,11},{10,... | collective-permute-start | bytes 786440 | tf_op jit(solution)/shard_map/right_far/ppermute | solution.py:26
  5.4 10.8 %collective-permute-start.2 = (bf16[1024,128]{1,0:T(8,128)(2,1)S(1)}, bf16[1024,128]{1,0:T(8,128)(2,1)S(1)}, u32[]{:S(2)}, u32[]{:S(2)}) collective-permute-start(bf16[1024,128]{1,0:T(8,128)(2,1)S(1)} %get-tuple-element.25), channel_id=1, source_target_pairs={{0,8},{4,12},{8,0},{12,4},{1,9},{5,13},{9,1},{13,5},{2,10},{6,14},... | collective-permute-start | bytes 786440 | tf_op jit(solution)/shard_map/left_across/ppermute | solution.py:26
  6.9 11.9 %collective-permute-start.4 = (bf16[1024,128]{1,0:T(8,128)(2,1)S(1)}, bf16[1024,128]{1,0:T(8,128)(2,1)S(1)}, u32[]{:S(2)}, u32[]{:S(2)}) collective-permute-start(bf16[1024,128]{1,0:T(8,128)(2,1)S(1)} %get-tuple-element.27), channel_id=1, source_target_pairs={{0,8},{4,12},{8,0},{12,4},{1,9},{5,13},{9,1},{13,5},{2,10},{6,14},... | collective-permute-start | bytes 786440 | tf_op jit(solution)/shard_map/left_across/ppermute | solution.py:26
  7.4 14.4 %collective-permute-start = (bf16[2048,128]{1,0:T(8,128)(2,1)S(1)}, bf16[2048,128]{1,0:T(8,128)(2,1)S(1)}, u32[]{:S(2)}, u32[]{:S(2)}) collective-permute-start(bf16[2048,128]{1,0:T(8,128)(2,1)S(1)} %get-tuple-element.24.refs_0_), channel_id=1, source_target_pairs={{0,4},{4,0},{8,12},{12,8},{1,5},{5,1},{9,13},{13,9},{2,6},{6,2},{1... | collective-permute-start | bytes 1572872 | tf_op jit(solution)/shard_map/left_early/ppermute | solution.py:26
  7.5 12.9 %collective-permute-start.6 = (bf16[256,512]{1,0:T(8,128)(2,1)}, bf16[256,512]{1,0:T(8,128)(2,1)S(1)}, u32[]{:S(2)}, u32[]{:S(2)}) collective-permute-start(bf16[256,512]{1,0:T(8,128)(2,1)} %target.1), channel_id=1, source_target_pairs={{0,16},{16,0},{1,17},{17,1},{2,18},{18,2},{3,19},{19,3},{4,20},{20... | collective-permute-start | bytes 786440 | tf_op jit(solution)/shard_map/right_near/ppermute | solution.py:26
  16.2 5.7 %collective-permute-start.3 = (bf16[1024,128]{1,0:T(8,128)(2,1)S(1)}, bf16[1024,128]{1,0:T(8,128)(2,1)S(1)}, u32[]{:S(2)}, u32[]{:S(2)}) collective-permute-start(bf16[1024,128]{1,0:T(8,128)(2,1)S(1)} %collective-permute-done.2.refs_2_), channel_id=1, source_target_pairs={{0,4},{4,0},{8,12},{12,8},{1,5},{5,1},{9,13},{13,9},{2,6},{6,2},{1... | collective-permute-start | bytes 786440 | tf_op jit(solution)/shard_map/left_late/ppermute | solution.py:26
  18.8 3.1 %collective-permute-start.5 = (bf16[1024,128]{1,0:T(8,128)(2,1)S(1)}, bf16[1024,128]{1,0:T(8,128)(2,1)S(1)}, u32[]{:S(2)}, u32[]{:S(2)}) collective-permute-start(bf16[1024,128]{1,0:T(8,128)(2,1)S(1)} %collective-permute-done.4.refs_4_), channel_id=1, source_target_pairs={{0,4},{4,0},{8,12},{12,8},{1,5},{5,1},{9,13},{13,9},{2,6},{6,2},{1... | collective-permute-start | bytes 786440 | tf_op jit(solution)/shard_map/left_late/ppermute | solution.py:26
  18.8 8.7 %collective-permute-start.8 = (bf16[256,512]{1,0:T(8,128)(2,1)S(1)}, bf16[256,512]{1,0:T(8,128)(2,1)S(1)}, u32[]{:S(2)}, u32[]{:S(2)}) collective-permute-start(bf16[256,512]{1,0:T(8,128)(2,1)S(1)} %collective-permute-done.1.refs_6_), channel_id=1, source_target_pairs={{0,1},{1,0},{2,3},{3,2},{4,5},{5,4},{6,7},{7,6},{8,9},{9,8},{10,11... | collective-permute-start | bytes 786440 | tf_op jit(solution)/shard_map/right_opposite/ppermute | solution.py:26
  20.4 8.5 %collective-permute-start.7 = (bf16[256,512]{1,0:T(8,128)(2,1)S(1)}, bf16[256,512]{1,0:T(8,128)(2,1)S(1)}, u32[]{:S(2)}, u32[]{:S(2)}) collective-permute-start(bf16[256,512]{1,0:T(8,128)(2,1)S(1)} %collective-permute-done.1.refs_6_), channel_id=1, source_target_pairs={{0,16},{16,0},{1,17},{17,1},{2,18},{18,2},{3,19},{19,3},{4,20},{20... | collective-permute-start | bytes 786440 | tf_op jit(solution)/shard_map/right_far_row/ppermute | solution.py:26
  23.8 5.1 %collective-permute-start.9 = (f32[4,128]{1,0:T(4,128)S(1)}, f32[4,128]{1,0:T(4,128)S(1)}, u32[]{:S(2)}, u32[]{:S(2)}) collective-permute-start(f32[4,128]{1,0:T(4,128)S(1)} %get-tuple-element.29.sums), channel_id=1, source_target_pairs={{0,16},{16,0},{1,17},{17,1},{2,18},{18,2},{3,19},{19,3},{4,20},{20... | collective-permute-start | bytes 6152 | tf_op jit(solution)/shard_map/sums_row/ppermute | solution.py:26
  29.0 8.0 %collective-permute-start.11 = (bf16[512,256]{1,0:T(8,128)(2,1)S(1)}, bf16[512,256]{1,0:T(8,128)(2,1)S(1)}, u32[]{:S(2)}, u32[]{:S(2)}) collective-permute-start(bf16[512,256]{1,0:T(8,128)(2,1)S(1)} %get-tuple-element.35), channel_id=1, source_target_pairs={{0,1},{1,0},{2,3},{3,2},{4,5},{5,4},{6,7},{7,6},{8,9},{9,8},{10,11... | collective-permute-start | bytes 786440 | tf_op jit(solution)/shard_map/sent/ppermute | solution.py:26
  29.5 7.5 %collective-permute-start.13 = (bf16[256,512]{1,0:T(8,128)(2,1)S(1)}, bf16[256,512]{1,0:T(8,128)(2,1)S(1)}, u32[]{:S(2)}, u32[]{:S(2)}) collective-permute-start(bf16[256,512]{1,0:T(8,128)(2,1)S(1)} %collective-permute-done.8.refs_0_), channel_id=1, source_target_pairs={{0,16},{16,0},{1,17},{17,1},{2,18},{18,2},{3,19},{19,3},{4,20},{20... | collective-permute-start | bytes 786440 | tf_op jit(solution)/shard_map/right_opposite_row/ppermute | solution.py:26
  31.0 4.6 %collective-permute-start.12 = (f32[8,128]{1,0:T(8,128)S(1)}, f32[8,128]{1,0:T(8,128)S(1)}, u32[]{:S(2)}, u32[]{:S(2)}) collective-permute-start(f32[8,128]{1,0:T(8,128)S(1)} %get-tuple-element.34), channel_id=1, source_target_pairs={{0,2},{1,3},{2,0},{3,1},{4,6},{5,7},{6,4},{7,5},{8,10},{9,11},{10,... | collective-permute-start | bytes 12296 | tf_op jit(solution)/shard_map/sums_far/ppermute | solution.py:26
  31.3 5.7 %collective-permute-start.10 = (f32[8,128]{1,0:T(8,128)S(1)}, f32[8,128]{1,0:T(8,128)S(1)}, u32[]{:S(2)}, u32[]{:S(2)}) collective-permute-start(f32[8,128]{1,0:T(8,128)S(1)} %get-tuple-element.34), channel_id=1, source_target_pairs={{0,3},{1,2},{2,1},{3,0},{4,7},{5,6},{6,5},{7,4},{8,11},{9,10},{10,... | collective-permute-start | bytes 12296 | tf_op jit(solution)/shard_map/sums_opposite/ppermute | solution.py:26
